TPU v7x, 512 devices: a whole 4x8x8 slice. The times are simulated.
512 devices in a mesh: league: 128 (over z, x_hi, y), rep: 4 (over x_lo, core).
Axes of the slice: x: 4 (x_hi: 2, x_lo: 2; x = x_hi * 2 + x_lo), y: 8, z: 8, core: 2. Of those that a mesh axis runs over, the one named last changes fastest.
Arguments:
- observations: bfloat16 [65536, 2048], P(('league', 'rep')), may hold values from -6 to 6
- weights: bfloat16 [128, 2048, 2048], P('league', None, 'rep'), may hold values from -0.125 to 0.125
- gains: float32 [128, 2048], P('league'), may hold values from 0.5 to 1.5
- heads: bfloat16 [128, 2048], P('league', 'rep'), may hold values from -0.125 to 0.125
- pairing: int32 [65536, 1], P(('league', 'rep')), may hold values from 0 to 127; in each aligned block of 128 rows (0 to 127, 128 to 255, ...) at most 2 rows name the same one
- valid: int32 [65536], P(('league', 'rep')), may hold values 0 or 1
Outputs:
- own_value: float32 [65536], P(('league', 'rep'))
- opponent_value: float32 [65536], P(('league', 'rep'))
Inputs may be any that keep to these rules, and one draw needn't show every extreme that they name: `pairing`: among the rows of one device, at most 2 name one agent; every agent is named by some row of the whole batch.
All inputs are finite; a program needn't handle non-finite values. No bound on the sum of `valid` on one device may be relied on, other than what follows from the above.
Results may differ from a plain program's by a relative error of at most 0.003.
Values may be sent and summed in bfloat16 or wider, within the bound.
No kernel may reach another device: no remote copies, remote signals or barrier semaphores. Data moves between devices by JAX's collectives and lax.ppermute only.
A program may use at most 64 MiB of HBM per device.

v0:
```python
import jax
import jax.numpy as jnp
from jax import lax
from jax.sharding import PartitionSpec as P


def normed_values(obs_rows, agent_gain, weight_cols, head_cols):
    wide_rows = obs_rows.astype(jnp.float32)
    squares = jnp.mean(wide_rows * wide_rows, axis=1, keepdims=True)
    scaled = (wide_rows * lax.rsqrt(squares + 1e-06) * agent_gain).astype(jnp.bfloat16)
    hidden = jax.nn.silu(jnp.dot(scaled, weight_cols, preferred_element_type=jnp.float32))
    return jnp.sum(hidden * head_cols.astype(jnp.float32), axis=1)


def per_device(observations, weights, gains, heads, pairing, valid):
    rows_dev, feature_width = observations.shape
    n_league = lax.axis_size("league")
    capacity = max(2, 2 * rows_dev // n_league)
    own_gain = gains[0]
    weight_cols = weights[0]
    head_cols = heads[0]
    weight_full, head_full = (
        lax.all_gather(weight_cols, "rep", axis=1, tiled=True),
        lax.all_gather(head_cols, "rep", axis=0, tiled=True),
    )
    own_value = normed_values(observations, own_gain, weight_full, head_full)
    owner_id = pairing[:, 0]
    is_live = valid == 1
    agent_iota = jnp.arange(n_league, dtype=jnp.int32)
    pick_table = ((owner_id[:, None] == agent_iota[None, :]) & is_live[:, None]).astype(jnp.float32)
    row_iota = jnp.arange(rows_dev, dtype=jnp.int32)
    earlier = (row_iota[:, None] > row_iota[None, :]).astype(jnp.float32)
    before = jnp.dot(earlier, pick_table, precision=lax.Precision.HIGHEST)
    slot_index = jnp.sum(before * pick_table, axis=1).astype(jnp.int32)
    target = jnp.where(is_live, owner_id * capacity + slot_index, n_league * capacity)
    outgoing = (
        jnp.zeros((n_league * capacity + 1, feature_width), jnp.bfloat16)
        .at[target]
        .set(observations)
    )
    outgoing = outgoing[: n_league * capacity].reshape(n_league, capacity, feature_width)
    received = lax.all_to_all(outgoing, "league", split_axis=0, concat_axis=0, tiled=True)
    flat_rows = received.reshape(received.shape[0] * received.shape[1], feature_width)
    answers = normed_values(flat_rows, own_gain, weight_full, head_full).reshape(
        received.shape[0], received.shape[1]
    )
    returned = lax.all_to_all(answers, "league", split_axis=0, concat_axis=0, tiled=True)
    flat_back = jnp.concatenate([returned.reshape(-1), jnp.zeros((1,), jnp.float32)])
    opponent_value = jnp.where(is_live, flat_back[target], 0.0)
    return (own_value, opponent_value)


def solution(mesh):
    return jax.shard_map(
        per_device,
        mesh=mesh,
        in_specs=(
            P(("league", "rep"), None),
            P("league", None, "rep"),
            P("league", None),
            P("league", "rep"),
            P(("league", "rep"), None),
            P(("league", "rep")),
        ),
        out_specs=(P(("league", "rep")), P(("league", "rep"))),
        check_vma=False,
    )
```

profile of v0, /device:TPU:1, one launch (start us, length us, event | category | flops | bytes accessed | tf_op | source)
XLA Modules:
  0.0 159.3 jit_solution(9110506336919727464)
XLA Ops:
  7.2 0.0 copy-start.4
  7.2 0.0 copy-start.3
  7.2 0.0 copy-start
  7.2 0.0 all-gather.4.cloned.1.call-start
  7.2 0.7 all-gather.4.cloned.1.call-update
  7.9 0.0 copy-done.4
  8.0 0.0 copy-done.3
  8.0 0.2 fusion.6
  8.2 0.1 copy-done
  8.2 1.7 %scatter_custom_fusion = bf16[257,2048]{1,0:T(8,128)(2,1)S(1)} fusion(s32[128]{0:T(128)S(1)} %compare_select_fusion, bf16[128,2048]{1,0:T(8,128)(2,1)S(1)} %copy-done, bf16[]{:T(256)} %constant.7.clone.1), kind=kCustom, calls=%fused_computation.19 | custom fusion | bytes 1052674 | tf_op jit(solution)/shard_map/scatter | solution.py:39
  10.0 0.1 slice.6
  10.1 0.0 copy-start.2
  10.1 1.6 reshape.45
  11.7 20.8 %all-to-all-start = ((bf16[128,2,2048]{2,1,0:T(2,128)(2,1)}), bf16[128,2,2048]{2,1,0:T(2,128)(2,1)S(1)}, u32[]{:S(2)}, u32[]{:S(2)}) async-start(bf16[128,2,2048]{2,1,0:T(2,128)(2,1)} %reshape.45), calls=%async_computation | async-start | bytes 2097152 | tf_op jit(solution)/shard_map/all_to_all | solution.py:42
  32.5 0.0 copy-done.2
  32.5 5.9 %all-gather.1 = bf16[1,2048]{1,0:T(2,128)(2,1)S(1)} all-gather(bf16[1,512]{1,0:T(2,128)(2,1)S(1)} %copy-done.2), channel_id=3, replica_groups=mesh['league'=128,'rep'=4] {'rep'}, dimensions={1}, use_global_device_ids=true | all-gather | bytes 5120 | tf_op jit(solution)/shard_map/all_gather | solution.py:24
  38.5 0.2 fusion.7
  38.7 0.0 copy-start.5
  38.7 24.7 %all-to-all-done = bf16[128,2,2048]{2,1,0:T(2,128)(2,1)S(1)} async-done(((bf16[128,2,2048]{2,1,0:T(2,128)(2,1)}), bf16[128,2,2048]{2,1,0:T(2,128)(2,1)S(1)}, u32[]{:S(2)}, u32[]{:S(2)}) %all-to-all-start) | async-done | bytes 1048608 | tf_op jit(solution)/shard_map/all_to_all | solution.py:42
  63.3 1.2 multiply_reduce_fusion.1
  64.5 0.1 rsqrt.21
  64.6 0.3 reshape.47
  65.0 48.6 %all-gather.4.cloned.1.call-done = bf16[1,2048,2048]{2,1,0:T(8,128)(2,1)} async-done(((bf16[1,2048,512]{2,1,0:T(8,128)(2,1)}), bf16[1,2048,2048]{2,1,0:T(8,128)(2,1)}) %all-gather.4.cloned.1.call-update) | async-done | bytes 8388624 | tf_op jit(solution)/shard_map/all_gather | solution.py:23
  113.6 0.0 copy-done.5
  113.6 0.0 copy-start.1
  113.6 6.1 %multiply_reduce_fusion = f32[256]{0:T(256)S(1)} fusion(bf16[1,2048,2048]{2,1,0:T(8,128)(2,1)} %all-gather.4.cloned.1.call-done, f32[256,2048]{1,0:T(8,128)S(1)} %reshape.47, f32[2048]{0:T(1024)S(1)} %bitcast.14, f32[2048]{0:T(1024)S(1)} %bitcast.17, f32[256]{0:T(256)S(1)} %rsqrt.21), kind=kOutput, calls=%fused_computation.6 | convolution fusion | flops 2152201984 | bytes 10504192 | tf_op jit(solution)/shard_map/dot_general | solution.py:11
  119.7 0.8 all_to_all.10
  120.5 15.7 %all-to-all-start.1 = ((f32[128,1,2]{2,1,0:T(1,128)}), f32[128,1,2]{2,1,0:T(1,128)S(1)}, u32[]{:S(2)}, u32[]{:S(2)}) async-start(f32[128,1,2]{2,1,0:T(1,128)} %bitcast.4), calls=%async_computation.1 | async-start | bytes 131072 | tf_op jit(solution)/shard_map/all_to_all | solution.py:47
  136.2 0.0 copy-done.1
  136.2 5.4 %multiply_reduce_fusion.2 = f32[128]{0:T(128)} fusion(bf16[1,2048,2048]{2,1,0:T(8,128)(2,1)} %all-gather.4.cloned.1.call-done, bf16[128,2048]{1,0:T(8,128)(2,1)S(1)} %copy-done.1, f32[2048]{0:T(1024)S(1)} %bitcast.15, f32[2048]{0:T(1024)S(1)} %bitcast.18, f32[128]{0:T(128)S(1)} %add_rsqrt_fusion.1), kind=kOutput, calls=%fused_computation.18 | convolution fusion | flops 1076363136 | bytes 8930304 | tf_op jit(solution)/shard_map/dot_general | solution.py:11
  141.6 7.6 %all-to-all-done.1 = f32[128,1,2]{2,1,0:T(1,128)S(1)} async-done(((f32[128,1,2]{2,1,0:T(1,128)}), f32[128,1,2]{2,1,0:T(1,128)S(1)}, u32[]{:S(2)}, u32[]{:S(2)}) %all-to-all-start.1) | async-done | bytes 1056 | tf_op jit(solution)/shard_map/all_to_all | solution.py:47
  149.2 0.5 broadcast.54
  149.7 0.8 reduce.4
  150.5 0.1 reshape.46
  150.7 1.3 gather_fusion
  152.0 0.5 broadcast_select_fusion
  (7 shorter events, 0.1 us)
Async XLA Ops:
  7.2 0.8 copy-start.4
  7.2 0.8 copy-start.3
  7.2 1.1 copy-start
  7.2 106.4 %all-gather.4.cloned.1.call-start = ((), (), s32[]{:S(2)}) async-start(), calls=%async_computation.2 | async-start | bytes 10485760 | tf_op jit(solution)/shard_map/all_gather | solution.py:23
  10.1 22.4 %copy-start.2 = (bf16[1,512]{1,0:T(2,128)(2,1)S(1)}, bf16[1,512]{1,0:T(2,128)(2,1)}, u32[]{:S(2)}) copy-start(bf16[1,512]{1,0:T(2,128)(2,1)} %param.9) | copy-start | bytes 3076
  11.7 51.7 %all-to-all-start = ((bf16[128,2,2048]{2,1,0:T(2,128)(2,1)}), bf16[128,2,2048]{2,1,0:T(2,128)(2,1)S(1)}, u32[]{:S(2)}, u32[]{:S(2)}) async-start(bf16[128,2,2048]{2,1,0:T(2,128)(2,1)} %reshape.45), calls=%async_computation | async-start | bytes 2097152 | tf_op jit(solution)/shard_map/all_to_all | solution.py:42
  38.7 74.9 %copy-start.5 = (f32[1,2048]{1,0:T(1,128)S(1)}, f32[1,2048]{1,0:T(1,128)}, u32[]{:S(2)}) copy-start(f32[1,2048]{1,0:T(1,128)} %param.8) | copy-start | bytes 24580
  113.6 22.6 %copy-start.1 = (bf16[128,2048]{1,0:T(8,128)(2,1)S(1)}, bf16[128,2048]{1,0:T(8,128)(2,1)}, u32[]{:S(2)}) copy-start(bf16[128,2048]{1,0:T(8,128)(2,1)} %param.6) | copy-start | bytes 1572868
  120.5 28.8 %all-to-all-start.1 = ((f32[128,1,2]{2,1,0:T(1,128)}), f32[128,1,2]{2,1,0:T(1,128)S(1)}, u32[]{:S(2)}, u32[]{:S(2)}) async-start(f32[128,1,2]{2,1,0:T(1,128)} %bitcast.4), calls=%async_computation.1 | async-start | bytes 131072 | tf_op jit(solution)/shard_map/all_to_all | solution.py:47
Sparse Core Ops, SparseCore 0:
  10.1 103.3 all-gather.3
where the time goes:
time: 160 us; the launch traced here: 159 us
  waiting for transfers between devices  81.5 us (51%)
  starting transfers between devices  36.6 us (23%)
  between operations  14.2 us (9%)
  matrix products  11.7 us (7%)
  local copies, waits for them, and re-layouts  6.68 us (4%)
  blocking collectives  5.93 us (4%)
  other arithmetic  2.73 us (2%)
    all_gather x1, waiting for transfers between devices, per_device(): lax.all_gather(weight_cols, 'rep', axis=1, tiled=True)  48.6 us
    all_to_all x1, waiting for transfers between devices, per_device(): lax.all_to_all(outgoing, 'league', split_axis=0, concat_axis=0, tiled=True)  24.7 us
    all_to_all x1, starting transfers between devices, per_device(): lax.all_to_all(outgoing, 'league', split_axis=0, concat_axis=0, tiled=True)  20.8 us
    all_to_all x1, starting transfers between devices, per_device(): lax.all_to_all(answers, 'league', split_axis=0, concat_axis=0, tiled=True)  15.7 us
    dot_general x2, matrix products, normed_values(): jnp.dot(scaled, weight_cols, preferred_element_type=jnp.float32)  11.5 us
    all_to_all x1, waiting for transfers between devices, per_device(): lax.all_to_all(answers, 'league', split_axis=0, concat_axis=0, tiled=True)  7.61 us
    all_gather x1, blocking collectives, per_device(): lax.all_gather(head_cols, 'rep', axis=0, tiled=True)  5.93 us
  transfers between devices with their start and end apart: 3, of which 3 were waited for; matrix products, arithmetic and copies ran while one was open for 7% of the time, Pallas kernels for 0%

commit v1 on v0

v1 whole, which is shorter than its diff:
```python
import jax
import jax.numpy as jnp
from jax import lax
from jax.sharding import Mesh, PartitionSpec as P

NZ, NXH, NY, NXL, NC = 8, 2, 8, 2, 2
AXES = ("z", "xh", "y", "xl", "c")
SWAP = [(0, 1), (1, 0)]
CHUNKS = (256, 128, 128)


def exchange_groups():
    groups = []
    for flip in range(2):
        group = []
        for z in range(NZ):
            for xh in range(NXH):
                for y in range(NY):
                    group.append(((z * NXH + xh) * NY + y) * NXL + (xh ^ flip))
        groups.append(group)
    return groups


def scaled_rows(rows, gain):
    wide = rows.astype(jnp.float32)
    squares = jnp.mean(wide * wide, axis=1, keepdims=True)
    return (wide * lax.rsqrt(squares + 1e-06) * gain).astype(jnp.bfloat16)


def partial_values(scaled, weight, head):
    hidden = jax.nn.silu(jnp.dot(scaled, weight, preferred_element_type=jnp.float32))
    return jnp.sum(hidden * head.astype(jnp.float32), axis=1)


def per_device(observations, weights, gains, heads, pairing, valid):
    rows_dev, width = observations.shape
    n_agents = NZ * NXH * NY
    groups = exchange_groups()
    gain = gains[0]
    own_w = weights[0]
    exchange = ("z", "xh", "y", "xl")

    sib_w = lax.ppermute(own_w, "c", SWAP)
    far_w, far_sib_w, start = [], [], 0
    for size in CHUNKS:
        chunk = lax.ppermute(own_w[:, start : start + size], "xl", SWAP)
        far_w.append(chunk)
        far_sib_w.append(lax.ppermute(chunk, "c", SWAP))
        start += size
    head_all = lax.all_gather(heads[0], ("xl", "c"), axis=0, tiled=False)
    my_xl, my_c = lax.axis_index("xl"), lax.axis_index("c")

    def head_of(xl, c):
        return lax.dynamic_index_in_dim(head_all, xl * NC + c, 0, keepdims=False)

    own_h = heads[0]
    sib_h, far_h, far_sib_h = head_of(my_xl, 1 - my_c), head_of(1 - my_xl, my_c), head_of(1 - my_xl, 1 - my_c)

    pieces = [(own_w, own_h), (sib_w, sib_h)]
    start = 0
    for size, chunk, sib_chunk in zip(CHUNKS, far_w, far_sib_w):
        pieces.append((chunk, far_h[start : start + size]))
        pieces.append((sib_chunk, far_sib_h[start : start + size]))
        start += size

    owner = pairing[:, 0]
    live = valid == 1
    row_iota = jnp.arange(rows_dev, dtype=jnp.int32)
    same = (owner[:, None] == owner[None, :]) & (row_iota[None, :] < row_iota[:, None]) & live[None, :]
    second = jnp.sum(same.astype(jnp.int32), axis=1)
    agent_iota = jnp.arange(n_agents, dtype=jnp.int32)
    named = (agent_iota[:, None] == owner[None, :]) & live[None, :]
    picks = [(named & (second[None, :] == k)).astype(jnp.bfloat16) for k in range(2)]
    outgoing = jnp.stack(
        [jnp.dot(p, observations, preferred_element_type=jnp.float32).astype(jnp.bfloat16) for p in picks], axis=1
    )
    received = lax.all_to_all(outgoing, exchange, 0, 0, axis_index_groups=groups, tiled=True)
    visiting = scaled_rows(received.reshape(2 * n_agents, width), gain)
    answers = sum(partial_values(visiting, w, h) for w, h in pieces)
    returned = lax.all_to_all(
        answers.reshape(n_agents, 2), exchange, 0, 0, axis_index_groups=groups, tiled=True
    )
    resident = scaled_rows(observations, gain)
    own_value = sum(partial_values(resident, w, h) for w, h in pieces)
    chosen = jnp.where(second[:, None] == 0, returned[None, :, 0], returned[None, :, 1])
    opponent_value = jnp.sum(jnp.where(named.T, chosen, 0.0), axis=1)
    return own_value, opponent_value


def solution(mesh):
    wide = Mesh(mesh.devices.reshape(NZ, NXH, NY, NXL, NC), AXES)
    league, rep = AXES[:3], AXES[3:]
    return jax.shard_map(
        per_device,
        mesh=wide,
        in_specs=(
            P(AXES, None),
            P(league, None, rep),
            P(league, None),
            P(league, rep),
            P(AXES, None),
            P(AXES),
        ),
        out_specs=(P(AXES), P(AXES)),
        check_vma=False,
    )
```

time: 160 us -> 147 us (0.919)
  waiting for transfers between devices: 81.5 us -> 8.3 us
  blocking collectives: 5.93 us -> 43.6 us
  starting transfers between devices: 36.6 us -> 52.9 us
  matrix products: 11.7 us -> 27 us
  between operations: 14.2 us -> 1.1 us
  other arithmetic: 2.73 us -> 5.73 us
    all_gather x1 -> x0, waiting for transfers between devices: 48.6 us -> none  [per_device(): lax.all_gather(weight_cols, 'rep', axis=1, tiled=True)]
    all_gather x1, blocking collectives: 5.93 us -> 43.6 us  [per_device(): head_all = lax.all_gather(heads[0], ('xl', 'c'), axis=0, tiled=False)]
    all_to_all x2, waiting for transfers between devices: 32.3 us -> 8.28 us  [the longest x1 8.27 us: per_device(): lax.all_to_all(answers.reshape(n_agents, 2), exchange, 0, 0, axis_index_g...]
    ppermute x0 -> x7, starting transfers between devices: none -> 16.8 us  [the longest x3 7.19 us: per_device(): chunk = lax.ppermute(own_w[:, start:start + size], 'xl', SWAP)]
    dot_general x3 -> x18, matrix products: 11.7 us -> 27 us  [the longest x16 24.3 us: partial_values(): jnp.dot(scaled, weight, preferred_element_type=jnp.float32)]
    slice x1 -> x3, local copies, waits for them, and re-layouts: 0.1 us -> 2.32 us  [the longest x2 2.15 us: per_device(): chunk = lax.ppermute(own_w[:, start:start + size], 'xl', SWAP)]
    another operation x0 -> x1, local copies, waits for them, and re-layouts: none -> 2.05 us  [per_device(): jnp.stack([jnp.dot(p, observations, preferred_element_type=jnp.float32).a...]
    scatter x1 -> x0, local copies, waits for them, and re-layouts: 1.72 us -> none  [per_device(): outgoing = jnp.zeros((n_league * capacity + 1, feature_width), jnp.bfloat...]
  transfers between devices with their start and end apart: 3 -> 9, of which waited for: 3 -> 1; matrix products, arithmetic and copies ran while one was open for 7% -> 19% of each run, Pallas kernels for 0% -> 0%
where the time goes in v1:
time: 147 us; the launch traced here: 146 us
  starting transfers between devices  52.9 us (36%)
  blocking collectives  43.6 us (30%)
  matrix products  27 us (18%)
  waiting for transfers between devices  8.3 us (6%)
  local copies, waits for them, and re-layouts  6.89 us (5%)
  other arithmetic  5.73 us (4%)
    all_gather x1, blocking collectives, per_device(): head_all = lax.all_gather(heads[0], ('xl', 'c'), axis=0, tiled=False)  43.6 us
    dot_general x16, matrix products, partial_values(): jnp.dot(scaled, weight, preferred_element_type=jnp.float32)  24.3 us
    all_to_all x1, starting transfers between devices, per_device(): lax.all_to_all(outgoing, exchange, 0, 0, axis_index_groups=groups, tiled=...  20.6 us
    all_to_all x1, starting transfers between devices, per_device(): lax.all_to_all(answers.reshape(n_agents, 2), exchange, 0, 0, axis_index_g...  15.6 us
    all_to_all x1, waiting for transfers between devices, per_device(): lax.all_to_all(answers.reshape(n_agents, 2), exchange, 0, 0, axis_index_g...  8.27 us
    ppermute x3, starting transfers between devices, per_device(): chunk = lax.ppermute(own_w[:, start:start + size], 'xl', SWAP)  7.19 us
    ppermute x3, starting transfers between devices, per_device(): far_sib_w.append(lax.ppermute(chunk, 'c', SWAP))  6.62 us
    ppermute x1, starting transfers between devices, per_device(): sib_w = lax.ppermute(own_w, 'c', SWAP)  2.99 us
  transfers between devices with their start and end apart: 9, of which 1 were waited for; matrix products, arithmetic and copies ran while one was open for 19% of the time, Pallas kernels for 0%

profile of v1, /device:TPU:1, one launch (start us, length us, event | category | flops | bytes accessed | tf_op | source)
XLA Modules:
  0.0 145.5 jit_solution(2284164862693433335)
XLA Ops:
  0.6 0.7 broadcast_compare_fusion.2
  1.3 0.9 convert_reduce_fusion
  2.2 1.3 fusion.1
  3.6 1.3 fusion
  4.9 0.1 pad_maximum_fusion
  5.0 2.1 %copy.19 = bf16[128,2,2048]{2,1,0:T(2,128)(2,1)} copy(bf16[128,2,2048]{2,0,1:T(8,128)(2,1)S(1)} %pad_maximum_fusion) | data formatting | bytes 2097152 | tf_op jit(solution)/shard_map/stack | solution.py:74
  7.1 20.6 %all-to-all-start = ((bf16[128,2,2048]{2,1,0:T(2,128)(2,1)}), bf16[128,2,2048]{2,1,0:T(2,128)(2,1)S(1)}, u32[]{:S(2)}, u32[]{:S(2)}) async-start(bf16[128,2,2048]{2,1,0:T(2,128)(2,1)} %copy.19), calls=%async_computation | async-start | bytes 2097152 | tf_op jit(solution)/shard_map/all_to_all | solution.py:77
  27.6 0.0 copy-start.2
  27.7 0.0 copy-start.8
  27.7 0.0 copy-start
  27.7 0.0 copy-start.6
  27.7 3.0 %collective-permute-start = (bf16[2048,512]{1,0:T(8,128)(2,1)}, bf16[2048,512]{1,0:T(8,128)(2,1)}, u32[]{:S(2)}, u32[]{:S(2)}) collective-permute-start(bf16[2048,512]{1,0:T(8,128)(2,1)} %bitcast.70), channel_id=1, source_target_pairs={{0,1},{1,0},{2,3},{3,2},{4,5},{5,4},{6,7},{7,6},{8,9},{9,8},{10,11... | collective-permute-start | bytes 6291464 | tf_op jit(solution)/shard_map/ppermute | solution.py:43
  30.7 2.1 %fusion.60 = (bf16[2048,128]{1,0:T(8,128)(2,1)}, bf16[2048,128]{1,0:T(8,128)(2,1)S(1)}) fusion(bf16[2048,512]{1,0:T(8,128)(2,1)} %bitcast.71), kind=kLoop, calls=%fused_computation.79 | loop fusion | bytes 2097152 | tf_op jit(solution)/shard_map/slice | solution.py:46
  32.8 1.9 %collective-permute-start.3 = (bf16[2048,128]{1,0:T(8,128)(2,1)}, bf16[2048,128]{1,0:T(8,128)(2,1)}, u32[]{:S(2)}, u32[]{:S(2)}) collective-permute-start(bf16[2048,128]{1,0:T(8,128)(2,1)} %get-tuple-element.4), channel_id=1, source_target_pairs={{0,2},{2,0},{1,3},{3,1},{4,6},{6,4},{5,7},{7,5},{8,10},{10,8},{9,1... | collective-permute-start | bytes 1572872 | tf_op jit(solution)/shard_map/ppermute | solution.py:46
  34.7 3.4 %collective-permute-start.5 = (bf16[2048,128]{1,0:T(8,128)(2,1)S(1)}, bf16[2048,128]{1,0:T(8,128)(2,1)}, u32[]{:S(2)}, u32[]{:S(2)}) collective-permute-start(bf16[2048,128]{1,0:T(8,128)(2,1)S(1)} %get-tuple-element.5), channel_id=1, source_target_pairs={{0,2},{2,0},{1,3},{3,1},{4,6},{6,4},{5,7},{7,5},{8,10},{10,8},{9,1... | collective-permute-start | bytes 1572872 | tf_op jit(solution)/shard_map/ppermute | solution.py:46
  38.1 0.1 slice.50
  38.1 1.9 %collective-permute-start.1 = (bf16[2048,256]{1,0:T(8,128)(2,1)S(1)}, bf16[2048,256]{1,0:T(8,128)(2,1)}, u32[]{:S(2)}, u32[]{:S(2)}) collective-permute-start(bf16[2048,256]{1,0:T(8,128)(2,1)S(1)} %slice.50), channel_id=1, source_target_pairs={{0,2},{2,0},{1,3},{3,1},{4,6},{6,4},{5,7},{7,5},{8,10},{10,8},{9,1... | collective-permute-start | bytes 3145736 | tf_op jit(solution)/shard_map/ppermute | solution.py:46
  40.1 43.6 %all-gather = bf16[4,1,512]{2,1,0:T(2,128)(2,1)S(1)} all-gather(bf16[1,1,512]{2,1,0:T(2,128)(2,1)S(1)} %bitcast.88), channel_id=1, replica_groups=mesh['z'=8,'xh'=2,'y'=8,'xl'=2,'c'=2] {'xl','c'}, dimensions={0}, use_global_device_ids=true | all-gather | bytes 5120 | tf_op jit(solution)/shard_map/all_gather | solution.py:50
  83.7 0.0 copy-done
  83.7 0.2 fusion.2
  83.9 0.0 copy-done.6
  84.0 2.2 %multiply_reduce_fusion.6 = f32[128]{0:T(128)S(1)} fusion(f32[512]{0:T(512)S(1)} %bitcast.91, bf16[1,2048,512]{2,1,0:T(8,128)(2,1)} %param.7, bf16[128,2048]{1,0:T(8,128)(2,1)S(1)} %copy-done, f32[2048]{0:T(1024)S(1)} %bitcast.74, f32[128]{0:T(128)S(1)} %add_rsqrt_fusion.1), kind=kOutput, calls=%fused_computation.18 | convolution fusion | flops 269877120 | bytes 2632704 | tf_op jit(solution)/shard_map/dot_general | solution.py:31
  86.2 0.0 collective-permute-done.3
  86.2 2.1 %collective-permute-start.4 = (bf16[2048,128]{1,0:T(8,128)(2,1)}, bf16[2048,128]{1,0:T(8,128)(2,1)S(1)}, u32[]{:S(2)}, u32[]{:S(2)}) collective-permute-start(bf16[2048,128]{1,0:T(8,128)(2,1)} %collective-permute-done.3), channel_id=1, source_target_pairs={{0,1},{1,0},{2,3},{3,2},{4,5},{5,4},{6,7},{7,6},{8,9},{9,8},{10,11... | collective-permute-start | bytes 1572872 | tf_op jit(solution)/shard_map/ppermute | solution.py:48
  88.3 0.0 collective-permute-done.5
  88.3 2.2 %collective-permute-start.6 = (bf16[2048,128]{1,0:T(8,128)(2,1)}, bf16[2048,128]{1,0:T(8,128)(2,1)S(1)}, u32[]{:S(2)}, u32[]{:S(2)}) collective-permute-start(bf16[2048,128]{1,0:T(8,128)(2,1)} %collective-permute-done.5), channel_id=1, source_target_pairs={{0,1},{1,0},{2,3},{3,2},{4,5},{5,4},{6,7},{7,6},{8,9},{9,8},{10,11... | collective-permute-start | bytes 1572872 | tf_op jit(solution)/shard_map/ppermute | solution.py:48
  90.5 1.5 %multiply_reduce_fusion.16 = f32[128]{0:T(128)S(1)} fusion(f32[128]{0:T(128)S(1)} %get-tuple-element.9, bf16[2048,128]{1,0:T(8,128)(2,1)} %collective-permute-done.3, bf16[128,2048]{1,0:T(8,128)(2,1)S(1)} %copy-done, f32[2048]{0:T(1024)S(1)} %bitcast.75, f32[128]{0:T(128)S(1)} %add_rsqrt_fusion.1), kind=kOutput, calls=%fused_computation.36 | convolution fusion | flops 68255616 | bytes 1058304 | tf_op jit(solution)/shard_map/dot_general | solution.py:31
  92.0 1.5 %multiply_reduce_fusion.14 = f32[128]{0:T(128)S(1)} fusion(f32[128]{0:T(128)S(1)} %get-tuple-element.10, bf16[2048,128]{1,0:T(8,128)(2,1)} %collective-permute-done.5, bf16[128,2048]{1,0:T(8,128)(2,1)S(1)} %copy-done, f32[2048]{0:T(1024)S(1)} %bitcast.76, f32[128]{0:T(128)S(1)} %add_rsqrt_fusion.1), kind=kOutput, calls=%fused_computation.34 | convolution fusion | flops 68255616 | bytes 1058304 | tf_op jit(solution)/shard_map/dot_general | solution.py:31
  93.5 0.0 collective-permute-done.1
  93.5 2.3 %collective-permute-start.2 = (bf16[2048,256]{1,0:T(8,128)(2,1)}, bf16[2048,256]{1,0:T(8,128)(2,1)}, u32[]{:S(2)}, u32[]{:S(2)}) collective-permute-start(bf16[2048,256]{1,0:T(8,128)(2,1)} %collective-permute-done.1), channel_id=1, source_target_pairs={{0,1},{1,0},{2,3},{3,2},{4,5},{5,4},{6,7},{7,6},{8,9},{9,8},{10,11... | collective-permute-start | bytes 3145736 | tf_op jit(solution)/shard_map/ppermute | solution.py:48
  95.8 0.0 collective-permute-done.4
  95.8 0.4 multiply_reduce_fusion.15
  96.2 0.0 collective-permute-done.6
  96.2 0.4 multiply_reduce_fusion.13
  96.7 1.7 %multiply_reduce_fusion.12 = f32[128]{0:T(128)S(1)} fusion(f32[256]{0:T(256)S(1)} %bitcast.95, bf16[2048,256]{1,0:T(8,128)(2,1)} %collective-permute-done.1, bf16[128,2048]{1,0:T(8,128)(2,1)S(1)} %copy-done, f32[2048]{0:T(1024)S(1)} %bitcast.79, f32[128]{0:T(128)S(1)} %add_rsqrt_fusion.1), kind=kOutput, calls=%fused_computation.24 | convolution fusion | flops 135462784 | bytes 1583104 | tf_op jit(solution)/shard_map/dot_general | solution.py:31
  98.4 0.0 all-to-all-done
  98.4 1.2 multiply_reduce_fusion
  99.6 0.1 rsqrt.22
  99.7 0.3 reshape.165
  100.0 0.2 multiply_convert_fusion
  100.3 2.0 %multiply_reduce_fusion.10 = f32[256]{0:T(256)S(1)} fusion(f32[128]{0:T(128)S(1)} %get-tuple-element.9, bf16[256,2048]{1,0:T(8,128)(2,1)S(1)} %multiply_convert_fusion, bf16[2048,128]{1,0:T(8,128)(2,1)} %collective-permute-done.3), kind=kOutput, calls=%fused_computation.22 | convolution fusion | flops 134414080 | bytes 1574400 | tf_op jit(solution)/shard_map/dot_general | solution.py:31
  102.3 1.2 multiply_convert_fusion.1
  103.5 0.5 multiply_reduce_fusion.9
  104.0 0.4 convert_element_type.66
  104.5 0.8 copy-done.5
  105.2 1.6 %multiply_reduce_fusion.8 = f32[256]{0:T(256)S(1)} fusion(f32[128]{0:T(128)S(1)} %get-tuple-element.10, bf16[256,2048]{1,0:T(8,128)(2,1)S(1)} %copy-done.5, bf16[2048,128]{1,0:T(8,128)(2,1)} %collective-permute-done.5), kind=kOutput, calls=%fused_computation.20 | convolution fusion | flops 134414080 | bytes 1574400 | tf_op jit(solution)/shard_map/dot_general | solution.py:31
  106.8 0.0 copy-start.3
  106.8 1.7 %multiply_reduce_fusion.7 = f32[256]{0:T(256)S(1)} fusion(f32[128]{0:T(128)S(1)} %get-tuple-element.12, bf16[256,2048]{1,0:T(8,128)(2,1)S(1)} %copy-done.5, bf16[2048,128]{1,0:T(8,128)(2,1)} %copy-done.11), kind=kOutput, calls=%fused_computation.19 | convolution fusion | flops 134414080 | bytes 1574400 | tf_op jit(solution)/shard_map/dot_general | solution.py:31
  108.5 1.8 %multiply_reduce_fusion.4 = f32[256]{0:T(256)S(1)} fusion(f32[256]{0:T(256)S(1)} %bitcast.96, bf16[256,2048]{1,0:T(8,128)(2,1)S(1)} %copy-done.5, bf16[2048,256]{1,0:T(8,128)(2,1)} %collective-permute-done.1), kind=kOutput, calls=%fused_computation.16 | convolution fusion | flops 268828416 | bytes 2099200 | tf_op jit(solution)/shard_map/dot_general | solution.py:31
  110.3 0.9 multiply_reduce_fusion.2
  111.2 0.0 collective-permute-done.2
  111.2 1.8 %multiply_reduce_fusion.3 = f32[256]{0:T(256)S(1)} fusion(f32[256]{0:T(256)S(1)} %bitcast.93, bf16[256,2048]{1,0:T(8,128)(2,1)S(1)} %copy-done.5, bf16[2048,256]{1,0:T(8,128)(2,1)} %collective-permute-done.2), kind=kOutput, calls=%fused_computation.15 | convolution fusion | flops 268828416 | bytes 2099200 | tf_op jit(solution)/shard_map/dot_general | solution.py:31
  113.0 0.0 collective-permute-done
  113.0 0.0 copy-start.1
  113.0 2.5 %multiply_reduce_fusion.1 = f32[256]{0:T(256)S(1)} fusion(f32[512]{0:T(512)S(1)} %bitcast.89, bf16[256,2048]{1,0:T(8,128)(2,1)S(1)} %copy-done.5, bf16[2048,512]{1,0:T(8,128)(2,1)} %collective-permute-done), kind=kOutput, calls=%fused_computation.13 | convolution fusion | flops 537657088 | bytes 3148800 | tf_op jit(solution)/shard_map/dot_general | solution.py:31
  115.6 0.8 reshape.168
  116.3 15.6 %all-to-all-start.1 = ((f32[128,1,2]{2,1,0:T(1,128)}), f32[128,1,2]{2,1,0:T(1,128)S(1)}, u32[]{:S(2)}, u32[]{:S(2)}) async-start(f32[128,1,2]{2,1,0:T(1,128)} %bitcast.20), calls=%async_computation.1 | async-start | bytes 131072 | tf_op jit(solution)/shard_map/all_to_all | solution.py:80
  131.9 1.7 %multiply_reduce_fusion.11 = f32[128]{0:T(128)S(1)} fusion(f32[256]{0:T(256)S(1)} %bitcast.94, bf16[2048,256]{1,0:T(8,128)(2,1)} %collective-permute-done.2, bf16[128,2048]{1,0:T(8,128)(2,1)S(1)} %copy-done.1, f32[2048]{0:T(1024)S(1)} %bitcast.82, f32[128]{0:T(128)S(1)} %add_rsqrt_fusion.1), kind=kOutput, calls=%fused_computation.23 | convolution fusion | flops 135462784 | bytes 1583104 | tf_op jit(solution)/shard_map/dot_general | solution.py:31
  133.6 0.0 copy-start.7
  133.6 2.2 %multiply_reduce_fusion.5 = f32[128]{0:T(128)S(1)} fusion(f32[512]{0:T(512)S(1)} %bitcast.90, bf16[2048,512]{1,0:T(8,128)(2,1)} %collective-permute-done, bf16[128,2048]{1,0:T(8,128)(2,1)S(1)} %copy-done.1, f32[2048]{0:T(1024)S(1)} %bitcast.83, f32[128]{0:T(128)S(1)} %add_rsqrt_fusion.1), kind=kOutput, calls=%fused_computation.17 | convolution fusion | flops 269877120 | bytes 2632704 | tf_op jit(solution)/shard_map/dot_general | solution.py:31
  135.8 0.5 add_add_fusion.1
  136.4 8.3 %all-to-all-done.1 = f32[128,1,2]{2,1,0:T(1,128)S(1)} async-done(((f32[128,1,2]{2,1,0:T(1,128)}), f32[128,1,2]{2,1,0:T(1,128)S(1)}, u32[]{:S(2)}, u32[]{:S(2)}) %all-to-all-start.1) | async-done | bytes 1056 | tf_op jit(solution)/shard_map/all_to_all | solution.py:80
  144.6 0.2 slice_reduce_fusion.1
  144.8 0.7 select_reduce_fusion
  (24 shorter events, 0.1 us)
Async XLA Ops:
  7.1 91.3 %all-to-all-start = ((bf16[128,2,2048]{2,1,0:T(2,128)(2,1)}), bf16[128,2,2048]{2,1,0:T(2,128)(2,1)S(1)}, u32[]{:S(2)}, u32[]{:S(2)}) async-start(bf16[128,2,2048]{2,1,0:T(2,128)(2,1)} %copy.19), calls=%async_computation | async-start | bytes 2097152 | tf_op jit(solution)/shard_map/all_to_all | solution.py:77
  27.6 10.4 %copy-start.2 = (bf16[1,2048,512]{2,1,0:T(8,128)(2,1)S(1)}, bf16[1,2048,512]{2,1,0:T(8,128)(2,1)}, u32[]{:S(2)}) copy-start(bf16[1,2048,512]{2,1,0:T(8,128)(2,1)} %param.7) | copy-start | bytes 6291460
  27.7 12.4 %copy-start.8 = (bf16[1,512]{1,0:T(2,128)(2,1)S(1)}, bf16[1,512]{1,0:T(2,128)(2,1)}, u32[]{:S(2)}) copy-start(bf16[1,512]{1,0:T(2,128)(2,1)} %param.9) | copy-start | bytes 3076
  27.7 56.1 %copy-start = (bf16[128,2048]{1,0:T(8,128)(2,1)S(1)}, bf16[128,2048]{1,0:T(8,128)(2,1)}, u32[]{:S(2)}) copy-start(bf16[128,2048]{1,0:T(8,128)(2,1)} %param.6) | copy-start | bytes 1572868
  27.7 56.3 %copy-start.6 = (f32[1,2048]{1,0:T(1,128)S(1)}, f32[1,2048]{1,0:T(1,128)}, u32[]{:S(2)}) copy-start(f32[1,2048]{1,0:T(1,128)} %param.8) | copy-start | bytes 24580
  27.7 85.3 %collective-permute-start = (bf16[2048,512]{1,0:T(8,128)(2,1)}, bf16[2048,512]{1,0:T(8,128)(2,1)}, u32[]{:S(2)}, u32[]{:S(2)}) collective-permute-start(bf16[2048,512]{1,0:T(8,128)(2,1)} %bitcast.70), channel_id=1, source_target_pairs={{0,1},{1,0},{2,3},{3,2},{4,5},{5,4},{6,7},{7,6},{8,9},{9,8},{10,11... | collective-permute-start | bytes 6291464 | tf_op jit(solution)/shard_map/ppermute | solution.py:43
  32.8 53.4 %collective-permute-start.3 = (bf16[2048,128]{1,0:T(8,128)(2,1)}, bf16[2048,128]{1,0:T(8,128)(2,1)}, u32[]{:S(2)}, u32[]{:S(2)}) collective-permute-start(bf16[2048,128]{1,0:T(8,128)(2,1)} %get-tuple-element.4), channel_id=1, source_target_pairs={{0,2},{2,0},{1,3},{3,1},{4,6},{6,4},{5,7},{7,5},{8,10},{10,8},{9,1... | collective-permute-start | bytes 1572872 | tf_op jit(solution)/shard_map/ppermute | solution.py:46
  34.7 53.6 %collective-permute-start.5 = (bf16[2048,128]{1,0:T(8,128)(2,1)S(1)}, bf16[2048,128]{1,0:T(8,128)(2,1)}, u32[]{:S(2)}, u32[]{:S(2)}) collective-permute-start(bf16[2048,128]{1,0:T(8,128)(2,1)S(1)} %get-tuple-element.5), channel_id=1, source_target_pairs={{0,2},{2,0},{1,3},{3,1},{4,6},{6,4},{5,7},{7,5},{8,10},{10,8},{9,1... | collective-permute-start | bytes 1572872 | tf_op jit(solution)/shard_map/ppermute | solution.py:46
  38.1 55.3 %collective-permute-start.1 = (bf16[2048,256]{1,0:T(8,128)(2,1)S(1)}, bf16[2048,256]{1,0:T(8,128)(2,1)}, u32[]{:S(2)}, u32[]{:S(2)}) collective-permute-start(bf16[2048,256]{1,0:T(8,128)(2,1)S(1)} %slice.50), channel_id=1, source_target_pairs={{0,2},{2,0},{1,3},{3,1},{4,6},{6,4},{5,7},{7,5},{8,10},{10,8},{9,1... | collective-permute-start | bytes 3145736 | tf_op jit(solution)/shard_map/ppermute | solution.py:46
  86.2 9.6 %collective-permute-start.4 = (bf16[2048,128]{1,0:T(8,128)(2,1)}, bf16[2048,128]{1,0:T(8,128)(2,1)S(1)}, u32[]{:S(2)}, u32[]{:S(2)}) collective-permute-start(bf16[2048,128]{1,0:T(8,128)(2,1)} %collective-permute-done.3), channel_id=1, source_target_pairs={{0,1},{1,0},{2,3},{3,2},{4,5},{5,4},{6,7},{7,6},{8,9},{9,8},{10,11... | collective-permute-start | bytes 1572872 | tf_op jit(solution)/shard_map/ppermute | solution.py:48
  88.3 7.9 %collective-permute-start.6 = (bf16[2048,128]{1,0:T(8,128)(2,1)}, bf16[2048,128]{1,0:T(8,128)(2,1)S(1)}, u32[]{:S(2)}, u32[]{:S(2)}) collective-permute-start(bf16[2048,128]{1,0:T(8,128)(2,1)} %collective-permute-done.5), channel_id=1, source_target_pairs={{0,1},{1,0},{2,3},{3,2},{4,5},{5,4},{6,7},{7,6},{8,9},{9,8},{10,11... | collective-permute-start | bytes 1572872 | tf_op jit(solution)/shard_map/ppermute | solution.py:48
  93.5 17.7 %collective-permute-start.2 = (bf16[2048,256]{1,0:T(8,128)(2,1)}, bf16[2048,256]{1,0:T(8,128)(2,1)}, u32[]{:S(2)}, u32[]{:S(2)}) collective-permute-start(bf16[2048,256]{1,0:T(8,128)(2,1)} %collective-permute-done.1), channel_id=1, source_target_pairs={{0,1},{1,0},{2,3},{3,2},{4,5},{5,4},{6,7},{7,6},{8,9},{9,8},{10,11... | collective-permute-start | bytes 3145736 | tf_op jit(solution)/shard_map/ppermute | solution.py:48
  95.8 0.9 copy-start.9
  96.2 3.3 %copy-start.11 = (bf16[2048,128]{1,0:T(8,128)(2,1)}, bf16[2048,128]{1,0:T(8,128)(2,1)S(1)}, u32[]{:S(2)}) copy-start(bf16[2048,128]{1,0:T(8,128)(2,1)S(1)} %collective-permute-done.6) | copy-start | bytes 1572868
  100.3 3.2 %copy-start.4 = (bf16[256,2048]{1,0:T(8,128)(2,1)}, bf16[256,2048]{1,0:T(8,128)(2,1)S(1)}, u32[]{:S(2)}) copy-start(bf16[256,2048]{1,0:T(8,128)(2,1)S(1)} %multiply_convert_fusion) | copy-start | bytes 3145732
  100.3 3.2 %copy-start.10 = (bf16[2048,128]{1,0:T(8,128)(2,1)S(1)}, bf16[2048,128]{1,0:T(8,128)(2,1)}, u32[]{:S(2)}) copy-start(bf16[2048,128]{1,0:T(8,128)(2,1)} %copy-done.9) | copy-start | bytes 1572868
  104.0 1.2 copy-start.5
  106.8 3.5 %copy-start.3 = (bf16[1,2048,512]{2,1,0:T(8,128)(2,1)S(1)}, bf16[1,2048,512]{2,1,0:T(8,128)(2,1)}, u32[]{:S(2)}) copy-start(bf16[1,2048,512]{2,1,0:T(8,128)(2,1)} %param.7) | copy-start | bytes 6291460
  113.0 18.9 %copy-start.1 = (bf16[128,2048]{1,0:T(8,128)(2,1)S(1)}, bf16[128,2048]{1,0:T(8,128)(2,1)}, u32[]{:S(2)}) copy-start(bf16[128,2048]{1,0:T(8,128)(2,1)} %param.6) | copy-start | bytes 1572868
  116.3 28.3 %all-to-all-start.1 = ((f32[128,1,2]{2,1,0:T(1,128)}), f32[128,1,2]{2,1,0:T(1,128)S(1)}, u32[]{:S(2)}, u32[]{:S(2)}) async-start(f32[128,1,2]{2,1,0:T(1,128)} %bitcast.20), calls=%async_computation.1 | async-start | bytes 131072 | tf_op jit(solution)/shard_map/all_to_all | solution.py:80
  133.6 11.2 %copy-start.7 = (s32[128,1]{0,1:T(1,128)S(1)}, s32[128,1]{0,1:T(1,128)}, u32[]{:S(2)}) copy-start(s32[128,1]{0,1:T(1,128)} %param.10) | copy-start | bytes 1540

commit v2 on v1

v2 whole, which is shorter than its diff:
```python
import functools

import jax
import jax.numpy as jnp
from jax import lax
from jax.experimental import pallas as pl
from jax.experimental.pallas import tpu as pltpu
from jax.sharding import Mesh, PartitionSpec as P

NZ, NXH, NY, NXL, NC = 8, 2, 8, 2, 2
AXES = ("z", "xh", "y", "xl", "c")
SWAP = [(0, 1), (1, 0)]
CHUNKS = (256, 256)
PAD = 8
COST_EARLY = 5
VMEM_LIMIT = 40 * 1024 * 1024


def exchange_groups():
    groups = []
    for flip in range(2):
        group = []
        for z in range(NZ):
            for xh in range(NXH):
                for y in range(NY):
                    group.append(((z * NXH + xh) * NY + y) * NXL + (xh ^ flip))
        groups.append(group)
    return groups


def hint(weight):
    return pl.CostEstimate(flops=weight * 1_000_000_000, bytes_accessed=0, transcendentals=0)


def whole(shape):
    return pl.BlockSpec(shape, lambda *_: (0,) * len(shape))


def fill_slots(owner_ref, valid_ref, rows_ref, out_ref):
    count = owner_ref.shape[1]
    agents = out_ref.shape[0]
    owner = owner_ref[...]
    live = valid_ref[...]
    owner_down = jnp.broadcast_to(owner, (count, count)).T
    live_down = jnp.broadcast_to(live, (count, count)).T
    down = lax.broadcasted_iota(jnp.int32, (count, count), 0)
    across = lax.broadcasted_iota(jnp.int32, (count, count), 1)
    earlier = (owner_down == owner) & (live_down == 1) & (down < across)
    slot = jnp.sum(earlier.astype(jnp.int32), axis=0, keepdims=True)
    agent = lax.broadcasted_iota(jnp.int32, (agents, count), 0)
    named = (agent == owner) & (live == 1)
    rows = rows_ref[...]
    for k in range(2):
        pick = (named & (slot == k)).astype(jnp.float32).astype(jnp.bfloat16)
        out_ref[:, k, :] = jnp.dot(pick, rows, preferred_element_type=jnp.float32).astype(jnp.bfloat16)


def slots_call(owner, valid, rows, agents):
    count, width = rows.shape
    return pl.pallas_call(
        fill_slots,
        out_shape=jax.ShapeDtypeStruct((agents, 2, width), jnp.bfloat16),
        compiler_params=pltpu.CompilerParams(vmem_limit_bytes=VMEM_LIMIT),
        cost_estimate=hint(200),
        name="fill_slots",
    )(owner, valid, rows)


def scaled_rows(rows, gain):
    wide = rows.astype(jnp.float32)
    squares = jnp.mean(wide * wide, axis=1, keepdims=True)
    return (wide * lax.rsqrt(squares + 1e-06) * gain).astype(jnp.bfloat16)


def partial_values(scaled, weight, head):
    hidden = jnp.dot(scaled, weight, preferred_element_type=jnp.float32)
    half = 0.5 * hidden
    return jnp.sum((half + half * jnp.tanh(half)) * head.astype(jnp.float32), axis=1, keepdims=True)


def score_near(slotted, x_ref, gain_ref, w0_ref, h0_ref, w1_ref, h1_ref, scaled_ref, value_ref):
    @pl.when(pl.program_id(0) == 0)
    def _():
        gain = gain_ref[...]
        if slotted:
            count = x_ref.shape[0]
            for k in range(2):
                scaled_ref[k * count : (k + 1) * count, :] = scaled_rows(x_ref[:, k, :], gain)
        else:
            scaled_ref[...] = scaled_rows(x_ref[...], gain)
        value_ref[...] = jnp.zeros_like(value_ref)

    scaled = scaled_ref[...]
    value_ref[...] += partial_values(scaled, w0_ref[...], h0_ref[...]) + partial_values(scaled, w1_ref[...], h1_ref[...])


def near_call(x, gain, own_w, own_h, sib_w, sib_h, slotted, step=256):
    rows = x.shape[0] * 2 if slotted else x.shape[0]
    width, units = own_w.shape
    w_spec = pl.BlockSpec((width, step), lambda j: (0, j))
    h_spec = pl.BlockSpec((1, step), lambda j: (0, j))
    return pl.pallas_call(
        functools.partial(score_near, slotted),
        grid=(units // step,),
        in_specs=[whole(x.shape), whole(gain.shape), w_spec, h_spec, w_spec, h_spec],
        out_specs=[whole((rows, width)), whole((rows, 1))],
        out_shape=[jax.ShapeDtypeStruct((rows, width), jnp.bfloat16), jax.ShapeDtypeStruct((rows, 1), jnp.float32)],
        compiler_params=pltpu.CompilerParams(vmem_limit_bytes=VMEM_LIMIT),
        cost_estimate=hint(0),
        name="score_near",
    )(x, gain, own_w, own_h, sib_w, sib_h)


def score_far(slotted, scaled_ref, near_ref, *refs):
    *chunk_refs, out_ref, value_ref = refs
    step = pl.program_id(0)

    @pl.when(step == 0)
    def _():
        value_ref[...] = near_ref[...]

    scaled = scaled_ref[...]
    total = value_ref[...]
    for w_ref, h_ref in zip(chunk_refs[::2], chunk_refs[1::2]):
        total += partial_values(scaled, w_ref[...], h_ref[0:1, :])
    value_ref[...] = total

    @pl.when(step == pl.num_programs(0) - 1)
    def _():
        if slotted:
            half = total.shape[0] // 2
            out_ref[:, 0:1] = total[:half]
            out_ref[:, 1:2] = total[half:]
        else:
            out_ref[...] = total


def far_call(scaled, near, chunks, slotted, weight, steps=2):
    rows, width = scaled.shape
    specs, args, units = [], [], 0
    for chunk in chunks:
        step = chunk.shape[1] // steps
        specs += [pl.BlockSpec((width, step), lambda j: (0, j)), pl.BlockSpec((PAD, step), lambda j: (width // PAD, j))]
        args += [chunk, chunk]
        units += chunk.shape[1]
    out = (rows // 2, 2) if slotted else (rows, 1)
    return pl.pallas_call(
        functools.partial(score_far, slotted),
        grid=(steps,),
        in_specs=[whole(scaled.shape), whole(near.shape)] + specs,
        out_specs=whole(out),
        out_shape=jax.ShapeDtypeStruct(out, jnp.float32),
        scratch_shapes=[pltpu.VMEM((rows, 1), jnp.float32)],
        compiler_params=pltpu.CompilerParams(vmem_limit_bytes=VMEM_LIMIT),
        cost_estimate=hint(weight),
        name="score_far",
    )(scaled, near, *args)


def per_device(observations, weights, gains, heads, pairing, valid):
    rows_dev, width = observations.shape
    n_agents = NZ * NXH * NY
    groups = exchange_groups()
    own_w = weights[0]
    exchange = ("z", "xh", "y", "xl")

    def pack(start, stop):
        head = jnp.broadcast_to(heads[:, start:stop], (PAD, stop - start))
        return jnp.concatenate([own_w[:, start:stop], head], axis=0)

    first = lax.ppermute(pack(0, CHUNKS[0]), "xl", SWAP)
    second = lax.ppermute(pack(CHUNKS[0], sum(CHUNKS)), "xl", SWAP)
    outgoing = slots_call(pairing.reshape(1, rows_dev), valid.reshape(1, rows_dev), observations, n_agents)
    near_w, near_h, outgoing = lax.optimization_barrier((own_w, heads, outgoing))
    sib_w = lax.ppermute(near_w, "c", SWAP)
    sib_h = lax.ppermute(near_h, "c", SWAP)
    early = (first, lax.ppermute(first, "c", SWAP))
    own_scaled, own = near_call(observations, gains, own_w, heads, sib_w, sib_h, False)
    own = far_call(own_scaled, own, early, False, 0)
    second, own, own_scaled = lax.optimization_barrier((second, own, own_scaled))
    late = (second, lax.ppermute(second, "c", SWAP))

    received = lax.all_to_all(outgoing, exchange, 0, 0, axis_index_groups=groups, tiled=True)
    visit_scaled, visit = near_call(received, gains, own_w, heads, sib_w, sib_h, True)
    visit = far_call(visit_scaled, visit, early, False, COST_EARLY)
    answers = far_call(visit_scaled, visit, late, True, 0)
    returned = lax.all_to_all(answers, exchange, 0, 0, axis_index_groups=groups, tiled=True)
    own_value = far_call(own_scaled, own, late, False, 0)[:, 0]

    owner = pairing[:, 0]
    is_live = valid == 1
    row_iota = jnp.arange(rows_dev, dtype=jnp.int32)
    same = (owner[:, None] == owner[None, :]) & (row_iota[None, :] < row_iota[:, None]) & is_live[None, :]
    second = jnp.sum(same.astype(jnp.int32), axis=1)
    agent_iota = jnp.arange(n_agents, dtype=jnp.int32)
    chosen = jnp.where(second[:, None] == 0, returned[None, :, 0], returned[None, :, 1])
    named = (owner[:, None] == agent_iota[None, :]) & is_live[:, None]
    opponent_value = jnp.sum(jnp.where(named, chosen, 0.0), axis=1)
    return own_value, opponent_value


def solution(mesh):
    wide = Mesh(mesh.devices.reshape(NZ, NXH, NY, NXL, NC), AXES)
    league, rep = AXES[:3], AXES[3:]
    return jax.shard_map(
        per_device,
        mesh=wide,
        in_specs=(
            P(AXES, None),
            P(league, None, rep),
            P(league, None),
            P(league, rep),
            P(AXES, None),
            P(AXES),
        ),
        out_specs=(P(AXES), P(AXES)),
        check_vma=False,
    )
```

time: 147 us -> 112 us (0.76)
  blocking collectives: 43.6 us -> 0 us
  matrix products: 27 us -> 0 us
  Pallas kernels: 0 us -> 20.5 us
  waiting for transfers between devices: 8.3 us -> 25.8 us
  starting transfers between devices: 52.9 us -> 57 us
  other arithmetic: 5.73 us -> 2.66 us
  local copies, waits for them, and re-layouts: 6.89 us -> 4.15 us
    all_gather x1 -> x0, blocking collectives: 43.6 us -> none  [per_device(): head_all = lax.all_gather(heads[0], ('xl', 'c'), axis=0, tiled=False)]
    dot_general x18 -> x0, matrix products: 27 us -> none  [the longest x16 24.3 us: partial_values(): jnp.dot(scaled, weight, preferred_element_type=jnp.float32)]
    pallas_call x0 -> x7, Pallas kernels: none -> 20.5 us  [the longest x4 10.9 us: far_call(): pl.pallas_call(functools.partial(score_far, slotted), grid=(steps,), in_s...]
    ppermute x7 -> x6, waiting for transfers between devices: 0.02 us -> 15.9 us  [the longest x1 15.1 us: per_device(): second = lax.ppermute(pack(CHUNKS[0], sum(CHUNKS)), 'xl', SWAP)]
    all_to_all x1, starting transfers between devices: 20.6 us -> 15.7 us  [per_device(): lax.all_to_all(outgoing, exchange, 0, 0, axis_index_groups=groups, tiled=...]
    ppermute x7 -> x6, starting transfers between devices: 16.8 us -> 21.4 us  [the longest x1 6.89 us: per_device(): sib_w = lax.ppermute(near_w, 'c', SWAP)]
    all_to_all x1, starting transfers between devices: 15.6 us -> 19.8 us  [per_device(): lax.all_to_all(answers, exchange, 0, 0, axis_index_groups=groups, tiled=T...]
    another operation x1 -> x0, local copies, waits for them, and re-layouts: 2.05 us -> none  [per_device(): jnp.stack([jnp.dot(p, observations, preferred_element_type=jnp.float32).a...]
  transfers between devices with their start and end apart: 9 -> 8, of which waited for: 1 -> 3; matrix products, arithmetic and copies ran while one was open for 19% -> 1% of each run, Pallas kernels for 0% -> 15%
where the time goes in v2:
time: 112 us; the launch traced here: 111 us
  starting transfers between devices  57 us (51%)
  waiting for transfers between devices  25.8 us (23%)
  Pallas kernels  20.5 us (18%)
  local copies, waits for them, and re-layouts  4.15 us (4%)
  other arithmetic  2.66 us (2%)
    all_to_all x1, starting transfers between devices, per_device(): lax.all_to_all(answers, exchange, 0, 0, axis_index_groups=groups, tiled=T...  19.8 us
    all_to_all x1, starting transfers between devices, per_device(): lax.all_to_all(outgoing, exchange, 0, 0, axis_index_groups=groups, tiled=...  15.7 us
    ppermute x1, waiting for transfers between devices, per_device(): second = lax.ppermute(pack(CHUNKS[0], sum(CHUNKS)), 'xl', SWAP)  15.1 us
    pallas_call x4, Pallas kernels, far_call(): pl.pallas_call(functools.partial(score_far, slotted), grid=(steps,), in_s...  10.9 us
    all_to_all x1, waiting for transfers between devices, per_device(): lax.all_to_all(answers, exchange, 0, 0, axis_index_groups=groups, tiled=T...  9.84 us
    pallas_call x2, Pallas kernels, near_call(): pl.pallas_call(functools.partial(score_near, slotted), grid=(units // ste...  8 us
    ppermute x1, starting transfers between devices, per_device(): sib_w = lax.ppermute(near_w, 'c', SWAP)  6.89 us
    ppermute x1, starting transfers between devices, per_device(): first = lax.ppermute(pack(0, CHUNKS[0]), 'xl', SWAP)  3.94 us
  transfers between devices with their start and end apart: 8, of which 3 were waited for; matrix products, arithmetic and copies ran while one was open for 1% of the time, Pallas kernels for 15%

profile of v2, /device:TPU:1, one launch (start us, length us, event | category | flops | bytes accessed | tf_op | source)
XLA Modules:
  0.0 111.0 jit_solution(16639923965408550752)
XLA Ops:
  0.6 1.2 %slice_reduce_fusion.2 = (bf16[256]{0:T(256)(128)(2,1)S(1)}, bf16[256]{0:T(256)(128)(2,1)}) fusion(bf16[1,512]{1,0:T(2,128)(2,1)} %h0_ref.3), kind=kLoop, calls=%fused_computation.11 | loop fusion | bytes 2048 | tf_op jit(solution)/shard_map/slice | solution.py:168
  1.9 2.7 %fusion.3 = (bf16[2048,256]{1,0:T(8,128)(2,1)S(1)}, bf16[2048,256]{1,0:T(8,128)(2,1)}) fusion(bf16[2048,512]{1,0:T(8,128)(2,1)} %bitcast.8), kind=kLoop, calls=%fused_computation.15 | loop fusion | bytes 4194304 | tf_op jit(solution)/shard_map/slice | solution.py:169
  4.5 0.0 copy-start.5
  4.5 0.0 copy-start.9
  4.5 0.0 copy-start.10
  4.6 1.1 pad_maximum_fusion.1
  5.6 3.9 %collective-permute-start.3 = (bf16[2056,256]{1,0:T(8,128)(2,1)}, bf16[2056,256]{1,0:T(8,128)(2,1)}, u32[]{:S(2)}, u32[]{:S(2)}) collective-permute-start(bf16[2056,256]{1,0:T(8,128)(2,1)} %pad_maximum_fusion.1), channel_id=1, source_target_pairs={{0,2},{2,0},{1,3},{3,1},{4,6},{6,4},{5,7},{7,5},{8,10},{10,8},{9,1... | collective-permute-start | bytes 3158024 | tf_op jit(solution)/shard_map/ppermute | solution.py:171
  9.6 0.0 copy-done.5
  9.6 0.0 copy-done.9
  9.6 0.0 copy-done.10
  9.6 0.0 copy-start
  9.6 1.7 %fill_slots.1 = bf16[128,2,2048]{2,1,0:T(2,128)(2,1)} custom-call(s32[1,128]{1,0:T(1,128)S(1)} %bitcast.12, s32[1,128]{1,0:T(1,128)S(1)} %bitcast.15, bf16[128,2048]{1,0:T(8,128)(2,1)S(1)} %copy-done.5), custom_call_target="tpu_custom_call" | custom-call | flops 199999995904 | tf_op jit(solution)/shard_map/fill_slots/pallas_call | solution.py:60
  11.3 0.0 copy-done
  11.3 0.0 copy-start.12
  11.3 0.0 copy-start.11
  11.3 6.9 %collective-permute-start.1 = (bf16[2048,512]{1,0:T(8,128)(2,1)S(1)}, bf16[2048,512]{1,0:T(8,128)(2,1)}, u32[]{:S(2)}, u32[]{:S(2)}) collective-permute-start(bf16[2048,512]{1,0:T(8,128)(2,1)S(1)} %bitcast.9), channel_id=1, source_target_pairs={{0,1},{1,0},{2,3},{3,2},{4,5},{5,4},{6,7},{7,6},{8,9},{9,8},{10,11... | collective-permute-start | bytes 6291464 | tf_op jit(solution)/shard_map/ppermute | solution.py:175
  18.2 15.7 %all-to-all-start = ((bf16[128,2,2048]{2,1,0:T(2,128)(2,1)}), bf16[128,2,2048]{2,1,0:T(2,128)(2,1)}, u32[]{:S(2)}, u32[]{:S(2)}) async-start(bf16[128,2,2048]{2,1,0:T(2,128)(2,1)} %fill_slots.1), calls=%async_computation | async-start | bytes 2097152 | tf_op jit(solution)/shard_map/all_to_all | solution.py:183
  33.9 0.0 collective-permute-done.3.refs_0_.refs_1_
  33.9 2.2 %collective-permute-start.4 = (bf16[2056,256]{1,0:T(8,128)(2,1)}, bf16[2056,256]{1,0:T(8,128)(2,1)S(1)}, u32[]{:S(2)}, u32[]{:S(2)}) collective-permute-start(bf16[2056,256]{1,0:T(8,128)(2,1)} %collective-permute-done.3.refs_0_.refs_1_), channel_id=1, source_target_pairs={{0,1},{1,0},{2,3},{3,2},{4,5},{5,4},{6,7},{7,6},{8,9},{9,8},{10,11... | collective-permute-start | bytes 3158024 | tf_op jit(solution)/shard_map/ppermute | solution.py:177
  36.1 0.0 copy-done.12
  36.1 0.0 copy-done.11
  36.1 0.0 copy-start.8
  36.1 0.0 copy-start.6
  36.1 0.0 copy-start.7
  36.2 0.1 pad_maximum_fusion
  36.2 3.4 %collective-permute-start = (bf16[2056,256]{1,0:T(8,128)(2,1)S(1)}, bf16[2056,256]{1,0:T(8,128)(2,1)S(1)}, u32[]{:S(2)}, u32[]{:S(2)}) collective-permute-start(bf16[2056,256]{1,0:T(8,128)(2,1)S(1)} %pad_maximum_fusion), channel_id=1, source_target_pairs={{0,2},{2,0},{1,3},{3,1},{4,6},{6,4},{5,7},{7,5},{8,10},{10,8},{9,1... | collective-permute-start | bytes 3158024 | tf_op jit(solution)/shard_map/ppermute | solution.py:172
  39.6 0.0 copy-done.8
  39.6 2.2 %collective-permute-start.2 = (bf16[1,512]{1,0:T(2,128)(2,1)S(1)}, bf16[1,512]{1,0:T(2,128)(2,1)S(1)}, u32[]{:S(2)}, u32[]{:S(2)}) collective-permute-start(bf16[1,512]{1,0:T(2,128)(2,1)S(1)} %copy-done.8), channel_id=1, source_target_pairs={{0,1},{1,0},{2,3},{3,2},{4,5},{5,4},{6,7},{7,6},{8,9},{9,8},{10,11... | collective-permute-start | bytes 3080 | tf_op jit(solution)/shard_map/ppermute | solution.py:176
  41.8 0.8 collective-permute-done.2.h1_ref
  42.7 0.0 collective-permute-done.1.w1_ref
  42.7 0.0 copy-done.6
  42.7 0.0 copy-done.7
  42.7 2.7 %score_near.2 = (bf16[128,2048]{1,0:T(8,128)(2,1)S(1)}, f32[128,1]{1,0:T(8,128)S(1)}) custom-call(bf16[128,2048]{1,0:T(8,128)(2,1)S(1)} %copy-done.6, f32[1,2048]{1,0:T(1,128)S(1)} %copy-done.7, bf16[2048,512]{1,0:T(8,128)(2,1)S(1)} %bitcast.10, bf16[1,512]{1,0:T(2,128)(2,1)S(1)} %copy-done.8, bf16[2048,512]{1,0:T(8,128)(2,1)} %collective-permute-done.1.w1_ref, ...), custom_call_target="tpu_custom_call" | custom-call | tf_op jit(solution)/shard_map/score_near/pallas_call | solution.py:102
  45.4 0.0 copy-start.3
  45.4 0.0 collective-permute-done.4.refs_2_.refs_3_
  45.4 0.0 copy-start.1
  45.4 2.5 %score_far.4.near_ref = f32[128,1]{1,0:T(8,128)S(1)} custom-call(bf16[128,2048]{1,0:T(8,128)(2,1)S(1)} %get-tuple-element.16.scaled_ref, f32[128,1]{1,0:T(8,128)S(1)} %get-tuple-element.15.near_ref, bf16[2056,256]{1,0:T(8,128)(2,1)} %collective-permute-done.3.refs_0_.refs_1_, bf16[2056,256]{1,0:T(8,128)(2,1)} %collective-permute-done.3.refs_0_.refs_1_, ...), custom_call_target="tpu_custom_call" | custom-call | tf_op jit(solution)/shard_map/score_far/pallas_call | solution.py:147
  47.9 0.0 copy-done.3
  47.9 0.0 copy-done.1
  47.9 15.1 %collective-permute-done.refs_0_.refs_1_ = bf16[2056,256]{1,0:T(8,128)(2,1)S(1)} collective-permute-done((bf16[2056,256]{1,0:T(8,128)(2,1)S(1)}, bf16[2056,256]{1,0:T(8,128)(2,1)S(1)}, u32[]{:S(2)}, u32[]{:S(2)}) %collective-permute-start) | collective-permute-done | bytes 1052704 | tf_op jit(solution)/shard_map/ppermute | solution.py:172
  63.0 2.8 %collective-permute-start.5 = (bf16[2056,256]{1,0:T(8,128)(2,1)S(1)}, bf16[2056,256]{1,0:T(8,128)(2,1)}, u32[]{:S(2)}, u32[]{:S(2)}) collective-permute-start(bf16[2056,256]{1,0:T(8,128)(2,1)S(1)} %collective-permute-done.refs_0_.refs_1_), channel_id=1, source_target_pairs={{0,1},{1,0},{2,3},{3,2},{4,5},{5,4},{6,7},{7,6},{8,9},{9,8},{10,11... | collective-permute-start | bytes 3158024 | tf_op jit(solution)/shard_map/ppermute | solution.py:181
  65.8 0.2 convert_reduce_fusion
  66.0 0.0 all-to-all-done.x_ref
  66.0 0.0 copy-start.2
  66.0 5.3 %score_near.3 = (bf16[256,2048]{1,0:T(8,128)(2,1)S(1)}, f32[256,1]{1,0:T(8,128)S(1)}) custom-call(bf16[128,2,2048]{2,1,0:T(2,128)(2,1)} %all-to-all-done.x_ref, f32[1,2048]{1,0:T(1,128)S(1)} %copy-done.7, bf16[2048,512]{1,0:T(8,128)(2,1)S(1)} %bitcast.11, bf16[1,512]{1,0:T(2,128)(2,1)S(1)} %copy-done.8, bf16[2048,512]{1,0:T(8,128)(2,1)} %collective-permute-done.1.w1_ref, ...), custom_call_target="tpu_custom_call" | custom-call | tf_op jit(solution)/shard_map/score_near/pallas_call | solution.py:102
  71.4 0.0 copy-done.2
  71.4 2.7 %score_far.6.near_ref = f32[256,1]{1,0:T(8,128)S(1)} custom-call(bf16[256,2048]{1,0:T(8,128)(2,1)S(1)} %get-tuple-element.20.scaled_ref, f32[256,1]{1,0:T(8,128)S(1)} %get-tuple-element.21.near_ref, bf16[2056,256]{1,0:T(8,128)(2,1)} %collective-permute-done.3.refs_0_.refs_1_, bf16[2056,256]{1,0:T(8,128)(2,1)} %collective-permute-done.3.refs_0_.refs_1_, ...), custom_call_target="tpu_custom_call" | custom-call | flops 5000000000 | tf_op jit(solution)/shard_map/score_far/pallas_call | solution.py:147
  74.1 0.0 copy-start.4
  74.1 0.0 collective-permute-done.5.refs_2_.refs_3_
  74.1 3.5 %score_far.7 = f32[128,2]{1,0:T(8,128)} custom-call(bf16[256,2048]{1,0:T(8,128)(2,1)S(1)} %get-tuple-element.20.scaled_ref, f32[256,1]{1,0:T(8,128)S(1)} %score_far.6.near_ref, bf16[2056,256]{1,0:T(8,128)(2,1)S(1)} %collective-permute-done.refs_0_.refs_1_, bf16[2056,256]{1,0:T(8,128)(2,1)S(1)} %collective-permute-done.refs_0_.refs_1_, ...), custom_call_target="tpu_custom_call" | custom-call | tf_op jit(solution)/shard_map/score_far/pallas_call | solution.py:147
  77.6 19.8 %all-to-all-start.1 = ((f32[128,1,2]{2,1,0:T(1,128)}), f32[128,1,2]{2,1,0:T(1,128)S(1)}, u32[]{:S(2)}, u32[]{:S(2)}) async-start(f32[128,1,2]{2,1,0:T(1,128)} %bitcast.5), calls=%async_computation.1 | async-start | bytes 131072 | tf_op jit(solution)/shard_map/all_to_all | solution.py:187
  97.4 0.0 copy-done.4
  97.4 2.2 %score_far.5 = f32[128,1]{1,0:T(8,128)S(1)} custom-call(bf16[128,2048]{1,0:T(8,128)(2,1)S(1)} %copy-done.4, f32[128,1]{1,0:T(8,128)S(1)} %score_far.4.near_ref, bf16[2056,256]{1,0:T(8,128)(2,1)S(1)} %collective-permute-done.refs_0_.refs_1_, bf16[2056,256]{1,0:T(8,128)(2,1)S(1)} %collective-permute-done.refs_0_.refs_1_, ...), custom_call_target="tpu_custom_call" | custom-call | tf_op jit(solution)/shard_map/score_far/pallas_call | solution.py:147
  99.7 0.6 reduce.2
  100.3 9.8 %all-to-all-done.1 = f32[128,1,2]{2,1,0:T(1,128)S(1)} async-done(((f32[128,1,2]{2,1,0:T(1,128)}), f32[128,1,2]{2,1,0:T(1,128)S(1)}, u32[]{:S(2)}, u32[]{:S(2)}) %all-to-all-start.1) | async-done | bytes 1056 | tf_op jit(solution)/shard_map/all_to_all | solution.py:187
  110.1 0.2 slice_reduce_fusion.1
  110.3 0.7 select_reduce_fusion
  (4 shorter events, 0.0 us)
Async XLA Ops:
  4.5 5.0 %copy-start.5 = (bf16[128,2048]{1,0:T(8,128)(2,1)S(1)}, bf16[128,2048]{1,0:T(8,128)(2,1)}, u32[]{:S(2)}) copy-start(bf16[128,2048]{1,0:T(8,128)(2,1)} %x_ref.1) | copy-start | bytes 1572868
  4.5 5.0 %copy-start.9 = (s32[128,1]{0,1:T(1,128)S(1)}, s32[128,1]{0,1:T(1,128)}, u32[]{:S(2)}) copy-start(s32[128,1]{0,1:T(1,128)} %param.10) | copy-start | bytes 1540
  4.5 5.0 %copy-start.10 = (s32[128]{0:T(128)S(1)}, s32[128]{0:T(128)}, u32[]{:S(2)}) copy-start(s32[128]{0:T(128)} %param.11) | copy-start | bytes 1540
  5.6 28.3 %collective-permute-start.3 = (bf16[2056,256]{1,0:T(8,128)(2,1)}, bf16[2056,256]{1,0:T(8,128)(2,1)}, u32[]{:S(2)}, u32[]{:S(2)}) collective-permute-start(bf16[2056,256]{1,0:T(8,128)(2,1)} %pad_maximum_fusion.1), channel_id=1, source_target_pairs={{0,2},{2,0},{1,3},{3,1},{4,6},{6,4},{5,7},{7,5},{8,10},{10,8},{9,1... | collective-permute-start | bytes 3158024 | tf_op jit(solution)/shard_map/ppermute | solution.py:171
  9.6 1.7 %copy-start = (bf16[1,2048,512]{2,1,0:T(8,128)(2,1)S(1)}, bf16[1,2048,512]{2,1,0:T(8,128)(2,1)}, u32[]{:S(2)}) copy-start(bf16[1,2048,512]{2,1,0:T(8,128)(2,1)} %param.7) | copy-start | bytes 6291460
  11.3 24.8 %copy-start.12 = (bf16[256]{0:T(256)(128)(2,1)S(1)}, bf16[256]{0:T(256)(128)(2,1)}, u32[]{:S(2)}) copy-start(bf16[256]{0:T(256)(128)(2,1)} %get-tuple-element.25) | copy-start | bytes 1540
  11.3 24.8 %copy-start.11 = (bf16[2048,256]{1,0:T(8,128)(2,1)S(1)}, bf16[2048,256]{1,0:T(8,128)(2,1)}, u32[]{:S(2)}) copy-start(bf16[2048,256]{1,0:T(8,128)(2,1)} %get-tuple-element.27) | copy-start | bytes 3145732
  11.3 31.4 %collective-permute-start.1 = (bf16[2048,512]{1,0:T(8,128)(2,1)S(1)}, bf16[2048,512]{1,0:T(8,128)(2,1)}, u32[]{:S(2)}, u32[]{:S(2)}) collective-permute-start(bf16[2048,512]{1,0:T(8,128)(2,1)S(1)} %bitcast.9), channel_id=1, source_target_pairs={{0,1},{1,0},{2,3},{3,2},{4,5},{5,4},{6,7},{7,6},{8,9},{9,8},{10,11... | collective-permute-start | bytes 6291464 | tf_op jit(solution)/shard_map/ppermute | solution.py:175
  18.2 47.9 %all-to-all-start = ((bf16[128,2,2048]{2,1,0:T(2,128)(2,1)}), bf16[128,2,2048]{2,1,0:T(2,128)(2,1)}, u32[]{:S(2)}, u32[]{:S(2)}) async-start(bf16[128,2,2048]{2,1,0:T(2,128)(2,1)} %fill_slots.1), calls=%async_computation | async-start | bytes 2097152 | tf_op jit(solution)/shard_map/all_to_all | solution.py:183
  33.9 11.5 %collective-permute-start.4 = (bf16[2056,256]{1,0:T(8,128)(2,1)}, bf16[2056,256]{1,0:T(8,128)(2,1)S(1)}, u32[]{:S(2)}, u32[]{:S(2)}) collective-permute-start(bf16[2056,256]{1,0:T(8,128)(2,1)} %collective-permute-done.3.refs_0_.refs_1_), channel_id=1, source_target_pairs={{0,1},{1,0},{2,3},{3,2},{4,5},{5,4},{6,7},{7,6},{8,9},{9,8},{10,11... | collective-permute-start | bytes 3158024 | tf_op jit(solution)/shard_map/ppermute | solution.py:177
  36.1 3.5 %copy-start.8 = (bf16[1,512]{1,0:T(2,128)(2,1)S(1)}, bf16[1,512]{1,0:T(2,128)(2,1)}, u32[]{:S(2)}) copy-start(bf16[1,512]{1,0:T(2,128)(2,1)} %h0_ref.3) | copy-start | bytes 3076
  36.1 6.5 %copy-start.6 = (bf16[128,2048]{1,0:T(8,128)(2,1)S(1)}, bf16[128,2048]{1,0:T(8,128)(2,1)}, u32[]{:S(2)}) copy-start(bf16[128,2048]{1,0:T(8,128)(2,1)} %x_ref.1) | copy-start | bytes 1572868
  36.1 6.5 %copy-start.7 = (f32[1,2048]{1,0:T(1,128)S(1)}, f32[1,2048]{1,0:T(1,128)}, u32[]{:S(2)}) copy-start(f32[1,2048]{1,0:T(1,128)} %gain_ref.3) | copy-start | bytes 24580
  36.2 26.8 %collective-permute-start = (bf16[2056,256]{1,0:T(8,128)(2,1)S(1)}, bf16[2056,256]{1,0:T(8,128)(2,1)S(1)}, u32[]{:S(2)}, u32[]{:S(2)}) collective-permute-start(bf16[2056,256]{1,0:T(8,128)(2,1)S(1)} %pad_maximum_fusion), channel_id=1, source_target_pairs={{0,2},{2,0},{1,3},{3,1},{4,6},{6,4},{5,7},{7,5},{8,10},{10,8},{9,1... | collective-permute-start | bytes 3158024 | tf_op jit(solution)/shard_map/ppermute | solution.py:172
  39.6 3.1 %collective-permute-start.2 = (bf16[1,512]{1,0:T(2,128)(2,1)S(1)}, bf16[1,512]{1,0:T(2,128)(2,1)S(1)}, u32[]{:S(2)}, u32[]{:S(2)}) collective-permute-start(bf16[1,512]{1,0:T(2,128)(2,1)S(1)} %copy-done.8), channel_id=1, source_target_pairs={{0,1},{1,0},{2,3},{3,2},{4,5},{5,4},{6,7},{7,6},{8,9},{9,8},{10,11... | collective-permute-start | bytes 3080 | tf_op jit(solution)/shard_map/ppermute | solution.py:176
  45.4 2.6 %copy-start.3 = (bf16[128,2048]{1,0:T(8,128)(2,1)}, bf16[128,2048]{1,0:T(8,128)(2,1)S(1)}, u32[]{:S(2)}) copy-start(bf16[128,2048]{1,0:T(8,128)(2,1)S(1)} %get-tuple-element.16.scaled_ref) | copy-start | bytes 1572868
  45.4 2.6 %copy-start.1 = (bf16[2056,256]{1,0:T(8,128)(2,1)}, bf16[2056,256]{1,0:T(8,128)(2,1)S(1)}, u32[]{:S(2)}) copy-start(bf16[2056,256]{1,0:T(8,128)(2,1)S(1)} %collective-permute-done.4.refs_2_.refs_3_) | copy-start | bytes 3158020
  63.0 11.1 %collective-permute-start.5 = (bf16[2056,256]{1,0:T(8,128)(2,1)S(1)}, bf16[2056,256]{1,0:T(8,128)(2,1)}, u32[]{:S(2)}, u32[]{:S(2)}) collective-permute-start(bf16[2056,256]{1,0:T(8,128)(2,1)S(1)} %collective-permute-done.refs_0_.refs_1_), channel_id=1, source_target_pairs={{0,1},{1,0},{2,3},{3,2},{4,5},{5,4},{6,7},{7,6},{8,9},{9,8},{10,11... | collective-permute-start | bytes 3158024 | tf_op jit(solution)/shard_map/ppermute | solution.py:181
  66.0 5.4 %copy-start.2 = (bf16[2056,256]{1,0:T(8,128)(2,1)S(1)}, bf16[2056,256]{1,0:T(8,128)(2,1)}, u32[]{:S(2)}) copy-start(bf16[2056,256]{1,0:T(8,128)(2,1)} %copy-done.1) | copy-start | bytes 3158020
  74.1 23.4 %copy-start.4 = (bf16[128,2048]{1,0:T(8,128)(2,1)S(1)}, bf16[128,2048]{1,0:T(8,128)(2,1)}, u32[]{:S(2)}) copy-start(bf16[128,2048]{1,0:T(8,128)(2,1)} %copy-done.3) | copy-start | bytes 1572868
  77.6 32.6 %all-to-all-start.1 = ((f32[128,1,2]{2,1,0:T(1,128)}), f32[128,1,2]{2,1,0:T(1,128)S(1)}, u32[]{:S(2)}, u32[]{:S(2)}) async-start(f32[128,1,2]{2,1,0:T(1,128)} %bitcast.5), calls=%async_computation.1 | async-start | bytes 131072 | tf_op jit(solution)/shard_map/all_to_all | solution.py:187

commit v3 on v1

v3 whole, which is shorter than its diff:
```python
import functools

import jax
import jax.numpy as jnp
from jax import lax
from jax.experimental import pallas as pl
from jax.experimental.pallas import tpu as pltpu
from jax.sharding import Mesh, PartitionSpec as P

NZ, NXH, NY, NXL, NC = 8, 2, 8, 2, 2
AXES = ("z", "xh", "y", "xl", "c")
SWAP = [(0, 1), (1, 0)]
COST_FIRST = 5
VMEM_LIMIT = 40 * 1024 * 1024


def exchange_groups():
    groups = []
    for flip in range(2):
        group = []
        for z in range(NZ):
            for xh in range(NXH):
                for y in range(NY):
                    group.append(((z * NXH + xh) * NY + y) * NXL + (xh ^ flip))
        groups.append(group)
    return groups


def hint(weight):
    return pl.CostEstimate(flops=weight * 1_000_000_000, bytes_accessed=0, transcendentals=0)


def whole(shape):
    return pl.BlockSpec(shape, lambda *_: (0,) * len(shape))


def fill_slots(owner_ref, valid_ref, rows_ref, out_ref, slot_ref):
    count = owner_ref.shape[1]
    agents = out_ref.shape[0]
    owner = owner_ref[...]
    live = valid_ref[...]
    owner_down = jnp.broadcast_to(owner, (count, count)).T
    live_down = jnp.broadcast_to(live, (count, count)).T
    down = lax.broadcasted_iota(jnp.int32, (count, count), 0)
    across = lax.broadcasted_iota(jnp.int32, (count, count), 1)
    earlier = (owner_down == owner) & (live_down == 1) & (down < across)
    slot = jnp.sum(earlier.astype(jnp.int32), axis=0, keepdims=True)
    agent = lax.broadcasted_iota(jnp.int32, (agents, count), 0)
    named = (agent == owner) & (live == 1)
    slot_ref[...] = jnp.where(live == 1, slot, 2)
    rows = rows_ref[...]
    for k in range(2):
        pick = (named & (slot == k)).astype(jnp.float32).astype(jnp.bfloat16)
        out_ref[:, k, :] = jnp.dot(pick, rows, preferred_element_type=jnp.float32).astype(jnp.bfloat16)


def slots_call(owner, valid, rows, agents):
    count, width = rows.shape
    return pl.pallas_call(
        fill_slots,
        out_shape=[
            pltpu.HBM((agents, 2, width), jnp.bfloat16),
            jax.ShapeDtypeStruct((1, count), jnp.int32),
        ],
        compiler_params=pltpu.CompilerParams(vmem_limit_bytes=VMEM_LIMIT),
        cost_estimate=hint(200),
        name="fill_slots",
    )(owner, valid, rows)


def pick_answers(returned_ref, owner_ref, slot_ref, out_ref):
    agents, count = returned_ref.shape[0], owner_ref.shape[1]
    slot = slot_ref[...]
    answer = jnp.where(slot == 0, returned_ref[:, 0:1], returned_ref[:, 1:2])
    agent = lax.broadcasted_iota(jnp.int32, (agents, count), 0)
    named = (agent == owner_ref[...]) & (slot < 2)
    out_ref[...] = jnp.sum(jnp.where(named, answer, 0.0), axis=0, keepdims=True)


def pick_call(returned, owner, slot):
    return pl.pallas_call(
        pick_answers,
        out_shape=jax.ShapeDtypeStruct(owner.shape, jnp.float32),
        cost_estimate=hint(0),
        name="pick_answers",
    )(returned, owner, slot)


def scaled_rows(rows, gain):
    wide = rows.astype(jnp.float32)
    squares = jnp.mean(wide * wide, axis=1, keepdims=True)
    return (wide * lax.rsqrt(squares + 1e-06) * gain).astype(jnp.bfloat16)


def partial_values(scaled, weight, head):
    hidden = jnp.dot(scaled, weight, preferred_element_type=jnp.float32)
    half = 0.5 * hidden
    return jnp.sum((half + half * jnp.tanh(half)) * head.astype(jnp.float32), axis=1, keepdims=True)


def score_own(x_ref, gain_ref, w_ref, h_ref, scaled_ref, value_ref):
    @pl.when(pl.program_id(0) == 0)
    def _():
        scaled_ref[...] = scaled_rows(x_ref[...], gain_ref[...])
        value_ref[...] = jnp.zeros_like(value_ref)

    value_ref[...] += partial_values(scaled_ref[...], w_ref[...], h_ref[...])


def score_first(x_ref, gain_ref, own_ref, own_near_ref, w0_ref, h0_ref, w1_ref, h1_ref, scaled_ref, visit_out, own_out):
    @pl.when(pl.program_id(0) == 0)
    def _():
        gain = gain_ref[...]
        count = x_ref.shape[0]
        for k in range(2):
            scaled_ref[k * count : (k + 1) * count, :] = scaled_rows(x_ref[:, k, :], gain)
        visit_out[...] = jnp.zeros_like(visit_out)
        own_out[...] = own_near_ref[...]

    scaled = scaled_ref[...]
    visit_out[...] += partial_values(scaled, w0_ref[...], h0_ref[...]) + partial_values(scaled, w1_ref[...], h1_ref[0:1])
    own_out[...] += partial_values(own_ref[...], w1_ref[...], h1_ref[0:1])


def score_last(
    visit_ref, own_ref, visit_near_ref, own_near_ref, w0_ref, h0_ref, w1_ref, h1_ref, answer_out, value_out, visit_total, own_total
):
    @pl.when(pl.program_id(0) == 0)
    def _():
        visit_total[...] = visit_near_ref[...]
        own_total[...] = own_near_ref[...]

    for rows_ref, total in ((visit_ref, visit_total), (own_ref, own_total)):
        rows = rows_ref[...]
        total[...] += partial_values(rows, w0_ref[...], h0_ref[...]) + partial_values(rows, w1_ref[...], h1_ref[1:2])

    @pl.when(pl.program_id(0) == pl.num_programs(0) - 1)
    def _():
        half = answer_out.shape[0]
        answer_out[:, 0:1] = visit_total[:half]
        answer_out[:, 1:2] = visit_total[half:]
        value_out[...] = jnp.broadcast_to(own_total[...], (half, half)).T[0:1]


def score_call(body, fixed, weights, heads, outs, scratch, weight, step=256):
    width, units = weights[0].shape
    specs, args = [whole(x.shape) for x in fixed], list(fixed)
    for w, h in zip(weights, heads):
        specs += [pl.BlockSpec((width, step), lambda j: (0, j)), pl.BlockSpec((h.shape[0], step), lambda j: (0, j))]
        args += [w, h]
    return pl.pallas_call(
        body,
        grid=(units // step,),
        in_specs=specs,
        out_specs=[whole(shape) for shape, _ in outs],
        out_shape=[jax.ShapeDtypeStruct(*out) for out in outs],
        scratch_shapes=[pltpu.VMEM(shape, jnp.float32) for shape in scratch],
        compiler_params=pltpu.CompilerParams(vmem_limit_bytes=VMEM_LIMIT),
        cost_estimate=hint(weight),
        name=body.__name__,
    )(*args)


def per_device(observations, weights, gains, heads, pairing, valid):
    rows_dev, width = observations.shape
    n_agents = NZ * NXH * NY
    groups = exchange_groups()
    own_w = weights[0]
    exchange = ("z", "xh", "y", "xl")

    far_w = lax.ppermute(own_w, "xl", SWAP)
    owner = pairing.reshape(1, rows_dev)
    outgoing, slot = slots_call(owner, valid.reshape(1, rows_dev), observations, n_agents)
    near_h, slot = lax.optimization_barrier((heads, slot))
    received = lax.all_to_all(outgoing, exchange, 0, 0, axis_index_groups=groups, tiled=True)
    sib_h = lax.ppermute(near_h, "c", SWAP)
    near_w, sib_h = lax.optimization_barrier((own_w, sib_h))
    sib_w = lax.ppermute(near_w, "c", SWAP)
    far_h = lax.ppermute(jnp.concatenate([heads, sib_h], axis=0), "xl", SWAP)
    f32, bf16 = jnp.float32, jnp.bfloat16
    visits = 2 * n_agents
    own_scaled, own = score_call(
        score_own, (observations, gains), (own_w,), (heads,), [((rows_dev, width), bf16), ((rows_dev, 1), f32)], [], 0
    )
    received, far_w, far_h, own_scaled, own = lax.optimization_barrier((received, far_w, far_h, own_scaled, own))
    far_sib_w = lax.ppermute(far_w, "c", SWAP)
    visit_scaled, visit, own = score_call(
        score_first,
        (received, gains, own_scaled, own),
        (own_w, far_w),
        (heads, far_h),
        [((visits, width), bf16), ((visits, 1), f32), ((rows_dev, 1), f32)],
        [],
        COST_FIRST,
    )
    answers, own_value = score_call(
        score_last,
        (visit_scaled, own_scaled, visit, own),
        (sib_w, far_sib_w),
        (sib_h, far_h),
        [((n_agents, 2), f32), ((1, rows_dev), f32)],
        [(visits, 1), (rows_dev, 1)],
        0,
    )
    returned = lax.all_to_all(answers, exchange, 0, 0, axis_index_groups=groups, tiled=True)

    opponent_value = pick_call(returned, owner, slot)
    return own_value.reshape(rows_dev), opponent_value.reshape(rows_dev)


def solution(mesh):
    wide = Mesh(mesh.devices.reshape(NZ, NXH, NY, NXL, NC), AXES)
    league, rep = AXES[:3], AXES[3:]
    return jax.shard_map(
        per_device,
        mesh=wide,
        in_specs=(
            P(AXES, None),
            P(league, None, rep),
            P(league, None),
            P(league, rep),
            P(AXES, None),
            P(AXES),
        ),
        out_specs=(P(AXES), P(AXES)),
        check_vma=False,
    )
```

time: 147 us -> 98.9 us (0.67)
  matrix products: 27 us -> 0 us
  blocking collectives: 43.6 us -> 23 us
  starting transfers between devices: 52.9 us -> 35.9 us
  Pallas kernels: 0 us -> 13.9 us
  waiting for transfers between devices: 8.3 us -> 17.5 us
  other arithmetic: 5.73 us -> 0.69 us
    all_gather x1 -> x0, blocking collectives: 43.6 us -> none  [per_device(): head_all = lax.all_gather(heads[0], ('xl', 'c'), axis=0, tiled=False)]
    dot_general x18 -> x0, matrix products: 27 us -> none  [the longest x16 24.3 us: partial_values(): jnp.dot(scaled, weight, preferred_element_type=jnp.float32)]
    all_to_all x0 -> x1, blocking collectives: none -> 23 us  [per_device(): lax.all_to_all(answers, exchange, 0, 0, axis_index_groups=groups, tiled=T...]
    all_to_all x1 -> x0, starting transfers between devices: 15.6 us -> none  [per_device(): lax.all_to_all(answers.reshape(n_agents, 2), exchange, 0, 0, axis_index_g...]
    pallas_call x0 -> x5, Pallas kernels: none -> 13.9 us  [the longest x3 10.7 us: score_call(): pl.pallas_call(body, grid=(units // step,), in_specs=specs, out_specs=[wh...]
    all_to_all x1, waiting for transfers between devices: 0.01 us -> 12.9 us  [per_device(): lax.all_to_all(outgoing, exchange, 0, 0, axis_index_groups=groups, tiled=...]
    all_to_all x1 -> x0, waiting for transfers between devices: 8.27 us -> none  [per_device(): lax.all_to_all(answers.reshape(n_agents, 2), exchange, 0, 0, axis_index_g...]
    unnamed x24, local copies, waits for them, and re-layouts: 0.83 us -> 6.42 us
  transfers between devices with their start and end apart: 9 -> 6, of which waited for: 1 -> 3; matrix products, arithmetic and copies ran while one was open for 19% -> 1% of each run, Pallas kernels for 0% -> 8%
where the time goes in v3:
time: 98.9 us; the launch traced here: 98.2 us
  starting transfers between devices  35.9 us (36%)
  blocking collectives  23 us (23%)
  waiting for transfers between devices  17.5 us (18%)
  Pallas kernels  13.9 us (14%)
  local copies, waits for them, and re-layouts  6.42 us (6%)
    all_to_all x1, blocking collectives, per_device(): lax.all_to_all(answers, exchange, 0, 0, axis_index_groups=groups, tiled=T...  23 us
    all_to_all x1, starting transfers between devices, per_device(): lax.all_to_all(outgoing, exchange, 0, 0, axis_index_groups=groups, tiled=...  19.2 us
    all_to_all x1, waiting for transfers between devices, per_device(): lax.all_to_all(outgoing, exchange, 0, 0, axis_index_groups=groups, tiled=...  12.9 us
    pallas_call x3, Pallas kernels, score_call(): pl.pallas_call(body, grid=(units // step,), in_specs=specs, out_specs=[wh...  10.7 us
    unnamed x24, local copies, waits for them, and re-layouts  6.42 us
    ppermute x1, starting transfers between devices, per_device(): far_sib_w = lax.ppermute(far_w, 'c', SWAP)  4.92 us
    ppermute x1, starting transfers between devices, per_device(): far_w = lax.ppermute(own_w, 'xl', SWAP)  3.95 us
    ppermute x1, waiting for transfers between devices, per_device(): far_h = lax.ppermute(jnp.concatenate([heads, sib_h], axis=0), 'xl', SWAP)  3.55 us
  transfers between devices with their start and end apart: 6, of which 3 were waited for; matrix products, arithmetic and copies ran while one was open for 1% of the time, Pallas kernels for 8%

profile of v3, /device:TPU:1, one launch (start us, length us, event | category | flops | bytes accessed | tf_op | source)
XLA Modules:
  0.0 98.2 jit_solution(7501350776013867597)
XLA Ops:
  0.6 4.0 %collective-permute-start = (bf16[2048,512]{1,0:T(8,128)(2,1)}, bf16[2048,512]{1,0:T(8,128)(2,1)}, u32[]{:S(2)}, u32[]{:S(2)}) collective-permute-start(bf16[2048,512]{1,0:T(8,128)(2,1)} %bitcast.9), channel_id=1, source_target_pairs={{0,2},{2,0},{1,3},{3,1},{4,6},{6,4},{5,7},{7,5},{8,10},{10,8},{9,1... | collective-permute-start | bytes 6291464 | tf_op jit(solution)/shard_map/ppermute | solution.py:171
  4.6 0.0 copy-start.4
  4.6 1.0 %copy-done.4 = bf16[128,2048]{1,0:T(8,128)(2,1)S(1)} copy-done((bf16[128,2048]{1,0:T(8,128)(2,1)S(1)}, bf16[128,2048]{1,0:T(8,128)(2,1)}, u32[]{:S(2)}) %copy-start.4) | copy-done | bytes 524312
  5.6 0.0 copy-start.9
  5.6 0.7 copy-done.9
  6.3 0.0 copy-start.11
  6.3 0.7 copy-done.11
  6.9 1.7 %fill_slots.1 = (bf16[128,2,2048]{2,1,0:T(2,128)(2,1)}, s32[1,128]{1,0:T(1,128)S(1)}) custom-call(s32[1,128]{1,0:T(1,128)S(1)} %bitcast.15, s32[1,128]{1,0:T(1,128)S(1)} %bitcast.16, bf16[128,2048]{1,0:T(8,128)(2,1)S(1)} %copy-done.4), custom_call_target="tpu_custom_call" | custom-call | flops 199999995904 | tf_op jit(solution)/shard_map/fill_slots/pallas_call | solution.py:59
  8.6 0.0 copy-start.10
  8.6 0.5 copy-done.10
  9.1 0.0 copy-start
  9.1 0.0 copy-start.6
  9.1 19.2 %all-to-all-start = ((bf16[128,2,2048]{2,1,0:T(2,128)(2,1)}), bf16[128,2,2048]{2,1,0:T(2,128)(2,1)S(1)}, u32[]{:S(2)}, u32[]{:S(2)}) async-start(bf16[128,2,2048]{2,1,0:T(2,128)(2,1)} %get-tuple-element.20), calls=%async_computation | async-start | bytes 2097152 | tf_op jit(solution)/shard_map/all_to_all | solution.py:175
  28.3 3.1 %collective-permute-start.1 = (bf16[1,512]{1,0:T(2,128)(2,1)}, bf16[1,512]{1,0:T(2,128)(2,1)S(1)}, u32[]{:S(2)}, u32[]{:S(2)}) collective-permute-start(bf16[1,512]{1,0:T(2,128)(2,1)} %h0_ref.1), channel_id=1, source_target_pairs={{0,1},{1,0},{2,3},{3,2},{4,5},{5,4},{6,7},{7,6},{8,9},{9,8},{10,11... | collective-permute-start | bytes 3080 | tf_op jit(solution)/shard_map/ppermute | solution.py:176
  31.5 1.0 %collective-permute-done.1.h0_ref = bf16[1,512]{1,0:T(2,128)(2,1)S(1)} collective-permute-done((bf16[1,512]{1,0:T(2,128)(2,1)}, bf16[1,512]{1,0:T(2,128)(2,1)S(1)}, u32[]{:S(2)}, u32[]{:S(2)}) %collective-permute-start.1) | collective-permute-done | bytes 1056 | tf_op jit(solution)/shard_map/ppermute | solution.py:176
  32.5 0.7 pad_maximum_fusion
  33.2 2.2 %collective-permute-start.2 = (bf16[2,512]{1,0:T(2,128)(2,1)S(1)}, bf16[2,512]{1,0:T(2,128)(2,1)S(1)}, u32[]{:S(2)}, u32[]{:S(2)}) collective-permute-start(bf16[2,512]{1,0:T(2,128)(2,1)S(1)} %pad_maximum_fusion), channel_id=1, source_target_pairs={{0,2},{2,0},{1,3},{3,1},{4,6},{6,4},{5,7},{7,5},{8,10},{10,8},{9,1... | collective-permute-start | bytes 6152 | tf_op jit(solution)/shard_map/ppermute | solution.py:179
  35.4 0.0 copy-done
  35.4 0.0 copy-done.6
  35.4 0.0 copy-start.5
  35.4 1.0 %copy-done.5 = bf16[128,2048]{1,0:T(8,128)(2,1)S(1)} copy-done((bf16[128,2048]{1,0:T(8,128)(2,1)S(1)}, bf16[128,2048]{1,0:T(8,128)(2,1)}, u32[]{:S(2)}) %copy-start.5) | copy-done | bytes 524312
  36.5 0.0 copy-start.7
  36.5 0.7 copy-done.7
  37.1 0.0 copy-start.8
  37.1 1.2 %score_own.1 = (bf16[128,2048]{1,0:T(8,128)(2,1)S(1)}, f32[128,1]{1,0:T(8,128)S(1)}) custom-call(bf16[128,2048]{1,0:T(8,128)(2,1)S(1)} %copy-done.5, f32[1,2048]{1,0:T(1,128)S(1)} %copy-done.6, bf16[2048,512]{1,0:T(8,128)(2,1)S(1)} %bitcast.10, bf16[1,512]{1,0:T(2,128)(2,1)S(1)} %copy-done.7), custom_call_target="tpu_custom_call" | custom-call | tf_op jit(solution)/shard_map/score_own/pallas_call | solution.py:151
  38.4 0.0 copy-start.1
  38.4 0.8 copy-done.1
  39.2 2.5 %collective-permute-start.3 = (bf16[2048,512]{1,0:T(8,128)(2,1)S(1)}, bf16[2048,512]{1,0:T(8,128)(2,1)}, u32[]{:S(2)}, u32[]{:S(2)}) collective-permute-start(bf16[2048,512]{1,0:T(8,128)(2,1)S(1)} %bitcast.11), channel_id=1, source_target_pairs={{0,1},{1,0},{2,3},{3,2},{4,5},{5,4},{6,7},{7,6},{8,9},{9,8},{10,11... | collective-permute-start | bytes 6291464 | tf_op jit(solution)/shard_map/ppermute | solution.py:178
  41.7 3.6 %collective-permute-done.2.h1_ref = bf16[2,512]{1,0:T(2,128)(2,1)S(1)} collective-permute-done((bf16[2,512]{1,0:T(2,128)(2,1)S(1)}, bf16[2,512]{1,0:T(2,128)(2,1)S(1)}, u32[]{:S(2)}, u32[]{:S(2)}) %collective-permute-start.2) | collective-permute-done | bytes 2080 | tf_op jit(solution)/shard_map/ppermute | solution.py:179
  45.2 12.9 %all-to-all-done.x_ref = bf16[128,2,2048]{2,1,0:T(2,128)(2,1)S(1)} async-done(((bf16[128,2,2048]{2,1,0:T(2,128)(2,1)}), bf16[128,2,2048]{2,1,0:T(2,128)(2,1)S(1)}, u32[]{:S(2)}, u32[]{:S(2)}) %all-to-all-start) | async-done | bytes 1048608 | tf_op jit(solution)/shard_map/all_to_all | solution.py:175
  58.2 0.0 collective-permute-done.w1_ref
  58.2 4.9 %collective-permute-start.4 = (bf16[2048,512]{1,0:T(8,128)(2,1)}, bf16[2048,512]{1,0:T(8,128)(2,1)S(1)}, u32[]{:S(2)}, u32[]{:S(2)}) collective-permute-start(bf16[2048,512]{1,0:T(8,128)(2,1)} %collective-permute-done.w1_ref), channel_id=1, source_target_pairs={{0,1},{1,0},{2,3},{3,2},{4,5},{5,4},{6,7},{7,6},{8,9},{9,8},{10,11... | collective-permute-start | bytes 6291464 | tf_op jit(solution)/shard_map/ppermute | solution.py:186
  63.1 0.0 copy-done.8
  63.1 0.0 copy-start.2
  63.1 1.0 %copy-done.2 = bf16[128,2048]{1,0:T(8,128)(2,1)S(1)} copy-done((bf16[128,2048]{1,0:T(8,128)(2,1)S(1)}, bf16[128,2048]{1,0:T(8,128)(2,1)}, u32[]{:S(2)}) %copy-start.2) | copy-done | bytes 524312
  64.2 0.0 copy-start.3
  64.2 5.3 %score_first.1 = (bf16[256,2048]{1,0:T(8,128)(2,1)S(1)}, f32[256,1]{1,0:T(8,128)S(1)}, f32[128,1]{1,0:T(8,128)S(1)}) custom-call(bf16[128,2,2048]{2,1,0:T(2,128)(2,1)S(1)} %all-to-all-done.x_ref, f32[1,2048]{1,0:T(1,128)S(1)} %copy-done.6, bf16[128,2048]{1,0:T(8,128)(2,1)S(1)} %copy-done.2, f32[128,1]{1,0:T(8,128)S(1)} %get-tuple-element.28.own_near_ref, ...), custom_call_target="tpu_custom_call" | custom-call | flops 5000000000 | tf_op jit(solution)/shard_map/score_first/pallas_call | solution.py:151
  69.4 0.0 collective-permute-done.3.w0_ref
  69.4 0.0 collective-permute-done.4.w1_ref
  69.4 0.0 copy-done.3
  69.5 4.3 %score_last.1 = (f32[128,2]{1,0:T(8,128)S(1)}, f32[1,128]{1,0:T(1,128)}) custom-call(bf16[256,2048]{1,0:T(8,128)(2,1)S(1)} %get-tuple-element.31.visit_ref, bf16[128,2048]{1,0:T(8,128)(2,1)S(1)} %copy-done.3, f32[256,1]{1,0:T(8,128)S(1)} %get-tuple-element.32.visit_near_ref, f32[128,1]{1,0:T(8,128)S(1)} %get-tuple-element.33.own_near_ref, ...), custom_call_target="tpu_custom_call" | custom-call | tf_op jit(solution)/shard_map/score_last/pallas_call | solution.py:151
  73.7 23.0 %all_to_all.16 = f32[128,1,2]{2,1,0:T(1,128)} all-to-all(f32[128,1,2]{2,1,0:T(1,128)S(1)} %bitcast.13), channel_id=1, replica_groups={{0,4,8,12,16,20,24,28,34,38,42,46,50,54,58,62,64,68,72,76,80,84,88,92,9..., dimensions={0} | all-to-all | bytes 2048 | tf_op jit(solution)/shard_map/all_to_all | solution.py:205
  96.7 1.5 %pick_answers.1 = f32[1,128]{1,0:T(1,128)} custom-call(f32[128,2]{1,0:T(8,128)} %bitcast.17, s32[1,128]{1,0:T(1,128)} %bitcast.14, s32[1,128]{1,0:T(1,128)} %copy-done.10), custom_call_target="tpu_custom_call" | custom-call | tf_op jit(solution)/shard_map/pick_answers/pallas_call | solution.py:81
Async XLA Ops:
  0.6 57.5 %collective-permute-start = (bf16[2048,512]{1,0:T(8,128)(2,1)}, bf16[2048,512]{1,0:T(8,128)(2,1)}, u32[]{:S(2)}, u32[]{:S(2)}) collective-permute-start(bf16[2048,512]{1,0:T(8,128)(2,1)} %bitcast.9), channel_id=1, source_target_pairs={{0,2},{2,0},{1,3},{3,1},{4,6},{6,4},{5,7},{7,5},{8,10},{10,8},{9,1... | collective-permute-start | bytes 6291464 | tf_op jit(solution)/shard_map/ppermute | solution.py:171
  4.6 1.0 %copy-start.4 = (bf16[128,2048]{1,0:T(8,128)(2,1)S(1)}, bf16[128,2048]{1,0:T(8,128)(2,1)}, u32[]{:S(2)}) copy-start(bf16[128,2048]{1,0:T(8,128)(2,1)} %x_ref.1) | copy-start | bytes 1572868
  5.6 0.7 copy-start.9
  6.3 0.7 copy-start.11
  8.6 0.5 copy-start.10
  9.1 26.3 %copy-start = (bf16[1,2048,512]{2,1,0:T(8,128)(2,1)S(1)}, bf16[1,2048,512]{2,1,0:T(8,128)(2,1)}, u32[]{:S(2)}) copy-start(bf16[1,2048,512]{2,1,0:T(8,128)(2,1)} %param.7) | copy-start | bytes 6291460
  9.1 26.3 %copy-start.6 = (f32[1,2048]{1,0:T(1,128)S(1)}, f32[1,2048]{1,0:T(1,128)}, u32[]{:S(2)}) copy-start(f32[1,2048]{1,0:T(1,128)} %gain_ref.3) | copy-start | bytes 24580
  9.1 49.0 %all-to-all-start = ((bf16[128,2,2048]{2,1,0:T(2,128)(2,1)}), bf16[128,2,2048]{2,1,0:T(2,128)(2,1)S(1)}, u32[]{:S(2)}, u32[]{:S(2)}) async-start(bf16[128,2,2048]{2,1,0:T(2,128)(2,1)} %get-tuple-element.20), calls=%async_computation | async-start | bytes 2097152 | tf_op jit(solution)/shard_map/all_to_all | solution.py:175
  28.3 4.2 %collective-permute-start.1 = (bf16[1,512]{1,0:T(2,128)(2,1)}, bf16[1,512]{1,0:T(2,128)(2,1)S(1)}, u32[]{:S(2)}, u32[]{:S(2)}) collective-permute-start(bf16[1,512]{1,0:T(2,128)(2,1)} %h0_ref.1), channel_id=1, source_target_pairs={{0,1},{1,0},{2,3},{3,2},{4,5},{5,4},{6,7},{7,6},{8,9},{9,8},{10,11... | collective-permute-start | bytes 3080 | tf_op jit(solution)/shard_map/ppermute | solution.py:176
  33.2 12.1 %collective-permute-start.2 = (bf16[2,512]{1,0:T(2,128)(2,1)S(1)}, bf16[2,512]{1,0:T(2,128)(2,1)S(1)}, u32[]{:S(2)}, u32[]{:S(2)}) collective-permute-start(bf16[2,512]{1,0:T(2,128)(2,1)S(1)} %pad_maximum_fusion), channel_id=1, source_target_pairs={{0,2},{2,0},{1,3},{3,1},{4,6},{6,4},{5,7},{7,5},{8,10},{10,8},{9,1... | collective-permute-start | bytes 6152 | tf_op jit(solution)/shard_map/ppermute | solution.py:179
  35.4 1.0 %copy-start.5 = (bf16[128,2048]{1,0:T(8,128)(2,1)S(1)}, bf16[128,2048]{1,0:T(8,128)(2,1)}, u32[]{:S(2)}) copy-start(bf16[128,2048]{1,0:T(8,128)(2,1)} %x_ref.1) | copy-start | bytes 1572868
  36.5 0.7 copy-start.7
  37.1 26.0 %copy-start.8 = (bf16[1,512]{1,0:T(2,128)(2,1)S(1)}, bf16[1,512]{1,0:T(2,128)(2,1)}, u32[]{:S(2)}) copy-start(bf16[1,512]{1,0:T(2,128)(2,1)} %h0_ref.1) | copy-start | bytes 3076
  38.4 0.8 copy-start.1
  39.2 30.3 %collective-permute-start.3 = (bf16[2048,512]{1,0:T(8,128)(2,1)S(1)}, bf16[2048,512]{1,0:T(8,128)(2,1)}, u32[]{:S(2)}, u32[]{:S(2)}) collective-permute-start(bf16[2048,512]{1,0:T(8,128)(2,1)S(1)} %bitcast.11), channel_id=1, source_target_pairs={{0,1},{1,0},{2,3},{3,2},{4,5},{5,4},{6,7},{7,6},{8,9},{9,8},{10,11... | collective-permute-start | bytes 6291464 | tf_op jit(solution)/shard_map/ppermute | solution.py:178
  58.2 11.3 %collective-permute-start.4 = (bf16[2048,512]{1,0:T(8,128)(2,1)}, bf16[2048,512]{1,0:T(8,128)(2,1)S(1)}, u32[]{:S(2)}, u32[]{:S(2)}) collective-permute-start(bf16[2048,512]{1,0:T(8,128)(2,1)} %collective-permute-done.w1_ref), channel_id=1, source_target_pairs={{0,1},{1,0},{2,3},{3,2},{4,5},{5,4},{6,7},{7,6},{8,9},{9,8},{10,11... | collective-permute-start | bytes 6291464 | tf_op jit(solution)/shard_map/ppermute | solution.py:186
  63.1 1.0 %copy-start.2 = (bf16[128,2048]{1,0:T(8,128)(2,1)S(1)}, bf16[128,2048]{1,0:T(8,128)(2,1)}, u32[]{:S(2)}) copy-start(bf16[128,2048]{1,0:T(8,128)(2,1)} %copy-done.1) | copy-start | bytes 1572868
  64.2 5.3 %copy-start.3 = (bf16[128,2048]{1,0:T(8,128)(2,1)S(1)}, bf16[128,2048]{1,0:T(8,128)(2,1)}, u32[]{:S(2)}) copy-start(bf16[128,2048]{1,0:T(8,128)(2,1)} %copy-done.1) | copy-start | bytes 1572868

commit v4 on v3

v4 whole, which is shorter than its diff:
```python
import functools

import jax
import jax.numpy as jnp
from jax import lax
from jax.experimental import pallas as pl
from jax.experimental.pallas import tpu as pltpu
from jax.sharding import Mesh, PartitionSpec as P

NZ, NXH, NY, NXL, NC = 8, 2, 8, 2, 2
AXES = ("z", "xh", "y", "xl", "c")
SWAP = [(0, 1), (1, 0)]
COST_FIRST = 5
SLOTS_VMEM = 60 * 1024 * 1024
SCORE_VMEM = 16 * 1024 * 1024
REST_VMEM = 32 * 1024 * 1024
STEP = 256


def exchange_groups():
    groups = []
    for flip in range(2):
        group = []
        for z in range(NZ):
            for xh in range(NXH):
                for y in range(NY):
                    group.append(((z * NXH + xh) * NY + y) * NXL + (xh ^ flip))
        groups.append(group)
    return groups


def hint(weight):
    return pl.CostEstimate(flops=weight * 1_000_000_000, bytes_accessed=0, transcendentals=0)


def fill_slots(owner_hbm, valid_hbm, rows_hbm, out_ref, slot_ref, owner_ref, valid_ref, rows_ref, arrived):
    pairs = ((owner_hbm, owner_ref), (valid_hbm, valid_ref), (rows_hbm, rows_ref))
    copies = [pltpu.make_async_copy(src, dst, arrived.at[i]) for i, (src, dst) in enumerate(pairs)]
    for copy in copies:
        copy.start()
    count = owner_ref.shape[1]
    agents = out_ref.shape[0]
    copies[0].wait()
    copies[1].wait()
    owner = owner_ref[...]
    live = valid_ref[...]
    owner_down = jnp.broadcast_to(owner, (count, count)).T
    live_down = jnp.broadcast_to(live, (count, count)).T
    down = lax.broadcasted_iota(jnp.int32, (count, count), 0)
    across = lax.broadcasted_iota(jnp.int32, (count, count), 1)
    earlier = (owner_down == owner) & (live_down == 1) & (down < across)
    slot = jnp.sum(earlier.astype(jnp.int32), axis=0, keepdims=True)
    agent = lax.broadcasted_iota(jnp.int32, (agents, count), 0)
    named = (agent == owner) & (live == 1)
    slot_ref[...] = jnp.where(live == 1, slot, 2)
    copies[2].wait()
    rows = rows_ref[...]
    for k in range(2):
        pick = (named & (slot == k)).astype(jnp.float32).astype(jnp.bfloat16)
        out_ref[:, k, :] = jnp.dot(pick, rows, preferred_element_type=jnp.float32).astype(jnp.bfloat16)


def slots_call(owner, valid, rows, agents):
    count, width = rows.shape
    return pl.pallas_call(
        fill_slots,
        in_specs=[pl.BlockSpec(memory_space=pltpu.HBM)] * 3,
        out_shape=[
            pltpu.HBM((agents, 2, width), jnp.bfloat16),
            jax.ShapeDtypeStruct((1, count), jnp.int32),
        ],
        scratch_shapes=[
            pltpu.VMEM(owner.shape, owner.dtype),
            pltpu.VMEM(valid.shape, valid.dtype),
            pltpu.VMEM(rows.shape, rows.dtype),
            pltpu.SemaphoreType.DMA((3,)),
        ],
        compiler_params=pltpu.CompilerParams(vmem_limit_bytes=SLOTS_VMEM),
        cost_estimate=hint(200),
        name="fill_slots",
    )(owner, valid, rows)


def pick_answers(returned_ref, owner_ref, slot_ref, out_ref):
    agents, count = returned_ref.shape[0], owner_ref.shape[1]
    slot = slot_ref[...]
    answer = jnp.where(slot == 0, returned_ref[:, 0:1], returned_ref[:, 1:2])
    agent = lax.broadcasted_iota(jnp.int32, (agents, count), 0)
    named = (agent == owner_ref[...]) & (slot < 2)
    out_ref[...] = jnp.sum(jnp.where(named, answer, 0.0), axis=0, keepdims=True)


def pick_call(returned, owner, slot):
    return pl.pallas_call(
        pick_answers,
        out_shape=jax.ShapeDtypeStruct(owner.shape, jnp.float32),
        cost_estimate=hint(0),
        name="pick_answers",
    )(returned, owner, slot)


def scaled_rows(rows, gain):
    wide = rows.astype(jnp.float32)
    squares = jnp.mean(wide * wide, axis=1, keepdims=True)
    return (wide * lax.rsqrt(squares + 1e-06) * gain).astype(jnp.bfloat16)


def values(rows, weight, head):
    hidden = jnp.dot(rows, weight, preferred_element_type=jnp.float32)
    half = 0.5 * hidden
    return jnp.sum((half + half * jnp.tanh(half)) * head, axis=1, keepdims=True)


def scale_own(x_ref, gain_ref, scaled_ref):
    scaled_ref[...] = scaled_rows(x_ref[...], gain_ref[...])


def scale_visit(x_ref, gain_ref, scaled_ref):
    count = x_ref.shape[0]
    for k in range(2):
        scaled_ref[k * count : (k + 1) * count, :] = scaled_rows(x_ref[:, k, :], gain_ref[...])


def score_rows(
    visit_ref, own_hbm, w0_hbm, h0_ref, w1_hbm, h1_ref, w2_hbm, w3_hbm, h23_ref,
    answer_out, value_out, own_ref, blocks_ref, arrived,
):
    weights = (w0_hbm, w1_hbm, w2_hbm, w3_hbm)
    copies = [pltpu.make_async_copy(own_hbm, own_ref, arrived.at[0])]
    jobs = []
    for n, w_hbm in enumerate(weights):
        for start in range(0, w_hbm.shape[1], STEP):
            i = len(jobs)
            jobs.append((n, start))
            copies.append(pltpu.make_async_copy(w_hbm.at[:, pl.ds(start, STEP)], blocks_ref.at[i], arrived.at[i + 1]))
    for copy in copies:
        copy.start()
    heads = [h0_ref[...].astype(jnp.float32), h1_ref[...].astype(jnp.float32)]
    far_heads = h23_ref[...].astype(jnp.float32)
    heads += [far_heads[0:1], far_heads[1:2]]
    copies[0].wait()
    visit = jnp.zeros((visit_ref.shape[0], 1), jnp.float32)
    own = jnp.zeros((own_ref.shape[0], 1), jnp.float32)
    for i, (n, start) in enumerate(jobs):
        copies[i + 1].wait()
        block, head = blocks_ref[i], heads[n][:, start : start + STEP]
        visit += values(visit_ref[...], block, head)
        own += values(own_ref[...], block, head)
    half = answer_out.shape[0]
    answer_out[:, 0:1] = visit[:half]
    answer_out[:, 1:2] = visit[half:]
    value_out[...] = jnp.broadcast_to(own, (half, half)).T[0:1]


def score_call(body, operands, outs, weight, hbm=(), scratch=(), limit=0):
    vmem, anywhere = pl.BlockSpec(memory_space=pltpu.VMEM), pl.BlockSpec(memory_space=pl.ANY)
    return pl.pallas_call(
        body,
        in_specs=[anywhere if i in hbm else vmem for i in range(len(operands))],
        out_shape=outs,
        scratch_shapes=scratch,
        compiler_params=pltpu.CompilerParams(vmem_limit_bytes=limit or SCORE_VMEM),
        cost_estimate=hint(weight),
        name=body.__name__,
    )(*operands)


def per_device(observations, weights, gains, heads, pairing, valid):
    rows_dev, width = observations.shape
    n_agents = NZ * NXH * NY
    groups = exchange_groups()
    own_w = weights[0]
    exchange = ("z", "xh", "y", "xl")

    far_w = lax.ppermute(own_w, "xl", SWAP)
    owner = pairing.reshape(1, rows_dev)
    outgoing, slot = slots_call(owner, valid.reshape(1, rows_dev), observations, n_agents)
    near_h, slot = lax.optimization_barrier((heads, slot))
    received = lax.all_to_all(outgoing, exchange, 0, 0, axis_index_groups=groups, tiled=True)
    sib_h = lax.ppermute(near_h, "c", SWAP)
    near_w, sib_h = lax.optimization_barrier((own_w, sib_h))
    sib_w = lax.ppermute(near_w, "c", SWAP)
    far_h = lax.ppermute(jnp.concatenate([heads, sib_h], axis=0), "xl", SWAP)
    f32, bf16 = jnp.float32, jnp.bfloat16
    visits, units = 2 * n_agents, own_w.shape[1]
    shape = jax.ShapeDtypeStruct
    own_scaled = score_call(scale_own, (observations, gains), pltpu.HBM((rows_dev, width), bf16), 0)
    received, far_h, own_scaled = lax.optimization_barrier((received, far_h, own_scaled))
    far_sib_w = lax.ppermute(far_w, "c", SWAP)
    visit_scaled = score_call(scale_visit, (received, gains), shape((visits, width), bf16), COST_FIRST)
    blocks = 4 * units // STEP
    answers, own_value = score_call(
        score_rows,
        (visit_scaled, own_scaled, own_w, heads, sib_w, sib_h, far_w, far_sib_w, far_h),
        [shape((n_agents, 2), f32), shape((1, rows_dev), f32)],
        0,
        hbm=(1, 2, 4, 6, 7),
        scratch=[
            pltpu.VMEM((rows_dev, width), bf16),
            pltpu.VMEM((blocks, width, STEP), bf16),
            pltpu.SemaphoreType.DMA((blocks + 1,)),
        ],
        limit=REST_VMEM,
    )
    returned = lax.all_to_all(answers, exchange, 0, 0, axis_index_groups=groups, tiled=True)

    opponent_value = pick_call(returned, owner, slot)
    return own_value.reshape(rows_dev), opponent_value.reshape(rows_dev)


def solution(mesh):
    wide = Mesh(mesh.devices.reshape(NZ, NXH, NY, NXL, NC), AXES)
    league, rep = AXES[:3], AXES[3:]
    return jax.shard_map(
        per_device,
        mesh=wide,
        in_specs=(
            P(AXES, None),
            P(league, None, rep),
            P(league, None),
            P(league, rep),
            P(AXES, None),
            P(AXES),
        ),
        out_specs=(P(AXES), P(AXES)),
        check_vma=False,
    )
```

time: 98.9 us -> 104 us (1.052)
  blocking collectives: 23 us -> 32 us
  local copies, waits for them, and re-layouts: 6.42 us -> 1.06 us
  starting transfers between devices: 35.9 us -> 40.6 us
  waiting for transfers between devices: 17.5 us -> 12.8 us
  Pallas kernels: 13.9 us -> 15.7 us
    all_to_all x1, waiting for transfers between devices: 12.9 us -> 0.01 us  [per_device(): lax.all_to_all(outgoing, exchange, 0, 0, axis_index_groups=groups, tiled=...]
    ppermute x1, waiting for transfers between devices: 0.01 us -> 11.8 us  [per_device(): far_w = lax.ppermute(own_w, 'xl', SWAP)]
    all_to_all x1, blocking collectives: 23 us -> 32 us  [per_device(): lax.all_to_all(answers, exchange, 0, 0, axis_index_groups=groups, tiled=T...]
    unnamed x24 -> x10, local copies, waits for them, and re-layouts: 6.42 us -> 1.06 us
    ppermute x1, waiting for transfers between devices: 3.55 us -> 0.01 us  [per_device(): far_h = lax.ppermute(jnp.concatenate([heads, sib_h], axis=0), 'xl', SWAP)]
    ppermute x1, starting transfers between devices: 4.92 us -> 8.14 us  [per_device(): far_sib_w = lax.ppermute(far_w, 'c', SWAP)]
    pallas_call x4, Pallas kernels: 12.4 us -> 14.2 us  [the longest x3 11.5 us: score_call(): pl.pallas_call(body, in_specs=[anywhere if i in hbm else vmem for i in ra...]
    ppermute x1, starting transfers between devices: 2.22 us -> 3.36 us  [per_device(): far_h = lax.ppermute(jnp.concatenate([heads, sib_h], axis=0), 'xl', SWAP)]
  transfers between devices with their start and end apart: 6 -> 6, of which waited for: 3 -> 2; matrix products, arithmetic and copies ran while one was open for 1% -> 1% of each run, Pallas kernels for 8% -> 7%
where the time goes in v4:
time: 104 us
  starting transfers between devices  40.6 us (39%)
  blocking collectives  32 us (31%)
  Pallas kernels  15.7 us (15%)
  waiting for transfers between devices  12.8 us (12%)
  local copies, waits for them, and re-layouts  1.06 us (1%)
    all_to_all x1, blocking collectives, per_device(): lax.all_to_all(answers, exchange, 0, 0, axis_index_groups=groups, tiled=T...  32 us
    all_to_all x1, starting transfers between devices, per_device(): lax.all_to_all(outgoing, exchange, 0, 0, axis_index_groups=groups, tiled=...  19.7 us
    ppermute x1, waiting for transfers between devices, per_device(): far_w = lax.ppermute(own_w, 'xl', SWAP)  11.8 us
    pallas_call x3, Pallas kernels, score_call(): pl.pallas_call(body, in_specs=[anywhere if i in hbm else vmem for i in ra...  11.5 us
    ppermute x1, starting transfers between devices, per_device(): far_sib_w = lax.ppermute(far_w, 'c', SWAP)  8.14 us
    ppermute x1, starting transfers between devices, per_device(): far_w = lax.ppermute(own_w, 'xl', SWAP)  3.95 us
    ppermute x1, starting transfers between devices, per_device(): far_h = lax.ppermute(jnp.concatenate([heads, sib_h], axis=0), 'xl', SWAP)  3.36 us
    ppermute x1, starting transfers between devices, per_device(): sib_h = lax.ppermute(near_h, 'c', SWAP)  3.15 us
  transfers between devices with their start and end apart: 6, of which 2 were waited for; matrix products, arithmetic and copies ran while one was open for 1% of the time, Pallas kernels for 7%

profile of v4, /device:TPU:1, one launch (start us, length us, event | category | flops | bytes accessed | tf_op | source)
XLA Modules:
  0.0 103.5 jit_solution(831767536801889)
XLA Ops:
  0.6 4.0 %collective-permute-start.3 = (bf16[2048,512]{1,0:T(8,128)(2,1)}, bf16[2048,512]{1,0:T(8,128)(2,1)}, u32[]{:S(2)}, u32[]{:S(2)}) collective-permute-start(bf16[2048,512]{1,0:T(8,128)(2,1)} %bitcast.9), channel_id=1, source_target_pairs={{0,2},{2,0},{1,3},{3,1},{4,6},{6,4},{5,7},{7,5},{8,10},{10,8},{9,1... | collective-permute-start | bytes 6291464 | tf_op jit(solution)/shard_map/ppermute | solution.py:175
  4.6 2.7 %fill_slots.1 = (bf16[128,2,2048]{2,1,0:T(2,128)(2,1)}, s32[1,128]{1,0:T(1,128)}) custom-call(s32[1,128]{1,0:T(1,128)} %bitcast.14, s32[1,128]{1,0:T(1,128)} %bitcast.17, bf16[128,2048]{1,0:T(8,128)(2,1)} %x_ref.1), custom_call_target="tpu_custom_call" | custom-call | flops 199999995904 | tf_op jit(solution)/shard_map/fill_slots/pallas_call | solution.py:65
  7.3 0.0 copy-start
  7.3 0.0 copy-start.3
  7.3 19.7 %all-to-all-start = ((bf16[128,2,2048]{2,1,0:T(2,128)(2,1)}), bf16[128,2,2048]{2,1,0:T(2,128)(2,1)}, u32[]{:S(2)}, u32[]{:S(2)}) async-start(bf16[128,2,2048]{2,1,0:T(2,128)(2,1)} %get-tuple-element.13), calls=%async_computation | async-start | bytes 2097152 | tf_op jit(solution)/shard_map/all_to_all | solution.py:179
  27.0 3.2 %collective-permute-start = (bf16[1,512]{1,0:T(2,128)(2,1)}, bf16[1,512]{1,0:T(2,128)(2,1)S(1)}, u32[]{:S(2)}, u32[]{:S(2)}) collective-permute-start(bf16[1,512]{1,0:T(2,128)(2,1)} %h0_ref.1), channel_id=1, source_target_pairs={{0,1},{1,0},{2,3},{3,2},{4,5},{5,4},{6,7},{7,6},{8,9},{9,8},{10,11... | collective-permute-start | bytes 3080 | tf_op jit(solution)/shard_map/ppermute | solution.py:180
  30.2 1.0 collective-permute-done.h1_ref
  31.2 0.0 copy-done
  31.2 2.2 %collective-permute-start.2 = (bf16[2048,512]{1,0:T(8,128)(2,1)S(1)}, bf16[2048,512]{1,0:T(8,128)(2,1)}, u32[]{:S(2)}, u32[]{:S(2)}) collective-permute-start(bf16[2048,512]{1,0:T(8,128)(2,1)S(1)} %bitcast.10), channel_id=1, source_target_pairs={{0,1},{1,0},{2,3},{3,2},{4,5},{5,4},{6,7},{7,6},{8,9},{9,8},{10,11... | collective-permute-start | bytes 6291464 | tf_op jit(solution)/shard_map/ppermute | solution.py:182
  33.4 11.8 %collective-permute-done.3.w2_hbm = bf16[2048,512]{1,0:T(8,128)(2,1)} collective-permute-done((bf16[2048,512]{1,0:T(8,128)(2,1)}, bf16[2048,512]{1,0:T(8,128)(2,1)}, u32[]{:S(2)}, u32[]{:S(2)}) %collective-permute-start.3) | collective-permute-done | bytes 2097184 | tf_op jit(solution)/shard_map/ppermute | solution.py:175
  45.2 8.1 %collective-permute-start.4 = (bf16[2048,512]{1,0:T(8,128)(2,1)}, bf16[2048,512]{1,0:T(8,128)(2,1)}, u32[]{:S(2)}, u32[]{:S(2)}) collective-permute-start(bf16[2048,512]{1,0:T(8,128)(2,1)} %collective-permute-done.3.w2_hbm), channel_id=1, source_target_pairs={{0,1},{1,0},{2,3},{3,2},{4,5},{5,4},{6,7},{7,6},{8,9},{9,8},{10,11... | collective-permute-start | bytes 6291464 | tf_op jit(solution)/shard_map/ppermute | solution.py:189
  53.4 0.7 pad_maximum_fusion
  54.1 3.4 %collective-permute-start.1 = (bf16[2,512]{1,0:T(2,128)(2,1)S(1)}, bf16[2,512]{1,0:T(2,128)(2,1)S(1)}, u32[]{:S(2)}, u32[]{:S(2)}) collective-permute-start(bf16[2,512]{1,0:T(2,128)(2,1)S(1)} %pad_maximum_fusion), channel_id=1, source_target_pairs={{0,2},{2,0},{1,3},{3,1},{4,6},{6,4},{5,7},{7,5},{8,10},{10,8},{9,1... | collective-permute-start | bytes 6152 | tf_op jit(solution)/shard_map/ppermute | solution.py:183
  57.4 0.0 copy-done.3
  57.5 0.0 copy-start.2
  57.5 1.0 copy-done.2
  58.5 1.1 %scale_own.1.own_hbm = bf16[128,2048]{1,0:T(8,128)(2,1)} custom-call(bf16[128,2048]{1,0:T(8,128)(2,1)S(1)} %copy-done.2, f32[1,2048]{1,0:T(1,128)S(1)} %copy-done.3), custom_call_target="tpu_custom_call" | custom-call | tf_op jit(solution)/shard_map/scale_own/pallas_call | solution.py:157
  59.6 0.0 copy-start.1
  59.6 0.0 copy-start.4
  59.6 0.0 collective-permute-done.1.h23_ref
  59.6 0.0 all-to-all-done.x_ref
  59.6 3.2 %scale_visit.1.visit_ref = bf16[256,2048]{1,0:T(8,128)(2,1)S(1)} custom-call(bf16[128,2,2048]{2,1,0:T(2,128)(2,1)} %all-to-all-done.x_ref, f32[1,2048]{1,0:T(1,128)S(1)} %copy-done.3), custom_call_target="tpu_custom_call" | custom-call | flops 5000000000 | tf_op jit(solution)/shard_map/scale_visit/pallas_call | solution.py:157
  62.8 0.0 collective-permute-done.2.w1_hbm
  62.8 0.0 collective-permute-done.4.w3_hbm
  62.8 0.0 copy-done.1
  62.8 0.0 copy-done.4
  62.8 7.3 %score_rows.1 = (f32[128,2]{1,0:T(8,128)S(1)}, f32[1,128]{1,0:T(1,128)}) custom-call(bf16[256,2048]{1,0:T(8,128)(2,1)S(1)} %scale_visit.1.visit_ref, bf16[128,2048]{1,0:T(8,128)(2,1)S(1)} %copy-done.1, bf16[2048,512]{1,0:T(8,128)(2,1)S(1)} %bitcast.11, bf16[1,512]{1,0:T(2,128)(2,1)S(1)} %copy-done.4, bf16[2048,512]{1,0:T(8,128)(2,1)} %collective-permute-done.2.w1_hbm, ...), custom_call_target="tpu_custom_call" | custom-call | tf_op jit(solution)/shard_map/score_rows/pallas_call | solution.py:157
  70.1 32.0 %all_to_all.16 = f32[128,1,2]{2,1,0:T(1,128)} all-to-all(f32[128,1,2]{2,1,0:T(1,128)S(1)} %bitcast.12), channel_id=1, replica_groups={{0,4,8,12,16,20,24,28,34,38,42,46,50,54,58,62,64,68,72,76,80,84,88,92,9..., dimensions={0} | all-to-all | bytes 2048 | tf_op jit(solution)/shard_map/all_to_all | solution.py:205
  102.1 1.5 %pick_answers.1 = f32[1,128]{1,0:T(1,128)} custom-call(f32[128,2]{1,0:T(8,128)} %bitcast.13, s32[1,128]{1,0:T(1,128)} %bitcast.15, s32[1,128]{1,0:T(1,128)} %get-tuple-element.23.slot_ref), custom_call_target="tpu_custom_call" | custom-call | tf_op jit(solution)/shard_map/pick_answers/pallas_call | solution.py:94
Async XLA Ops:
  0.6 44.6 %collective-permute-start.3 = (bf16[2048,512]{1,0:T(8,128)(2,1)}, bf16[2048,512]{1,0:T(8,128)(2,1)}, u32[]{:S(2)}, u32[]{:S(2)}) collective-permute-start(bf16[2048,512]{1,0:T(8,128)(2,1)} %bitcast.9), channel_id=1, source_target_pairs={{0,2},{2,0},{1,3},{3,1},{4,6},{6,4},{5,7},{7,5},{8,10},{10,8},{9,1... | collective-permute-start | bytes 6291464 | tf_op jit(solution)/shard_map/ppermute | solution.py:175
  7.3 23.9 %copy-start = (bf16[1,2048,512]{2,1,0:T(8,128)(2,1)S(1)}, bf16[1,2048,512]{2,1,0:T(8,128)(2,1)}, u32[]{:S(2)}) copy-start(bf16[1,2048,512]{2,1,0:T(8,128)(2,1)} %param.7) | copy-start | bytes 6291460
  7.3 50.2 %copy-start.3 = (f32[1,2048]{1,0:T(1,128)S(1)}, f32[1,2048]{1,0:T(1,128)}, u32[]{:S(2)}) copy-start(f32[1,2048]{1,0:T(1,128)} %gain_ref.3) | copy-start | bytes 24580
  7.3 52.3 %all-to-all-start = ((bf16[128,2,2048]{2,1,0:T(2,128)(2,1)}), bf16[128,2,2048]{2,1,0:T(2,128)(2,1)}, u32[]{:S(2)}, u32[]{:S(2)}) async-start(bf16[128,2,2048]{2,1,0:T(2,128)(2,1)} %get-tuple-element.13), calls=%async_computation | async-start | bytes 2097152 | tf_op jit(solution)/shard_map/all_to_all | solution.py:179
  27.0 4.2 %collective-permute-start = (bf16[1,512]{1,0:T(2,128)(2,1)}, bf16[1,512]{1,0:T(2,128)(2,1)S(1)}, u32[]{:S(2)}, u32[]{:S(2)}) collective-permute-start(bf16[1,512]{1,0:T(2,128)(2,1)} %h0_ref.1), channel_id=1, source_target_pairs={{0,1},{1,0},{2,3},{3,2},{4,5},{5,4},{6,7},{7,6},{8,9},{9,8},{10,11... | collective-permute-start | bytes 3080 | tf_op jit(solution)/shard_map/ppermute | solution.py:180
  31.2 31.6 %collective-permute-start.2 = (bf16[2048,512]{1,0:T(8,128)(2,1)S(1)}, bf16[2048,512]{1,0:T(8,128)(2,1)}, u32[]{:S(2)}, u32[]{:S(2)}) collective-permute-start(bf16[2048,512]{1,0:T(8,128)(2,1)S(1)} %bitcast.10), channel_id=1, source_target_pairs={{0,1},{1,0},{2,3},{3,2},{4,5},{5,4},{6,7},{7,6},{8,9},{9,8},{10,11... | collective-permute-start | bytes 6291464 | tf_op jit(solution)/shard_map/ppermute | solution.py:182
  45.2 17.6 %collective-permute-start.4 = (bf16[2048,512]{1,0:T(8,128)(2,1)}, bf16[2048,512]{1,0:T(8,128)(2,1)}, u32[]{:S(2)}, u32[]{:S(2)}) collective-permute-start(bf16[2048,512]{1,0:T(8,128)(2,1)} %collective-permute-done.3.w2_hbm), channel_id=1, source_target_pairs={{0,1},{1,0},{2,3},{3,2},{4,5},{5,4},{6,7},{7,6},{8,9},{9,8},{10,11... | collective-permute-start | bytes 6291464 | tf_op jit(solution)/shard_map/ppermute | solution.py:189
  54.1 5.5 %collective-permute-start.1 = (bf16[2,512]{1,0:T(2,128)(2,1)S(1)}, bf16[2,512]{1,0:T(2,128)(2,1)S(1)}, u32[]{:S(2)}, u32[]{:S(2)}) collective-permute-start(bf16[2,512]{1,0:T(2,128)(2,1)S(1)} %pad_maximum_fusion), channel_id=1, source_target_pairs={{0,2},{2,0},{1,3},{3,1},{4,6},{6,4},{5,7},{7,5},{8,10},{10,8},{9,1... | collective-permute-start | bytes 6152 | tf_op jit(solution)/shard_map/ppermute | solution.py:183
  57.5 1.0 %copy-start.2 = (bf16[128,2048]{1,0:T(8,128)(2,1)S(1)}, bf16[128,2048]{1,0:T(8,128)(2,1)}, u32[]{:S(2)}) copy-start(bf16[128,2048]{1,0:T(8,128)(2,1)} %x_ref.1) | copy-start | bytes 1572868
  59.6 3.3 %copy-start.1 = (bf16[128,2048]{1,0:T(8,128)(2,1)S(1)}, bf16[128,2048]{1,0:T(8,128)(2,1)}, u32[]{:S(2)}) copy-start(bf16[128,2048]{1,0:T(8,128)(2,1)} %scale_own.1.own_hbm) | copy-start | bytes 1572868
  59.6 3.3 %copy-start.4 = (bf16[1,512]{1,0:T(2,128)(2,1)S(1)}, bf16[1,512]{1,0:T(2,128)(2,1)}, u32[]{:S(2)}) copy-start(bf16[1,512]{1,0:T(2,128)(2,1)} %h0_ref.1) | copy-start | bytes 3076

commit v5 on v4

--- a/solution.py
+++ b/solution.py
@@ -15,6 +15,7 @@
 SCORE_VMEM = 16 * 1024 * 1024
 REST_VMEM = 32 * 1024 * 1024
 STEP = 256
+SCALE_AGENTS = 32
 
 
 def exchange_groups():
@@ -50,14 +51,12 @@
     across = lax.broadcasted_iota(jnp.int32, (count, count), 1)
     earlier = (owner_down == owner) & (live_down == 1) & (down < across)
     slot = jnp.sum(earlier.astype(jnp.int32), axis=0, keepdims=True)
-    agent = lax.broadcasted_iota(jnp.int32, (agents, count), 0)
-    named = (agent == owner) & (live == 1)
     slot_ref[...] = jnp.where(live == 1, slot, 2)
+    place = lax.broadcasted_iota(jnp.int32, (2 * agents, count), 0)
+    pick = ((place == 2 * owner + slot) & (live == 1)).astype(jnp.float32).astype(jnp.bfloat16)
     copies[2].wait()
-    rows = rows_ref[...]
-    for k in range(2):
-        pick = (named & (slot == k)).astype(jnp.float32).astype(jnp.bfloat16)
-        out_ref[:, k, :] = jnp.dot(pick, rows, preferred_element_type=jnp.float32).astype(jnp.bfloat16)
+    out = jnp.dot(pick, rows_ref[...], preferred_element_type=jnp.float32).astype(jnp.bfloat16)
+    out_ref[...] = out.reshape(out_ref.shape)
 
 
 def slots_call(owner, valid, rows, agents):
@@ -115,41 +114,56 @@
     scaled_ref[...] = scaled_rows(x_ref[...], gain_ref[...])
 
 
-def scale_visit(x_ref, gain_ref, scaled_ref):
-    count = x_ref.shape[0]
-    for k in range(2):
-        scaled_ref[k * count : (k + 1) * count, :] = scaled_rows(x_ref[:, k, :], gain_ref[...])
-
-
-def score_rows(
-    visit_ref, own_hbm, w0_hbm, h0_ref, w1_hbm, h1_ref, w2_hbm, w3_hbm, h23_ref,
-    answer_out, value_out, own_ref, blocks_ref, arrived,
-):
-    weights = (w0_hbm, w1_hbm, w2_hbm, w3_hbm)
-    copies = [pltpu.make_async_copy(own_hbm, own_ref, arrived.at[0])]
+def fetch_blocks(weights, blocks_ref, arrived):
     jobs = []
     for n, w_hbm in enumerate(weights):
         for start in range(0, w_hbm.shape[1], STEP):
             i = len(jobs)
-            jobs.append((n, start))
-            copies.append(pltpu.make_async_copy(w_hbm.at[:, pl.ds(start, STEP)], blocks_ref.at[i], arrived.at[i + 1]))
-    for copy in copies:
-        copy.start()
-    heads = [h0_ref[...].astype(jnp.float32), h1_ref[...].astype(jnp.float32)]
-    far_heads = h23_ref[...].astype(jnp.float32)
-    heads += [far_heads[0:1], far_heads[1:2]]
-    copies[0].wait()
-    visit = jnp.zeros((visit_ref.shape[0], 1), jnp.float32)
-    own = jnp.zeros((own_ref.shape[0], 1), jnp.float32)
-    for i, (n, start) in enumerate(jobs):
-        copies[i + 1].wait()
-        block, head = blocks_ref[i], heads[n][:, start : start + STEP]
-        visit += values(visit_ref[...], block, head)
-        own += values(own_ref[...], block, head)
-    half = answer_out.shape[0]
-    answer_out[:, 0:1] = visit[:half]
-    answer_out[:, 1:2] = visit[half:]
-    value_out[...] = jnp.broadcast_to(own, (half, half)).T[0:1]
+            copy = pltpu.make_async_copy(w_hbm.at[:, pl.ds(start, STEP)], blocks_ref.at[i], arrived.at[i])
+            copy.start()
+            jobs.append((copy, n, start))
+    return jobs
+
+
+def add_blocks(total, rows_ref, jobs, blocks_ref, heads):
+    for i, (copy, n, start) in enumerate(jobs):
+        copy.wait()
+        total += values(rows_ref[...], blocks_ref[i], heads[n][:, start : start + STEP])
+    return total
+
+
+def score_first(
+    x_hbm, gain_ref, own_hbm, w_hbm, h_ref, scaled_ref, value_ref, x_ref, blocks_ref, rows_here, arrived
+):
+    agents, slots, _ = x_ref.shape
+    visits, owns = agents * slots, own_hbm.shape[0]
+    visit_copy = pltpu.make_async_copy(x_hbm, x_ref, rows_here.at[0])
+    own_copy = pltpu.make_async_copy(own_hbm, scaled_ref.at[pl.ds(visits, owns), :], rows_here.at[1])
+    visit_copy.start()
+    jobs = fetch_blocks((w_hbm,), blocks_ref, arrived)
+    own_copy.start()
+    gain = gain_ref[...]
+    heads = (h_ref[...].astype(jnp.float32)[0:1],)
+    visit_copy.wait()
+    for start in range(0, agents, SCALE_AGENTS):
+        rows = x_ref[start : start + SCALE_AGENTS].reshape(SCALE_AGENTS * slots, gain.shape[1])
+        scaled_ref[start * slots : (start + SCALE_AGENTS) * slots, :] = scaled_rows(rows, gain)
+    own_copy.wait()
+    value_ref[...] = add_blocks(jnp.zeros(value_ref.shape, jnp.float32), scaled_ref, jobs, blocks_ref, heads)
+
+
+def score_last(
+    scaled_ref, near_ref, w0_hbm, h0_ref, w1_hbm, h1_ref, w2_hbm, h2_ref, answer_out, value_out, total_ref, blocks_ref, arrived
+):
+    jobs = fetch_blocks((w0_hbm, w1_hbm, w2_hbm), blocks_ref, arrived)
+    heads = (h0_ref[...].astype(jnp.float32), h1_ref[...].astype(jnp.float32), h2_ref[...].astype(jnp.float32)[1:2])
+    total = add_blocks(near_ref[...], scaled_ref, jobs, blocks_ref, heads)
+    total_ref[...] = total
+    agents, slots = answer_out.shape
+    for k in range(slots):
+        answer_out[:, k : k + 1] = total_ref[pl.ds(k, agents, stride=slots), :]
+    owns = value_out.shape[1]
+    value_out[...] = jnp.broadcast_to(total[agents * slots :], (owns, owns)).T[0:1]
 
 
 def score_call(body, operands, outs, weight, hbm=(), scratch=(), limit=0):
@@ -185,20 +199,33 @@
     visits, units = 2 * n_agents, own_w.shape[1]
     shape = jax.ShapeDtypeStruct
     own_scaled = score_call(scale_own, (observations, gains), pltpu.HBM((rows_dev, width), bf16), 0)
-    received, far_h, own_scaled = lax.optimization_barrier((received, far_h, own_scaled))
+    far_w, far_h, own_scaled = lax.optimization_barrier((far_w, far_h, own_scaled))
     far_sib_w = lax.ppermute(far_w, "c", SWAP)
-    visit_scaled = score_call(scale_visit, (received, gains), shape((visits, width), bf16), COST_FIRST)
-    blocks = 4 * units // STEP
+    blocks = units // STEP
+    scaled, near = score_call(
+        score_first,
+        (received, gains, own_scaled, far_w, far_h),
+        [shape((visits + rows_dev, width), bf16), shape((visits + rows_dev, 1), f32)],
+        COST_FIRST,
+        hbm=(0, 2, 3),
+        scratch=[
+            pltpu.VMEM(received.shape, bf16),
+            pltpu.VMEM((blocks, width, STEP), bf16),
+            pltpu.SemaphoreType.DMA((2,)),
+            pltpu.SemaphoreType.DMA((blocks,)),
+        ],
+        limit=REST_VMEM,
+    )
     answers, own_value = score_call(
-        score_rows,
-        (visit_scaled, own_scaled, own_w, heads, sib_w, sib_h, far_w, far_sib_w, far_h),
+        score_last,
+        (scaled, near, own_w, heads, sib_w, sib_h, far_sib_w, far_h),
         [shape((n_agents, 2), f32), shape((1, rows_dev), f32)],
         0,
-        hbm=(1, 2, 4, 6, 7),
+        hbm=(2, 4, 6),
         scratch=[
-            pltpu.VMEM((rows_dev, width), bf16),
-            pltpu.VMEM((blocks, width, STEP), bf16),
-            pltpu.SemaphoreType.DMA((blocks + 1,)),
+            pltpu.VMEM((visits + rows_dev, 1), f32),
+            pltpu.VMEM((3 * blocks, width, STEP), bf16),
+            pltpu.SemaphoreType.DMA((3 * blocks,)),
         ],
         limit=REST_VMEM,
     )

time: 104 us -> 99.9 us (0.961)
  blocking collectives: 32 us -> 29.9 us
  waiting for transfers between devices: 12.8 us -> 11 us
  starting transfers between devices: 40.6 us -> 39.2 us
    ppermute x1, waiting for transfers between devices: 11.8 us -> 0.01 us  [per_device(): far_w = lax.ppermute(own_w, 'xl', SWAP)]
    ppermute x1, waiting for transfers between devices: 0.01 us -> 7.17 us  [per_device(): far_h = lax.ppermute(jnp.concatenate([heads, sib_h], axis=0), 'xl', SWAP)]
    all_to_all x1, waiting for transfers between devices: 0.01 us -> 2.82 us  [per_device(): lax.all_to_all(outgoing, exchange, 0, 0, axis_index_groups=groups, tiled=...]
    all_to_all x1, blocking collectives: 32 us -> 29.9 us  [per_device(): lax.all_to_all(answers, exchange, 0, 0, axis_index_groups=groups, tiled=T...]
    ppermute x1, starting transfers between devices: 3.36 us -> 2.22 us  [per_device(): far_h = lax.ppermute(jnp.concatenate([heads, sib_h], axis=0), 'xl', SWAP)]
  transfers between devices with their start and end apart: 6 -> 6, of which waited for: 2 -> 3; matrix products, arithmetic and copies ran while one was open for 1% -> 1% of each run, Pallas kernels for 7% -> 7%
where the time goes in v5:
time: 99.9 us; the launch traced here: 99.3 us
  starting transfers between devices  39.2 us (39%)
  blocking collectives  29.9 us (30%)
  Pallas kernels  15.6 us (16%)
  waiting for transfers between devices  11 us (11%)
  local copies, waits for them, and re-layouts  2.09 us (2%)
    all_to_all x1, blocking collectives, per_device(): lax.all_to_all(answers, exchange, 0, 0, axis_index_groups=groups, tiled=T...  29.9 us
    all_to_all x1, starting transfers between devices, per_device(): lax.all_to_all(outgoing, exchange, 0, 0, axis_index_groups=groups, tiled=...  19.2 us
    pallas_call x3, Pallas kernels, score_call(): pl.pallas_call(body, in_specs=[anywhere if i in hbm else vmem for i in ra...  11.6 us
    ppermute x1, starting transfers between devices, per_device(): far_sib_w = lax.ppermute(far_w, 'c', SWAP)  8.16 us
    ppermute x1, waiting for transfers between devices, per_device(): far_h = lax.ppermute(jnp.concatenate([heads, sib_h], axis=0), 'xl', SWAP)  7.17 us
    ppermute x1, starting transfers between devices, per_device(): far_w = lax.ppermute(own_w, 'xl', SWAP)  3.95 us
    ppermute x1, starting transfers between devices, per_device(): sib_h = lax.ppermute(near_h, 'c', SWAP)  3.14 us
    all_to_all x1, waiting for transfers between devices, per_device(): lax.all_to_all(outgoing, exchange, 0, 0, axis_index_groups=groups, tiled=...  2.82 us
  transfers between devices with their start and end apart: 6, of which 3 were waited for; matrix products, arithmetic and copies ran while one was open for 1% of the time, Pallas kernels for 7%

profile of v5, /device:TPU:1, one launch (start us, length us, event | category | flops | bytes accessed | tf_op | source)
XLA Modules:
  0.0 99.3 jit_solution(10001977709324764705)
XLA Ops:
  0.6 4.0 %collective-permute-start = (bf16[2048,512]{1,0:T(8,128)(2,1)}, bf16[2048,512]{1,0:T(8,128)(2,1)}, u32[]{:S(2)}, u32[]{:S(2)}) collective-permute-start(bf16[2048,512]{1,0:T(8,128)(2,1)} %bitcast.9), channel_id=1, source_target_pairs={{0,2},{2,0},{1,3},{3,1},{4,6},{6,4},{5,7},{7,5},{8,10},{10,8},{9,1... | collective-permute-start | bytes 6291464 | tf_op jit(solution)/shard_map/ppermute | solution.py:189
  4.6 2.5 %fill_slots.1 = (bf16[128,2,2048]{2,1,0:T(2,128)(2,1)}, s32[1,128]{1,0:T(1,128)}) custom-call(s32[1,128]{1,0:T(1,128)} %bitcast.14, s32[1,128]{1,0:T(1,128)} %bitcast.17, bf16[128,2048]{1,0:T(8,128)(2,1)} %x_ref.1), custom_call_target="tpu_custom_call" | custom-call | flops 199999995904 | tf_op jit(solution)/shard_map/fill_slots/pallas_call | solution.py:64
  7.1 0.0 copy-start.3
  7.1 0.0 copy-start
  7.2 19.2 %all-to-all-start = ((bf16[128,2,2048]{2,1,0:T(2,128)(2,1)}), bf16[128,2,2048]{2,1,0:T(2,128)(2,1)S(1)}, u32[]{:S(2)}, u32[]{:S(2)}) async-start(bf16[128,2,2048]{2,1,0:T(2,128)(2,1)} %get-tuple-element.15), calls=%async_computation | async-start | bytes 2097152 | tf_op jit(solution)/shard_map/all_to_all | solution.py:193
  26.4 3.1 %collective-permute-start.1 = (bf16[1,512]{1,0:T(2,128)(2,1)}, bf16[1,512]{1,0:T(2,128)(2,1)S(1)}, u32[]{:S(2)}, u32[]{:S(2)}) collective-permute-start(bf16[1,512]{1,0:T(2,128)(2,1)} %h0_ref.1), channel_id=1, source_target_pairs={{0,1},{1,0},{2,3},{3,2},{4,5},{5,4},{6,7},{7,6},{8,9},{9,8},{10,11... | collective-permute-start | bytes 3080 | tf_op jit(solution)/shard_map/ppermute | solution.py:194
  29.5 1.0 %collective-permute-done.1.h1_ref = bf16[1,512]{1,0:T(2,128)(2,1)S(1)} collective-permute-done((bf16[1,512]{1,0:T(2,128)(2,1)}, bf16[1,512]{1,0:T(2,128)(2,1)S(1)}, u32[]{:S(2)}, u32[]{:S(2)}) %collective-permute-start.1) | collective-permute-done | bytes 1056 | tf_op jit(solution)/shard_map/ppermute | solution.py:194
  30.5 0.7 pad_maximum_fusion
  31.2 2.2 %collective-permute-start.2 = (bf16[2,512]{1,0:T(2,128)(2,1)S(1)}, bf16[2,512]{1,0:T(2,128)(2,1)S(1)}, u32[]{:S(2)}, u32[]{:S(2)}) collective-permute-start(bf16[2,512]{1,0:T(2,128)(2,1)S(1)} %pad_maximum_fusion), channel_id=1, source_target_pairs={{0,2},{2,0},{1,3},{3,1},{4,6},{6,4},{5,7},{7,5},{8,10},{10,8},{9,1... | collective-permute-start | bytes 6152 | tf_op jit(solution)/shard_map/ppermute | solution.py:197
  33.5 0.0 copy-done.3
  33.5 0.0 copy-start.1
  33.5 1.0 %copy-done.1 = bf16[128,2048]{1,0:T(8,128)(2,1)S(1)} copy-done((bf16[128,2048]{1,0:T(8,128)(2,1)S(1)}, bf16[128,2048]{1,0:T(8,128)(2,1)}, u32[]{:S(2)}) %copy-start.1) | copy-done | bytes 524312
  34.5 0.0 copy-start.4
  34.5 1.0 %scale_own.1.own_hbm = bf16[128,2048]{1,0:T(8,128)(2,1)} custom-call(bf16[128,2048]{1,0:T(8,128)(2,1)S(1)} %copy-done.1, f32[1,2048]{1,0:T(1,128)S(1)} %copy-done.3), custom_call_target="tpu_custom_call" | custom-call | tf_op jit(solution)/shard_map/scale_own/pallas_call | solution.py:171
  35.5 0.0 copy-done
  35.5 2.5 %collective-permute-start.3 = (bf16[2048,512]{1,0:T(8,128)(2,1)S(1)}, bf16[2048,512]{1,0:T(8,128)(2,1)}, u32[]{:S(2)}, u32[]{:S(2)}) collective-permute-start(bf16[2048,512]{1,0:T(8,128)(2,1)S(1)} %bitcast.10), channel_id=1, source_target_pairs={{0,1},{1,0},{2,3},{3,2},{4,5},{5,4},{6,7},{7,6},{8,9},{9,8},{10,11... | collective-permute-start | bytes 6291464 | tf_op jit(solution)/shard_map/ppermute | solution.py:196
  38.1 7.2 %collective-permute-done.2.h_ref.h2_ref = bf16[2,512]{1,0:T(2,128)(2,1)S(1)} collective-permute-done((bf16[2,512]{1,0:T(2,128)(2,1)S(1)}, bf16[2,512]{1,0:T(2,128)(2,1)S(1)}, u32[]{:S(2)}, u32[]{:S(2)}) %collective-permute-start.2) | collective-permute-done | bytes 2080 | tf_op jit(solution)/shard_map/ppermute | solution.py:197
  45.2 0.0 collective-permute-done.w_hbm
  45.2 8.2 %collective-permute-start.4 = (bf16[2048,512]{1,0:T(8,128)(2,1)}, bf16[2048,512]{1,0:T(8,128)(2,1)}, u32[]{:S(2)}, u32[]{:S(2)}) collective-permute-start(bf16[2048,512]{1,0:T(8,128)(2,1)} %collective-permute-done.w_hbm), channel_id=1, source_target_pairs={{0,1},{1,0},{2,3},{3,2},{4,5},{5,4},{6,7},{7,6},{8,9},{9,8},{10,11... | collective-permute-start | bytes 6291464 | tf_op jit(solution)/shard_map/ppermute | solution.py:203
  53.4 2.8 %all-to-all-done.x_hbm = bf16[128,2,2048]{2,1,0:T(2,128)(2,1)S(1)} async-done(((bf16[128,2,2048]{2,1,0:T(2,128)(2,1)}), bf16[128,2,2048]{2,1,0:T(2,128)(2,1)S(1)}, u32[]{:S(2)}, u32[]{:S(2)}) %all-to-all-start) | async-done | bytes 1048608 | tf_op jit(solution)/shard_map/all_to_all | solution.py:193
  56.2 0.0 copy-start.2
  56.2 1.0 %copy-done.2 = bf16[128,2048]{1,0:T(8,128)(2,1)S(1)} copy-done((bf16[128,2048]{1,0:T(8,128)(2,1)S(1)}, bf16[128,2048]{1,0:T(8,128)(2,1)}, u32[]{:S(2)}) %copy-start.2) | copy-done | bytes 524312
  57.3 3.4 %score_first.1 = (bf16[384,2048]{1,0:T(8,128)(2,1)S(1)}, f32[384,1]{1,0:T(8,128)S(1)}) custom-call(bf16[128,2,2048]{2,1,0:T(2,128)(2,1)S(1)} %all-to-all-done.x_hbm, f32[1,2048]{1,0:T(1,128)S(1)} %copy-done.3, bf16[128,2048]{1,0:T(8,128)(2,1)S(1)} %copy-done.2, bf16[2048,512]{1,0:T(8,128)(2,1)} %collective-permute-done.w_hbm, ...), custom_call_target="tpu_custom_call" | custom-call | flops 5000000000 | tf_op jit(solution)/shard_map/score_first/pallas_call | solution.py:171
  60.7 0.0 collective-permute-done.3.w1_hbm
  60.7 0.0 collective-permute-done.4.w2_hbm
  60.7 0.0 copy-done.4
  60.7 7.1 %score_last.1 = (f32[128,2]{1,0:T(8,128)S(1)}, f32[1,128]{1,0:T(1,128)}) custom-call(bf16[384,2048]{1,0:T(8,128)(2,1)S(1)} %get-tuple-element.22.scaled_ref, f32[384,1]{1,0:T(8,128)S(1)} %get-tuple-element.23.near_ref, bf16[2048,512]{1,0:T(8,128)(2,1)S(1)} %bitcast.11, bf16[1,512]{1,0:T(2,128)(2,1)S(1)} %copy-done.4, ...), custom_call_target="tpu_custom_call" | custom-call | tf_op jit(solution)/shard_map/score_last/pallas_call | solution.py:171
  67.9 29.9 %all_to_all.16 = f32[128,1,2]{2,1,0:T(1,128)} all-to-all(f32[128,1,2]{2,1,0:T(1,128)S(1)} %bitcast.12), channel_id=1, replica_groups={{0,4,8,12,16,20,24,28,34,38,42,46,50,54,58,62,64,68,72,76,80,84,88,92,9..., dimensions={0} | all-to-all | bytes 2048 | tf_op jit(solution)/shard_map/all_to_all | solution.py:232
  97.8 1.5 %pick_answers.1 = f32[1,128]{1,0:T(1,128)} custom-call(f32[128,2]{1,0:T(8,128)} %bitcast.13, s32[1,128]{1,0:T(1,128)} %bitcast.15, s32[1,128]{1,0:T(1,128)} %get-tuple-element.27.slot_ref), custom_call_target="tpu_custom_call" | custom-call | tf_op jit(solution)/shard_map/pick_answers/pallas_call | solution.py:93
Async XLA Ops:
  0.6 44.6 %collective-permute-start = (bf16[2048,512]{1,0:T(8,128)(2,1)}, bf16[2048,512]{1,0:T(8,128)(2,1)}, u32[]{:S(2)}, u32[]{:S(2)}) collective-permute-start(bf16[2048,512]{1,0:T(8,128)(2,1)} %bitcast.9), channel_id=1, source_target_pairs={{0,2},{2,0},{1,3},{3,1},{4,6},{6,4},{5,7},{7,5},{8,10},{10,8},{9,1... | collective-permute-start | bytes 6291464 | tf_op jit(solution)/shard_map/ppermute | solution.py:189
  7.1 26.3 %copy-start.3 = (f32[1,2048]{1,0:T(1,128)S(1)}, f32[1,2048]{1,0:T(1,128)}, u32[]{:S(2)}) copy-start(f32[1,2048]{1,0:T(1,128)} %gain_ref.3) | copy-start | bytes 24580
  7.1 28.4 %copy-start = (bf16[1,2048,512]{2,1,0:T(8,128)(2,1)S(1)}, bf16[1,2048,512]{2,1,0:T(8,128)(2,1)}, u32[]{:S(2)}) copy-start(bf16[1,2048,512]{2,1,0:T(8,128)(2,1)} %param.7) | copy-start | bytes 6291460
  7.2 49.1 %all-to-all-start = ((bf16[128,2,2048]{2,1,0:T(2,128)(2,1)}), bf16[128,2,2048]{2,1,0:T(2,128)(2,1)S(1)}, u32[]{:S(2)}, u32[]{:S(2)}) async-start(bf16[128,2,2048]{2,1,0:T(2,128)(2,1)} %get-tuple-element.15), calls=%async_computation | async-start | bytes 2097152 | tf_op jit(solution)/shard_map/all_to_all | solution.py:193
  26.4 4.2 %collective-permute-start.1 = (bf16[1,512]{1,0:T(2,128)(2,1)}, bf16[1,512]{1,0:T(2,128)(2,1)S(1)}, u32[]{:S(2)}, u32[]{:S(2)}) collective-permute-start(bf16[1,512]{1,0:T(2,128)(2,1)} %h0_ref.1), channel_id=1, source_target_pairs={{0,1},{1,0},{2,3},{3,2},{4,5},{5,4},{6,7},{7,6},{8,9},{9,8},{10,11... | collective-permute-start | bytes 3080 | tf_op jit(solution)/shard_map/ppermute | solution.py:194
  31.2 14.0 %collective-permute-start.2 = (bf16[2,512]{1,0:T(2,128)(2,1)S(1)}, bf16[2,512]{1,0:T(2,128)(2,1)S(1)}, u32[]{:S(2)}, u32[]{:S(2)}) collective-permute-start(bf16[2,512]{1,0:T(2,128)(2,1)S(1)} %pad_maximum_fusion), channel_id=1, source_target_pairs={{0,2},{2,0},{1,3},{3,1},{4,6},{6,4},{5,7},{7,5},{8,10},{10,8},{9,1... | collective-permute-start | bytes 6152 | tf_op jit(solution)/shard_map/ppermute | solution.py:197
  33.5 1.0 %copy-start.1 = (bf16[128,2048]{1,0:T(8,128)(2,1)S(1)}, bf16[128,2048]{1,0:T(8,128)(2,1)}, u32[]{:S(2)}) copy-start(bf16[128,2048]{1,0:T(8,128)(2,1)} %x_ref.1) | copy-start | bytes 1572868
  34.5 26.2 %copy-start.4 = (bf16[1,512]{1,0:T(2,128)(2,1)S(1)}, bf16[1,512]{1,0:T(2,128)(2,1)}, u32[]{:S(2)}) copy-start(bf16[1,512]{1,0:T(2,128)(2,1)} %h0_ref.1) | copy-start | bytes 3076
  35.5 25.2 %collective-permute-start.3 = (bf16[2048,512]{1,0:T(8,128)(2,1)S(1)}, bf16[2048,512]{1,0:T(8,128)(2,1)}, u32[]{:S(2)}, u32[]{:S(2)}) collective-permute-start(bf16[2048,512]{1,0:T(8,128)(2,1)S(1)} %bitcast.10), channel_id=1, source_target_pairs={{0,1},{1,0},{2,3},{3,2},{4,5},{5,4},{6,7},{7,6},{8,9},{9,8},{10,11... | collective-permute-start | bytes 6291464 | tf_op jit(solution)/shard_map/ppermute | solution.py:196
  45.2 15.5 %collective-permute-start.4 = (bf16[2048,512]{1,0:T(8,128)(2,1)}, bf16[2048,512]{1,0:T(8,128)(2,1)}, u32[]{:S(2)}, u32[]{:S(2)}) collective-permute-start(bf16[2048,512]{1,0:T(8,128)(2,1)} %collective-permute-done.w_hbm), channel_id=1, source_target_pairs={{0,1},{1,0},{2,3},{3,2},{4,5},{5,4},{6,7},{7,6},{8,9},{9,8},{10,11... | collective-permute-start | bytes 6291464 | tf_op jit(solution)/shard_map/ppermute | solution.py:203
  56.2 1.0 %copy-start.2 = (bf16[128,2048]{1,0:T(8,128)(2,1)S(1)}, bf16[128,2048]{1,0:T(8,128)(2,1)}, u32[]{:S(2)}) copy-start(bf16[128,2048]{1,0:T(8,128)(2,1)} %scale_own.1.own_hbm) | copy-start | bytes 1572868

commit v6 on v5

--- a/solution.py
+++ b/solution.py
@@ -14,7 +14,7 @@
 SLOTS_VMEM = 60 * 1024 * 1024
 SCORE_VMEM = 16 * 1024 * 1024
 REST_VMEM = 32 * 1024 * 1024
-STEP = 256
+STEP = 512
 SCALE_AGENTS = 32
 
 
@@ -110,10 +110,6 @@
     return jnp.sum((half + half * jnp.tanh(half)) * head, axis=1, keepdims=True)
 
 
-def scale_own(x_ref, gain_ref, scaled_ref):
-    scaled_ref[...] = scaled_rows(x_ref[...], gain_ref[...])
-
-
 def fetch_blocks(weights, blocks_ref, arrived):
     jobs = []
     for n, w_hbm in enumerate(weights):
@@ -125,45 +121,51 @@
     return jobs
 
 
-def add_blocks(total, rows_ref, jobs, blocks_ref, heads):
-    for i, (copy, n, start) in enumerate(jobs):
-        copy.wait()
-        total += values(rows_ref[...], blocks_ref[i], heads[n][:, start : start + STEP])
-    return total
-
-
-def score_first(
-    x_hbm, gain_ref, own_hbm, w_hbm, h_ref, scaled_ref, value_ref, x_ref, blocks_ref, rows_here, arrived
-):
+def score_own(x_ref, gain_ref, w_ref, h_ref, scaled_ref, value_ref):
+    rows = scaled_rows(x_ref[...], gain_ref[...])
+    scaled_ref[...] = rows
+    value_ref[...] = values(rows, w_ref[...], h_ref[...].astype(jnp.float32))
+
+
+def score_first(x_hbm, gain_ref, w_hbm, h_ref, scaled_ref, value_ref, x_ref, blocks_ref, rows_here, arrived):
     agents, slots, _ = x_ref.shape
-    visits, owns = agents * slots, own_hbm.shape[0]
     visit_copy = pltpu.make_async_copy(x_hbm, x_ref, rows_here.at[0])
-    own_copy = pltpu.make_async_copy(own_hbm, scaled_ref.at[pl.ds(visits, owns), :], rows_here.at[1])
     visit_copy.start()
     jobs = fetch_blocks((w_hbm,), blocks_ref, arrived)
-    own_copy.start()
     gain = gain_ref[...]
-    heads = (h_ref[...].astype(jnp.float32)[0:1],)
+    head = h_ref[...].astype(jnp.float32)[0:1]
     visit_copy.wait()
     for start in range(0, agents, SCALE_AGENTS):
         rows = x_ref[start : start + SCALE_AGENTS].reshape(SCALE_AGENTS * slots, gain.shape[1])
         scaled_ref[start * slots : (start + SCALE_AGENTS) * slots, :] = scaled_rows(rows, gain)
-    own_copy.wait()
-    value_ref[...] = add_blocks(jnp.zeros(value_ref.shape, jnp.float32), scaled_ref, jobs, blocks_ref, heads)
+    total = jnp.zeros(value_ref.shape, jnp.float32)
+    for i, (copy, _, start) in enumerate(jobs):
+        copy.wait()
+        total += values(scaled_ref[...], blocks_ref[i], head[:, start : start + STEP])
+    value_ref[...] = total
 
 
 def score_last(
-    scaled_ref, near_ref, w0_hbm, h0_ref, w1_hbm, h1_ref, w2_hbm, h2_ref, answer_out, value_out, total_ref, blocks_ref, arrived
+    visit_ref, visit_near_ref, own_ref, own_near_ref, w0_ref, h0_ref, w1_hbm, h1_ref, w2_hbm, w3_hbm, h23_ref,
+    answer_out, value_out, total_ref, blocks_ref, arrived,
 ):
-    jobs = fetch_blocks((w0_hbm, w1_hbm, w2_hbm), blocks_ref, arrived)
-    heads = (h0_ref[...].astype(jnp.float32), h1_ref[...].astype(jnp.float32), h2_ref[...].astype(jnp.float32)[1:2])
-    total = add_blocks(near_ref[...], scaled_ref, jobs, blocks_ref, heads)
-    total_ref[...] = total
+    jobs = fetch_blocks((w2_hbm, w1_hbm, w3_hbm), blocks_ref, arrived)
+    far_heads = h23_ref[...].astype(jnp.float32)
+    heads = (far_heads[0:1], h1_ref[...].astype(jnp.float32), far_heads[1:2])
+    visit = visit_near_ref[...] + values(visit_ref[...], w0_ref[...], h0_ref[...].astype(jnp.float32))
+    own = own_near_ref[...]
+    for i, (copy, n, start) in enumerate(jobs):
+        copy.wait()
+        head = heads[n][:, start : start + STEP]
+        own += values(own_ref[...], blocks_ref[i], head)
+        if n > 0:
+            visit += values(visit_ref[...], blocks_ref[i], head)
+    total_ref[...] = visit
     agents, slots = answer_out.shape
     for k in range(slots):
         answer_out[:, k : k + 1] = total_ref[pl.ds(k, agents, stride=slots), :]
     owns = value_out.shape[1]
-    value_out[...] = jnp.broadcast_to(total[agents * slots :], (owns, owns)).T[0:1]
+    value_out[...] = jnp.broadcast_to(own, (owns, owns)).T[0:1]
 
 
 def score_call(body, operands, outs, weight, hbm=(), scratch=(), limit=0):
@@ -198,32 +200,37 @@
     f32, bf16 = jnp.float32, jnp.bfloat16
     visits, units = 2 * n_agents, own_w.shape[1]
     shape = jax.ShapeDtypeStruct
-    own_scaled = score_call(scale_own, (observations, gains), pltpu.HBM((rows_dev, width), bf16), 0)
+    own_scaled, own_near = score_call(
+        score_own,
+        (observations, gains, own_w, heads),
+        [pltpu.HBM((rows_dev, width), bf16), shape((rows_dev, 1), f32)],
+        0,
+    )
     far_w, far_h, own_scaled = lax.optimization_barrier((far_w, far_h, own_scaled))
     far_sib_w = lax.ppermute(far_w, "c", SWAP)
     blocks = units // STEP
     scaled, near = score_call(
         score_first,
-        (received, gains, own_scaled, far_w, far_h),
-        [shape((visits + rows_dev, width), bf16), shape((visits + rows_dev, 1), f32)],
+        (received, gains, far_w, far_h),
+        [shape((visits, width), bf16), shape((visits, 1), f32)],
         COST_FIRST,
-        hbm=(0, 2, 3),
+        hbm=(0, 2),
         scratch=[
             pltpu.VMEM(received.shape, bf16),
             pltpu.VMEM((blocks, width, STEP), bf16),
-            pltpu.SemaphoreType.DMA((2,)),
+            pltpu.SemaphoreType.DMA((1,)),
             pltpu.SemaphoreType.DMA((blocks,)),
         ],
         limit=REST_VMEM,
     )
     answers, own_value = score_call(
         score_last,
-        (scaled, near, own_w, heads, sib_w, sib_h, far_sib_w, far_h),
+        (scaled, near, own_scaled, own_near, own_w, heads, sib_w, sib_h, far_w, far_sib_w, far_h),
         [shape((n_agents, 2), f32), shape((1, rows_dev), f32)],
         0,
-        hbm=(2, 4, 6),
+        hbm=(6, 8, 9),
         scratch=[
-            pltpu.VMEM((visits + rows_dev, 1), f32),
+            pltpu.VMEM((visits, 1), f32),
             pltpu.VMEM((3 * blocks, width, STEP), bf16),
             pltpu.SemaphoreType.DMA((3 * blocks,)),
         ],

time: 99.9 us -> 98.2 us (0.983)
  Pallas kernels: 15.6 us -> 13.6 us
  blocking collectives: 29.9 us -> 31.6 us
    pallas_call x3, Pallas kernels: 11.6 us -> 9.63 us  [score_call(): pl.pallas_call(body, in_specs=[anywhere if i in hbm else vmem for i in ra...]
    all_to_all x1, blocking collectives: 29.9 us -> 31.6 us  [per_device(): lax.all_to_all(answers, exchange, 0, 0, axis_index_groups=groups, tiled=T...]
    unnamed x10 -> x12, local copies, waits for them, and re-layouts: 2.09 us -> 1.75 us
  transfers between devices with their start and end apart: 6 -> 6, of which waited for: 3 -> 3; matrix products, arithmetic and copies ran while one was open for 1% -> 0% of each run, Pallas kernels for 7% -> 7%
where the time goes in v6:
time: 98.2 us; the launch traced here: 97.6 us
  starting transfers between devices  39.2 us (40%)
  blocking collectives  31.6 us (32%)
  Pallas kernels  13.6 us (14%)
  waiting for transfers between devices  10.7 us (11%)
  local copies, waits for them, and re-layouts  1.75 us (2%)
    all_to_all x1, blocking collectives, per_device(): lax.all_to_all(answers, exchange, 0, 0, axis_index_groups=groups, tiled=T...  31.6 us
    all_to_all x1, starting transfers between devices, per_device(): lax.all_to_all(outgoing, exchange, 0, 0, axis_index_groups=groups, tiled=...  19.2 us
    pallas_call x3, Pallas kernels, score_call(): pl.pallas_call(body, in_specs=[anywhere if i in hbm else vmem for i in ra...  9.63 us
    ppermute x1, starting transfers between devices, per_device(): far_sib_w = lax.ppermute(far_w, 'c', SWAP)  8.16 us
    ppermute x1, waiting for transfers between devices, per_device(): far_h = lax.ppermute(jnp.concatenate([heads, sib_h], axis=0), 'xl', SWAP)  7.11 us
    ppermute x1, starting transfers between devices, per_device(): far_w = lax.ppermute(own_w, 'xl', SWAP)  3.95 us
    ppermute x1, starting transfers between devices, per_device(): sib_h = lax.ppermute(near_h, 'c', SWAP)  3.14 us
    all_to_all x1, waiting for transfers between devices, per_device(): lax.all_to_all(outgoing, exchange, 0, 0, axis_index_groups=groups, tiled=...  2.81 us
  transfers between devices with their start and end apart: 6, of which 3 were waited for; matrix products, arithmetic and copies ran while one was open for 0% of the time, Pallas kernels for 7%

profile of v6, /device:TPU:1, one launch (start us, length us, event | category | flops | bytes accessed | tf_op | source)
XLA Modules:
  0.0 97.6 jit_solution(9254578842873255846)
XLA Ops:
  0.6 4.0 %collective-permute-start = (bf16[2048,512]{1,0:T(8,128)(2,1)}, bf16[2048,512]{1,0:T(8,128)(2,1)}, u32[]{:S(2)}, u32[]{:S(2)}) collective-permute-start(bf16[2048,512]{1,0:T(8,128)(2,1)} %bitcast.9), channel_id=1, source_target_pairs={{0,2},{2,0},{1,3},{3,1},{4,6},{6,4},{5,7},{7,5},{8,10},{10,8},{9,1... | collective-permute-start | bytes 6291464 | tf_op jit(solution)/shard_map/ppermute | solution.py:191
  4.6 2.5 %fill_slots.1 = (bf16[128,2,2048]{2,1,0:T(2,128)(2,1)}, s32[1,128]{1,0:T(1,128)}) custom-call(s32[1,128]{1,0:T(1,128)} %bitcast.15, s32[1,128]{1,0:T(1,128)} %bitcast.18, bf16[128,2048]{1,0:T(8,128)(2,1)} %x_ref.1), custom_call_target="tpu_custom_call" | custom-call | flops 199999995904 | tf_op jit(solution)/shard_map/fill_slots/pallas_call | solution.py:64
  7.1 0.0 copy-start.3
  7.1 0.0 copy-start
  7.2 19.2 %all-to-all-start = ((bf16[128,2,2048]{2,1,0:T(2,128)(2,1)}), bf16[128,2,2048]{2,1,0:T(2,128)(2,1)S(1)}, u32[]{:S(2)}, u32[]{:S(2)}) async-start(bf16[128,2,2048]{2,1,0:T(2,128)(2,1)} %get-tuple-element.17), calls=%async_computation | async-start | bytes 2097152 | tf_op jit(solution)/shard_map/all_to_all | solution.py:195
  26.4 0.0 copy-done.3
  26.4 3.1 %collective-permute-start.1 = (bf16[1,512]{1,0:T(2,128)(2,1)S(1)}, bf16[1,512]{1,0:T(2,128)(2,1)S(1)}, u32[]{:S(2)}, u32[]{:S(2)}) collective-permute-start(bf16[1,512]{1,0:T(2,128)(2,1)S(1)} %copy-done.3), channel_id=1, source_target_pairs={{0,1},{1,0},{2,3},{3,2},{4,5},{5,4},{6,7},{7,6},{8,9},{9,8},{10,11... | collective-permute-start | bytes 3080 | tf_op jit(solution)/shard_map/ppermute | solution.py:196
  29.5 0.8 collective-permute-done.1.h1_ref
  30.3 2.2 %collective-permute-start.2 = (bf16[2,512]{1,0:T(2,128)(2,1)S(1)}, bf16[2,512]{1,0:T(2,128)(2,1)S(1)}, u32[]{:S(2)}, u32[]{:S(2)}) collective-permute-start(bf16[2,512]{1,0:T(2,128)(2,1)S(1)} %pad_maximum_fusion), channel_id=1, source_target_pairs={{0,2},{2,0},{1,3},{3,1},{4,6},{6,4},{5,7},{7,5},{8,10},{10,8},{9,1... | collective-permute-start | bytes 6152 | tf_op jit(solution)/shard_map/ppermute | solution.py:199
  32.6 0.0 copy-done
  32.6 0.0 copy-start.2
  32.6 1.0 %copy-done.2 = bf16[128,2048]{1,0:T(8,128)(2,1)S(1)} copy-done((bf16[128,2048]{1,0:T(8,128)(2,1)S(1)}, bf16[128,2048]{1,0:T(8,128)(2,1)}, u32[]{:S(2)}) %copy-start.2) | copy-done | bytes 524312
  33.6 0.0 copy-start.4
  33.6 0.7 copy-done.4
  34.3 0.0 copy-start.5
  34.3 1.3 %score_own.1 = (bf16[128,2048]{1,0:T(8,128)(2,1)}, f32[128,1]{1,0:T(8,128)S(1)}) custom-call(bf16[128,2048]{1,0:T(8,128)(2,1)S(1)} %copy-done.2, f32[1,2048]{1,0:T(1,128)S(1)} %copy-done.4, bf16[2048,512]{1,0:T(8,128)(2,1)S(1)} %bitcast.10, bf16[1,512]{1,0:T(2,128)(2,1)S(1)} %copy-done.3), custom_call_target="tpu_custom_call" | custom-call | tf_op jit(solution)/shard_map/score_own/pallas_call | solution.py:173
  35.6 2.5 %collective-permute-start.3 = (bf16[2048,512]{1,0:T(8,128)(2,1)S(1)}, bf16[2048,512]{1,0:T(8,128)(2,1)}, u32[]{:S(2)}, u32[]{:S(2)}) collective-permute-start(bf16[2048,512]{1,0:T(8,128)(2,1)S(1)} %bitcast.11), channel_id=1, source_target_pairs={{0,1},{1,0},{2,3},{3,2},{4,5},{5,4},{6,7},{7,6},{8,9},{9,8},{10,11... | collective-permute-start | bytes 6291464 | tf_op jit(solution)/shard_map/ppermute | solution.py:198
  38.1 7.1 %collective-permute-done.2.h_ref.h23_ref = bf16[2,512]{1,0:T(2,128)(2,1)S(1)} collective-permute-done((bf16[2,512]{1,0:T(2,128)(2,1)S(1)}, bf16[2,512]{1,0:T(2,128)(2,1)S(1)}, u32[]{:S(2)}, u32[]{:S(2)}) %collective-permute-start.2) | collective-permute-done | bytes 2080 | tf_op jit(solution)/shard_map/ppermute | solution.py:199
  45.2 0.0 collective-permute-done.w_hbm.w2_hbm
  45.2 8.2 %collective-permute-start.4 = (bf16[2048,512]{1,0:T(8,128)(2,1)}, bf16[2048,512]{1,0:T(8,128)(2,1)}, u32[]{:S(2)}, u32[]{:S(2)}) collective-permute-start(bf16[2048,512]{1,0:T(8,128)(2,1)} %collective-permute-done.w_hbm.w2_hbm), channel_id=1, source_target_pairs={{0,1},{1,0},{2,3},{3,2},{4,5},{5,4},{6,7},{7,6},{8,9},{9,8},{10,11... | collective-permute-start | bytes 6291464 | tf_op jit(solution)/shard_map/ppermute | solution.py:210
  53.4 2.8 %all-to-all-done.x_hbm = bf16[128,2,2048]{2,1,0:T(2,128)(2,1)S(1)} async-done(((bf16[128,2,2048]{2,1,0:T(2,128)(2,1)}), bf16[128,2,2048]{2,1,0:T(2,128)(2,1)S(1)}, u32[]{:S(2)}, u32[]{:S(2)}) %all-to-all-start) | async-done | bytes 1048608 | tf_op jit(solution)/shard_map/all_to_all | solution.py:195
  56.2 0.0 copy-done.5
  56.2 0.0 copy-start.1
  56.2 2.6 %score_first.1 = (bf16[256,2048]{1,0:T(8,128)(2,1)S(1)}, f32[256,1]{1,0:T(8,128)S(1)}) custom-call(bf16[128,2,2048]{2,1,0:T(2,128)(2,1)S(1)} %all-to-all-done.x_hbm, f32[1,2048]{1,0:T(1,128)S(1)} %copy-done.5, bf16[2048,512]{1,0:T(8,128)(2,1)} %collective-permute-done.w_hbm.w2_hbm, bf16[2,512]{1,0:T(2,128)(2,1)S(1)} %collective-permute-done.2.h_ref.h23_ref), custom_call_target="tpu_custom_call" | custom-call | flops 5000000000 | tf_op jit(solution)/shard_map/score_first/pallas_call | solution.py:173
  58.8 0.0 collective-permute-done.3.w1_hbm
  58.8 0.0 collective-permute-done.4.w3_hbm
  58.8 0.0 copy-done.1
  58.8 5.8 %score_last.1 = (f32[128,2]{1,0:T(8,128)S(1)}, f32[1,128]{1,0:T(1,128)}) custom-call(bf16[256,2048]{1,0:T(8,128)(2,1)S(1)} %get-tuple-element.24.visit_ref, f32[256,1]{1,0:T(8,128)S(1)} %get-tuple-element.25.visit_near_ref, bf16[128,2048]{1,0:T(8,128)(2,1)S(1)} %copy-done.1, f32[128,1]{1,0:T(8,128)S(1)} %get-tuple-element.27.own_near_ref, ...), custom_call_target="tpu_custom_call" | custom-call | tf_op jit(solution)/shard_map/score_last/pallas_call | solution.py:173
  64.6 31.6 %all_to_all.16 = f32[128,1,2]{2,1,0:T(1,128)} all-to-all(f32[128,1,2]{2,1,0:T(1,128)S(1)} %bitcast.13), channel_id=1, replica_groups={{0,4,8,12,16,20,24,28,34,38,42,46,50,54,58,62,64,68,72,76,80,84,88,92,9..., dimensions={0} | all-to-all | bytes 2048 | tf_op jit(solution)/shard_map/all_to_all | solution.py:239
  96.2 1.5 %pick_answers.1 = f32[1,128]{1,0:T(1,128)} custom-call(f32[128,2]{1,0:T(8,128)} %bitcast.14, s32[1,128]{1,0:T(1,128)} %bitcast.16, s32[1,128]{1,0:T(1,128)} %get-tuple-element.31.slot_ref), custom_call_target="tpu_custom_call" | custom-call | tf_op jit(solution)/shard_map/pick_answers/pallas_call | solution.py:93
  (1 shorter events, 0.0 us)
Async XLA Ops:
  0.6 44.6 %collective-permute-start = (bf16[2048,512]{1,0:T(8,128)(2,1)}, bf16[2048,512]{1,0:T(8,128)(2,1)}, u32[]{:S(2)}, u32[]{:S(2)}) collective-permute-start(bf16[2048,512]{1,0:T(8,128)(2,1)} %bitcast.9), channel_id=1, source_target_pairs={{0,2},{2,0},{1,3},{3,1},{4,6},{6,4},{5,7},{7,5},{8,10},{10,8},{9,1... | collective-permute-start | bytes 6291464 | tf_op jit(solution)/shard_map/ppermute | solution.py:191
  7.1 19.2 %copy-start.3 = (bf16[1,512]{1,0:T(2,128)(2,1)S(1)}, bf16[1,512]{1,0:T(2,128)(2,1)}, u32[]{:S(2)}) copy-start(bf16[1,512]{1,0:T(2,128)(2,1)} %h0_ref.1) | copy-start | bytes 3076
  7.1 25.4 %copy-start = (bf16[1,2048,512]{2,1,0:T(8,128)(2,1)S(1)}, bf16[1,2048,512]{2,1,0:T(8,128)(2,1)}, u32[]{:S(2)}) copy-start(bf16[1,2048,512]{2,1,0:T(8,128)(2,1)} %param.7) | copy-start | bytes 6291460
  7.2 49.1 %all-to-all-start = ((bf16[128,2,2048]{2,1,0:T(2,128)(2,1)}), bf16[128,2,2048]{2,1,0:T(2,128)(2,1)S(1)}, u32[]{:S(2)}, u32[]{:S(2)}) async-start(bf16[128,2,2048]{2,1,0:T(2,128)(2,1)} %get-tuple-element.17), calls=%async_computation | async-start | bytes 2097152 | tf_op jit(solution)/shard_map/all_to_all | solution.py:195
  26.4 3.9 %collective-permute-start.1 = (bf16[1,512]{1,0:T(2,128)(2,1)S(1)}, bf16[1,512]{1,0:T(2,128)(2,1)S(1)}, u32[]{:S(2)}, u32[]{:S(2)}) collective-permute-start(bf16[1,512]{1,0:T(2,128)(2,1)S(1)} %copy-done.3), channel_id=1, source_target_pairs={{0,1},{1,0},{2,3},{3,2},{4,5},{5,4},{6,7},{7,6},{8,9},{9,8},{10,11... | collective-permute-start | bytes 3080 | tf_op jit(solution)/shard_map/ppermute | solution.py:196
  30.3 14.9 %collective-permute-start.2 = (bf16[2,512]{1,0:T(2,128)(2,1)S(1)}, bf16[2,512]{1,0:T(2,128)(2,1)S(1)}, u32[]{:S(2)}, u32[]{:S(2)}) collective-permute-start(bf16[2,512]{1,0:T(2,128)(2,1)S(1)} %pad_maximum_fusion), channel_id=1, source_target_pairs={{0,2},{2,0},{1,3},{3,1},{4,6},{6,4},{5,7},{7,5},{8,10},{10,8},{9,1... | collective-permute-start | bytes 6152 | tf_op jit(solution)/shard_map/ppermute | solution.py:199
  32.6 1.0 %copy-start.2 = (bf16[128,2048]{1,0:T(8,128)(2,1)S(1)}, bf16[128,2048]{1,0:T(8,128)(2,1)}, u32[]{:S(2)}) copy-start(bf16[128,2048]{1,0:T(8,128)(2,1)} %x_ref.1) | copy-start | bytes 1572868
  33.6 0.7 copy-start.4
  34.3 21.9 %copy-start.5 = (f32[1,2048]{1,0:T(1,128)S(1)}, f32[1,2048]{1,0:T(1,128)}, u32[]{:S(2)}) copy-start(f32[1,2048]{1,0:T(1,128)} %gain_ref.3) | copy-start | bytes 24580
  35.6 23.2 %collective-permute-start.3 = (bf16[2048,512]{1,0:T(8,128)(2,1)S(1)}, bf16[2048,512]{1,0:T(8,128)(2,1)}, u32[]{:S(2)}, u32[]{:S(2)}) collective-permute-start(bf16[2048,512]{1,0:T(8,128)(2,1)S(1)} %bitcast.11), channel_id=1, source_target_pairs={{0,1},{1,0},{2,3},{3,2},{4,5},{5,4},{6,7},{7,6},{8,9},{9,8},{10,11... | collective-permute-start | bytes 6291464 | tf_op jit(solution)/shard_map/ppermute | solution.py:198
  45.2 13.6 %collective-permute-start.4 = (bf16[2048,512]{1,0:T(8,128)(2,1)}, bf16[2048,512]{1,0:T(8,128)(2,1)}, u32[]{:S(2)}, u32[]{:S(2)}) collective-permute-start(bf16[2048,512]{1,0:T(8,128)(2,1)} %collective-permute-done.w_hbm.w2_hbm), channel_id=1, source_target_pairs={{0,1},{1,0},{2,3},{3,2},{4,5},{5,4},{6,7},{7,6},{8,9},{9,8},{10,11... | collective-permute-start | bytes 6291464 | tf_op jit(solution)/shard_map/ppermute | solution.py:210
  56.2 2.6 %copy-start.1 = (bf16[128,2048]{1,0:T(8,128)(2,1)S(1)}, bf16[128,2048]{1,0:T(8,128)(2,1)}, u32[]{:S(2)}) copy-start(bf16[128,2048]{1,0:T(8,128)(2,1)} %get-tuple-element.26.own_ref) | copy-start | bytes 1572868

commit v7 on v6

--- a/solution.py
+++ b/solution.py
@@ -11,6 +11,7 @@
 AXES = ("z", "xh", "y", "xl", "c")
 SWAP = [(0, 1), (1, 0)]
 COST_FIRST = 5
+COST_OWN = 5
 SLOTS_VMEM = 60 * 1024 * 1024
 SCORE_VMEM = 16 * 1024 * 1024
 REST_VMEM = 32 * 1024 * 1024
@@ -93,6 +94,7 @@
     return pl.pallas_call(
         pick_answers,
         out_shape=jax.ShapeDtypeStruct(owner.shape, jnp.float32),
+        compiler_params=pltpu.CompilerParams(vmem_limit_bytes=SCORE_VMEM),
         cost_estimate=hint(0),
         name="pick_answers",
     )(returned, owner, slot)
@@ -121,51 +123,51 @@
     return jobs
 
 
+def add_blocks(total, rows_ref, jobs, blocks_ref, heads):
+    for i, (copy, n, start) in enumerate(jobs):
+        copy.wait()
+        total += values(rows_ref[...], blocks_ref[i], heads[n][:, start : start + STEP])
+    return total
+
+
 def score_own(x_ref, gain_ref, w_ref, h_ref, scaled_ref, value_ref):
     rows = scaled_rows(x_ref[...], gain_ref[...])
     scaled_ref[...] = rows
     value_ref[...] = values(rows, w_ref[...], h_ref[...].astype(jnp.float32))
 
 
-def score_first(x_hbm, gain_ref, w_hbm, h_ref, scaled_ref, value_ref, x_ref, blocks_ref, rows_here, arrived):
+def score_first(
+    x_hbm, gain_ref, w0_ref, h0_ref, w1_hbm, h1_ref, scaled_ref, value_ref, x_ref, blocks_ref, rows_here, arrived
+):
     agents, slots, _ = x_ref.shape
     visit_copy = pltpu.make_async_copy(x_hbm, x_ref, rows_here.at[0])
     visit_copy.start()
-    jobs = fetch_blocks((w_hbm,), blocks_ref, arrived)
+    jobs = fetch_blocks((w1_hbm,), blocks_ref, arrived)
     gain = gain_ref[...]
-    head = h_ref[...].astype(jnp.float32)[0:1]
     visit_copy.wait()
     for start in range(0, agents, SCALE_AGENTS):
         rows = x_ref[start : start + SCALE_AGENTS].reshape(SCALE_AGENTS * slots, gain.shape[1])
         scaled_ref[start * slots : (start + SCALE_AGENTS) * slots, :] = scaled_rows(rows, gain)
-    total = jnp.zeros(value_ref.shape, jnp.float32)
-    for i, (copy, _, start) in enumerate(jobs):
-        copy.wait()
-        total += values(scaled_ref[...], blocks_ref[i], head[:, start : start + STEP])
-    value_ref[...] = total
-
-
-def score_last(
-    visit_ref, visit_near_ref, own_ref, own_near_ref, w0_ref, h0_ref, w1_hbm, h1_ref, w2_hbm, w3_hbm, h23_ref,
-    answer_out, value_out, total_ref, blocks_ref, arrived,
-):
-    jobs = fetch_blocks((w2_hbm, w1_hbm, w3_hbm), blocks_ref, arrived)
-    far_heads = h23_ref[...].astype(jnp.float32)
-    heads = (far_heads[0:1], h1_ref[...].astype(jnp.float32), far_heads[1:2])
-    visit = visit_near_ref[...] + values(visit_ref[...], w0_ref[...], h0_ref[...].astype(jnp.float32))
-    own = own_near_ref[...]
-    for i, (copy, n, start) in enumerate(jobs):
-        copy.wait()
-        head = heads[n][:, start : start + STEP]
-        own += values(own_ref[...], blocks_ref[i], head)
-        if n > 0:
-            visit += values(visit_ref[...], blocks_ref[i], head)
-    total_ref[...] = visit
+    total = values(scaled_ref[...], w0_ref[...], h0_ref[...].astype(jnp.float32))
+    value_ref[...] = add_blocks(total, scaled_ref, jobs, blocks_ref, (h1_ref[...].astype(jnp.float32)[0:1],))
+
+
+def score_last(scaled_ref, near_ref, w0_hbm, h0_ref, w1_hbm, h1_ref, answer_out, total_ref, blocks_ref, arrived):
+    jobs = fetch_blocks((w0_hbm, w1_hbm), blocks_ref, arrived)
+    heads = (h0_ref[...].astype(jnp.float32), h1_ref[...].astype(jnp.float32)[1:2])
+    total_ref[...] = add_blocks(near_ref[...], scaled_ref, jobs, blocks_ref, heads)
     agents, slots = answer_out.shape
     for k in range(slots):
         answer_out[:, k : k + 1] = total_ref[pl.ds(k, agents, stride=slots), :]
+
+
+def score_own_rest(scaled_ref, near_ref, w0_hbm, h0_ref, w1_hbm, w2_hbm, h12_ref, value_out, blocks_ref, arrived):
+    jobs = fetch_blocks((w0_hbm, w1_hbm, w2_hbm), blocks_ref, arrived)
+    far_heads = h12_ref[...].astype(jnp.float32)
+    heads = (h0_ref[...].astype(jnp.float32), far_heads[0:1], far_heads[1:2])
+    total = add_blocks(near_ref[...], scaled_ref, jobs, blocks_ref, heads)
     owns = value_out.shape[1]
-    value_out[...] = jnp.broadcast_to(own, (owns, owns)).T[0:1]
+    value_out[...] = jnp.broadcast_to(total, (owns, owns)).T[0:1]
 
 
 def score_call(body, operands, outs, weight, hbm=(), scratch=(), limit=0):
@@ -209,35 +211,40 @@
     far_w, far_h, own_scaled = lax.optimization_barrier((far_w, far_h, own_scaled))
     far_sib_w = lax.ppermute(far_w, "c", SWAP)
     blocks = units // STEP
+
+    def copied(count):
+        return [pltpu.VMEM((count * blocks, width, STEP), bf16), pltpu.SemaphoreType.DMA((count * blocks,))]
+
+    fetched, here = copied(1)
     scaled, near = score_call(
         score_first,
-        (received, gains, far_w, far_h),
+        (received, gains, own_w, heads, far_w, far_h),
         [shape((visits, width), bf16), shape((visits, 1), f32)],
         COST_FIRST,
-        hbm=(0, 2),
-        scratch=[
-            pltpu.VMEM(received.shape, bf16),
-            pltpu.VMEM((blocks, width, STEP), bf16),
-            pltpu.SemaphoreType.DMA((1,)),
-            pltpu.SemaphoreType.DMA((blocks,)),
-        ],
+        hbm=(0, 4),
+        scratch=[pltpu.VMEM(received.shape, bf16), fetched, pltpu.SemaphoreType.DMA((1,)), here],
         limit=REST_VMEM,
     )
-    answers, own_value = score_call(
+    answers = score_call(
         score_last,
-        (scaled, near, own_scaled, own_near, own_w, heads, sib_w, sib_h, far_w, far_sib_w, far_h),
-        [shape((n_agents, 2), f32), shape((1, rows_dev), f32)],
+        (scaled, near, sib_w, sib_h, far_sib_w, far_h),
+        shape((n_agents, 2), f32),
         0,
-        hbm=(6, 8, 9),
-        scratch=[
-            pltpu.VMEM((visits, 1), f32),
-            pltpu.VMEM((3 * blocks, width, STEP), bf16),
-            pltpu.SemaphoreType.DMA((3 * blocks,)),
-        ],
+        hbm=(2, 4),
+        scratch=[pltpu.VMEM((visits, 1), f32)] + copied(2),
         limit=REST_VMEM,
     )
     returned = lax.all_to_all(answers, exchange, 0, 0, axis_index_groups=groups, tiled=True)
-
+    own_scaled, answers = lax.optimization_barrier((own_scaled, answers))
+    own_value = score_call(
+        score_own_rest,
+        (own_scaled, own_near, sib_w, sib_h, far_w, far_sib_w, far_h),
+        shape((1, rows_dev), f32),
+        COST_OWN,
+        hbm=(2, 4, 5),
+        scratch=copied(3),
+        limit=REST_VMEM,
+    )
     opponent_value = pick_call(returned, owner, slot)
     return own_value.reshape(rows_dev), opponent_value.reshape(rows_dev)
 

time: 98.2 us -> 95.4 us (0.971)
  blocking collectives: 31.6 us -> 0 us
  starting transfers between devices: 39.2 us -> 57.9 us
  waiting for transfers between devices: 10.7 us -> 18.6 us
  Pallas kernels: 13.6 us -> 15.1 us
    all_to_all x1 -> x0, blocking collectives: 31.6 us -> none  [per_device(): lax.all_to_all(answers, exchange, 0, 0, axis_index_groups=groups, tiled=T...]
    all_to_all x0 -> x1, starting transfers between devices: none -> 18.7 us  [per_device(): lax.all_to_all(answers, exchange, 0, 0, axis_index_groups=groups, tiled=T...]
    all_to_all x0 -> x1, waiting for transfers between devices: none -> 8.56 us  [per_device(): lax.all_to_all(answers, exchange, 0, 0, axis_index_groups=groups, tiled=T...]
    pallas_call x3 -> x4, Pallas kernels: 9.63 us -> 12 us  [score_call(): pl.pallas_call(body, in_specs=[anywhere if i in hbm else vmem for i in ra...]
  transfers between devices with their start and end apart: 6 -> 7, of which waited for: 3 -> 4; matrix products, arithmetic and copies ran while one was open for 0% -> 1% of each run, Pallas kernels for 7% -> 11%
where the time goes in v7:
time: 95.4 us; the launch traced here: 94.9 us
  starting transfers between devices  57.9 us (61%)
  waiting for transfers between devices  18.6 us (19%)
  Pallas kernels  15.1 us (16%)
  local copies, waits for them, and re-layouts  1.75 us (2%)
    all_to_all x1, starting transfers between devices, per_device(): lax.all_to_all(outgoing, exchange, 0, 0, axis_index_groups=groups, tiled=...  19.2 us
    all_to_all x1, starting transfers between devices, per_device(): lax.all_to_all(answers, exchange, 0, 0, axis_index_groups=groups, tiled=T...  18.7 us
    pallas_call x4, Pallas kernels, score_call(): pl.pallas_call(body, in_specs=[anywhere if i in hbm else vmem for i in ra...  12 us
    all_to_all x1, waiting for transfers between devices, per_device(): lax.all_to_all(answers, exchange, 0, 0, axis_index_groups=groups, tiled=T...  8.56 us
    ppermute x1, starting transfers between devices, per_device(): far_sib_w = lax.ppermute(far_w, 'c', SWAP)  8.16 us
    ppermute x1, waiting for transfers between devices, per_device(): far_h = lax.ppermute(jnp.concatenate([heads, sib_h], axis=0), 'xl', SWAP)  6.26 us
    ppermute x1, starting transfers between devices, per_device(): far_w = lax.ppermute(own_w, 'xl', SWAP)  3.95 us
    ppermute x1, starting transfers between devices, per_device(): sib_h = lax.ppermute(near_h, 'c', SWAP)  3.14 us
  transfers between devices with their start and end apart: 7, of which 4 were waited for; matrix products, arithmetic and copies ran while one was open for 1% of the time, Pallas kernels for 11%

profile of v7, /device:TPU:1, one launch (start us, length us, event | category | flops | bytes accessed | tf_op | source)
XLA Modules:
  0.0 94.9 jit_solution(17416914119211970000)
XLA Ops:
  0.6 4.0 %collective-permute-start = (bf16[2048,512]{1,0:T(8,128)(2,1)}, bf16[2048,512]{1,0:T(8,128)(2,1)}, u32[]{:S(2)}, u32[]{:S(2)}) collective-permute-start(bf16[2048,512]{1,0:T(8,128)(2,1)} %bitcast.9), channel_id=1, source_target_pairs={{0,2},{2,0},{1,3},{3,1},{4,6},{6,4},{5,7},{7,5},{8,10},{10,8},{9,1... | collective-permute-start | bytes 6291464 | tf_op jit(solution)/shard_map/ppermute | solution.py:193
  4.6 2.5 %fill_slots.1 = (bf16[128,2,2048]{2,1,0:T(2,128)(2,1)}, s32[1,128]{1,0:T(1,128)}) custom-call(s32[1,128]{1,0:T(1,128)} %bitcast.14, s32[1,128]{1,0:T(1,128)} %bitcast.17, bf16[128,2048]{1,0:T(8,128)(2,1)} %x_ref.1), custom_call_target="tpu_custom_call" | custom-call | flops 199999995904 | tf_op jit(solution)/shard_map/fill_slots/pallas_call | solution.py:65
  7.1 0.0 copy-start
  7.1 0.0 copy-start.2
  7.1 19.2 %all-to-all-start = ((bf16[128,2,2048]{2,1,0:T(2,128)(2,1)}), bf16[128,2,2048]{2,1,0:T(2,128)(2,1)S(1)}, u32[]{:S(2)}, u32[]{:S(2)}) async-start(bf16[128,2,2048]{2,1,0:T(2,128)(2,1)} %get-tuple-element.21), calls=%async_computation | async-start | bytes 2097152 | tf_op jit(solution)/shard_map/all_to_all | solution.py:197
  26.3 3.1 %collective-permute-start.1 = (bf16[1,512]{1,0:T(2,128)(2,1)}, bf16[1,512]{1,0:T(2,128)(2,1)S(1)}, u32[]{:S(2)}, u32[]{:S(2)}) collective-permute-start(bf16[1,512]{1,0:T(2,128)(2,1)} %h0_ref.1), channel_id=1, source_target_pairs={{0,1},{1,0},{2,3},{3,2},{4,5},{5,4},{6,7},{7,6},{8,9},{9,8},{10,11... | collective-permute-start | bytes 3080 | tf_op jit(solution)/shard_map/ppermute | solution.py:198
  29.5 1.0 %collective-permute-done.1.h0_ref = bf16[1,512]{1,0:T(2,128)(2,1)S(1)} collective-permute-done((bf16[1,512]{1,0:T(2,128)(2,1)}, bf16[1,512]{1,0:T(2,128)(2,1)S(1)}, u32[]{:S(2)}, u32[]{:S(2)}) %collective-permute-start.1) | collective-permute-done | bytes 1056 | tf_op jit(solution)/shard_map/ppermute | solution.py:198
  30.5 0.7 pad_maximum_fusion
  31.2 2.2 %collective-permute-start.2 = (bf16[2,512]{1,0:T(2,128)(2,1)S(1)}, bf16[2,512]{1,0:T(2,128)(2,1)S(1)}, u32[]{:S(2)}, u32[]{:S(2)}) collective-permute-start(bf16[2,512]{1,0:T(2,128)(2,1)S(1)} %pad_maximum_fusion), channel_id=1, source_target_pairs={{0,2},{2,0},{1,3},{3,1},{4,6},{6,4},{5,7},{7,5},{8,10},{10,8},{9,1... | collective-permute-start | bytes 6152 | tf_op jit(solution)/shard_map/ppermute | solution.py:201
  33.4 0.0 copy-done
  33.4 0.0 copy-done.2
  33.5 0.0 copy-start.1
  33.5 1.0 %copy-done.1 = bf16[128,2048]{1,0:T(8,128)(2,1)S(1)} copy-done((bf16[128,2048]{1,0:T(8,128)(2,1)S(1)}, bf16[128,2048]{1,0:T(8,128)(2,1)}, u32[]{:S(2)}) %copy-start.1) | copy-done | bytes 524312
  34.5 0.0 copy-start.3
  34.5 0.7 copy-done.3
  35.2 0.0 copy-start.4
  35.2 1.3 %score_own.1 = (bf16[128,2048]{1,0:T(8,128)(2,1)}, f32[128,1]{1,0:T(8,128)S(1)}) custom-call(bf16[128,2048]{1,0:T(8,128)(2,1)S(1)} %copy-done.1, f32[1,2048]{1,0:T(1,128)S(1)} %copy-done.2, bf16[2048,512]{1,0:T(8,128)(2,1)S(1)} %bitcast.10, bf16[1,512]{1,0:T(2,128)(2,1)S(1)} %copy-done.3), custom_call_target="tpu_custom_call" | custom-call | tf_op jit(solution)/shard_map/score_own/pallas_call | solution.py:175
  36.5 2.5 %collective-permute-start.3 = (bf16[2048,512]{1,0:T(8,128)(2,1)S(1)}, bf16[2048,512]{1,0:T(8,128)(2,1)}, u32[]{:S(2)}, u32[]{:S(2)}) collective-permute-start(bf16[2048,512]{1,0:T(8,128)(2,1)S(1)} %bitcast.11), channel_id=1, source_target_pairs={{0,1},{1,0},{2,3},{3,2},{4,5},{5,4},{6,7},{7,6},{8,9},{9,8},{10,11... | collective-permute-start | bytes 6291464 | tf_op jit(solution)/shard_map/ppermute | solution.py:200
  39.0 6.3 %collective-permute-done.2.h1_ref.h12_ref = bf16[2,512]{1,0:T(2,128)(2,1)S(1)} collective-permute-done((bf16[2,512]{1,0:T(2,128)(2,1)S(1)}, bf16[2,512]{1,0:T(2,128)(2,1)S(1)}, u32[]{:S(2)}, u32[]{:S(2)}) %collective-permute-start.2) | collective-permute-done | bytes 2080 | tf_op jit(solution)/shard_map/ppermute | solution.py:201
  45.2 0.0 collective-permute-done.w1_hbm
  45.2 8.2 %collective-permute-start.4 = (bf16[2048,512]{1,0:T(8,128)(2,1)}, bf16[2048,512]{1,0:T(8,128)(2,1)}, u32[]{:S(2)}, u32[]{:S(2)}) collective-permute-start(bf16[2048,512]{1,0:T(8,128)(2,1)} %collective-permute-done.w1_hbm), channel_id=1, source_target_pairs={{0,1},{1,0},{2,3},{3,2},{4,5},{5,4},{6,7},{7,6},{8,9},{9,8},{10,11... | collective-permute-start | bytes 6291464 | tf_op jit(solution)/shard_map/ppermute | solution.py:212
  53.4 2.8 %all-to-all-done.x_hbm = bf16[128,2,2048]{2,1,0:T(2,128)(2,1)S(1)} async-done(((bf16[128,2,2048]{2,1,0:T(2,128)(2,1)}), bf16[128,2,2048]{2,1,0:T(2,128)(2,1)S(1)}, u32[]{:S(2)}, u32[]{:S(2)}) %all-to-all-start) | async-done | bytes 1048608 | tf_op jit(solution)/shard_map/all_to_all | solution.py:197
  56.2 0.0 copy-done.4
  56.2 2.5 %score_first.1 = (bf16[256,2048]{1,0:T(8,128)(2,1)S(1)}, f32[256,1]{1,0:T(8,128)S(1)}) custom-call(bf16[128,2,2048]{2,1,0:T(2,128)(2,1)S(1)} %all-to-all-done.x_hbm, f32[1,2048]{1,0:T(1,128)S(1)} %copy-done.2, bf16[2048,512]{1,0:T(8,128)(2,1)S(1)} %bitcast.12, bf16[1,512]{1,0:T(2,128)(2,1)S(1)} %copy-done.4, bf16[2048,512]{1,0:T(8,128)(2,1)} %collective-permute-done.w1_hbm, ...), custom_call_target="tpu_custom_call" | custom-call | flops 5000000000 | tf_op jit(solution)/shard_map/score_first/pallas_call | solution.py:175
  58.8 0.0 collective-permute-done.3.w0_hbm
  58.8 0.0 collective-permute-done.4.w1_hbm.w2_hbm
  58.8 0.0 copy-start.7
  58.8 4.1 %score_last.1 = f32[128,2]{1,0:T(8,128)} custom-call(bf16[256,2048]{1,0:T(8,128)(2,1)S(1)} %get-tuple-element.24.scaled_ref, f32[256,1]{1,0:T(8,128)S(1)} %get-tuple-element.25.near_ref, bf16[2048,512]{1,0:T(8,128)(2,1)} %collective-permute-done.3.w0_hbm, bf16[1,512]{1,0:T(2,128)(2,1)S(1)} %collective-permute-done.1.h0_ref, ...), custom_call_target="tpu_custom_call" | custom-call | tf_op jit(solution)/shard_map/score_last/pallas_call | solution.py:175
  62.9 18.7 %all-to-all-start.1 = ((f32[128,1,2]{2,1,0:T(1,128)}), f32[128,1,2]{2,1,0:T(1,128)S(1)}, u32[]{:S(2)}, u32[]{:S(2)}) async-start(f32[128,1,2]{2,1,0:T(1,128)} %bitcast.5), calls=%async_computation.1 | async-start | bytes 131072 | tf_op jit(solution)/shard_map/all_to_all | solution.py:237
  81.6 0.0 copy-done.7
  81.6 0.0 copy-start.5
  81.6 0.0 copy-start.6
  81.6 4.1 %score_own_rest.1 = f32[1,128]{1,0:T(1,128)} custom-call(bf16[128,2048]{1,0:T(8,128)(2,1)S(1)} %copy-done.7, f32[128,1]{1,0:T(8,128)S(1)} %get-tuple-element.28.near_ref, bf16[2048,512]{1,0:T(8,128)(2,1)} %collective-permute-done.3.w0_hbm, bf16[1,512]{1,0:T(2,128)(2,1)S(1)} %collective-permute-done.1.h0_ref, bf16[2048,512]{1,0:T(8,128)(2,1)} %collective-permute-done.w1_hbm, ...), custom_call_target="tpu_custom_call" | custom-call | flops 5000000000 | tf_op jit(solution)/shard_map/score_own_rest/pallas_call | solution.py:175
  85.7 8.6 %all-to-all-done.1 = f32[128,1,2]{2,1,0:T(1,128)S(1)} async-done(((f32[128,1,2]{2,1,0:T(1,128)}), f32[128,1,2]{2,1,0:T(1,128)S(1)}, u32[]{:S(2)}, u32[]{:S(2)}) %all-to-all-start.1) | async-done | bytes 1056 | tf_op jit(solution)/shard_map/all_to_all | solution.py:237
  94.3 0.0 copy-done.5
  94.3 0.0 copy-done.6
  94.3 0.6 pick_answers.1
Async XLA Ops:
  0.6 44.6 %collective-permute-start = (bf16[2048,512]{1,0:T(8,128)(2,1)}, bf16[2048,512]{1,0:T(8,128)(2,1)}, u32[]{:S(2)}, u32[]{:S(2)}) collective-permute-start(bf16[2048,512]{1,0:T(8,128)(2,1)} %bitcast.9), channel_id=1, source_target_pairs={{0,2},{2,0},{1,3},{3,1},{4,6},{6,4},{5,7},{7,5},{8,10},{10,8},{9,1... | collective-permute-start | bytes 6291464 | tf_op jit(solution)/shard_map/ppermute | solution.py:193
  7.1 26.3 %copy-start = (bf16[1,2048,512]{2,1,0:T(8,128)(2,1)S(1)}, bf16[1,2048,512]{2,1,0:T(8,128)(2,1)}, u32[]{:S(2)}) copy-start(bf16[1,2048,512]{2,1,0:T(8,128)(2,1)} %param.7) | copy-start | bytes 6291460
  7.1 26.3 %copy-start.2 = (f32[1,2048]{1,0:T(1,128)S(1)}, f32[1,2048]{1,0:T(1,128)}, u32[]{:S(2)}) copy-start(f32[1,2048]{1,0:T(1,128)} %gain_ref.3) | copy-start | bytes 24580
  7.1 49.1 %all-to-all-start = ((bf16[128,2,2048]{2,1,0:T(2,128)(2,1)}), bf16[128,2,2048]{2,1,0:T(2,128)(2,1)S(1)}, u32[]{:S(2)}, u32[]{:S(2)}) async-start(bf16[128,2,2048]{2,1,0:T(2,128)(2,1)} %get-tuple-element.21), calls=%async_computation | async-start | bytes 2097152 | tf_op jit(solution)/shard_map/all_to_all | solution.py:197
  26.3 4.2 %collective-permute-start.1 = (bf16[1,512]{1,0:T(2,128)(2,1)}, bf16[1,512]{1,0:T(2,128)(2,1)S(1)}, u32[]{:S(2)}, u32[]{:S(2)}) collective-permute-start(bf16[1,512]{1,0:T(2,128)(2,1)} %h0_ref.1), channel_id=1, source_target_pairs={{0,1},{1,0},{2,3},{3,2},{4,5},{5,4},{6,7},{7,6},{8,9},{9,8},{10,11... | collective-permute-start | bytes 3080 | tf_op jit(solution)/shard_map/ppermute | solution.py:198
  31.2 14.0 %collective-permute-start.2 = (bf16[2,512]{1,0:T(2,128)(2,1)S(1)}, bf16[2,512]{1,0:T(2,128)(2,1)S(1)}, u32[]{:S(2)}, u32[]{:S(2)}) collective-permute-start(bf16[2,512]{1,0:T(2,128)(2,1)S(1)} %pad_maximum_fusion), channel_id=1, source_target_pairs={{0,2},{2,0},{1,3},{3,1},{4,6},{6,4},{5,7},{7,5},{8,10},{10,8},{9,1... | collective-permute-start | bytes 6152 | tf_op jit(solution)/shard_map/ppermute | solution.py:201
  33.5 1.0 %copy-start.1 = (bf16[128,2048]{1,0:T(8,128)(2,1)S(1)}, bf16[128,2048]{1,0:T(8,128)(2,1)}, u32[]{:S(2)}) copy-start(bf16[128,2048]{1,0:T(8,128)(2,1)} %x_ref.1) | copy-start | bytes 1572868
  34.5 0.7 copy-start.3
  35.2 21.0 %copy-start.4 = (bf16[1,512]{1,0:T(2,128)(2,1)S(1)}, bf16[1,512]{1,0:T(2,128)(2,1)}, u32[]{:S(2)}) copy-start(bf16[1,512]{1,0:T(2,128)(2,1)} %h0_ref.1) | copy-start | bytes 3076
  36.5 22.3 %collective-permute-start.3 = (bf16[2048,512]{1,0:T(8,128)(2,1)S(1)}, bf16[2048,512]{1,0:T(8,128)(2,1)}, u32[]{:S(2)}, u32[]{:S(2)}) collective-permute-start(bf16[2048,512]{1,0:T(8,128)(2,1)S(1)} %bitcast.11), channel_id=1, source_target_pairs={{0,1},{1,0},{2,3},{3,2},{4,5},{5,4},{6,7},{7,6},{8,9},{9,8},{10,11... | collective-permute-start | bytes 6291464 | tf_op jit(solution)/shard_map/ppermute | solution.py:200
  45.2 13.5 %collective-permute-start.4 = (bf16[2048,512]{1,0:T(8,128)(2,1)}, bf16[2048,512]{1,0:T(8,128)(2,1)}, u32[]{:S(2)}, u32[]{:S(2)}) collective-permute-start(bf16[2048,512]{1,0:T(8,128)(2,1)} %collective-permute-done.w1_hbm), channel_id=1, source_target_pairs={{0,1},{1,0},{2,3},{3,2},{4,5},{5,4},{6,7},{7,6},{8,9},{9,8},{10,11... | collective-permute-start | bytes 6291464 | tf_op jit(solution)/shard_map/ppermute | solution.py:212
  58.8 22.8 %copy-start.7 = (bf16[128,2048]{1,0:T(8,128)(2,1)S(1)}, bf16[128,2048]{1,0:T(8,128)(2,1)}, u32[]{:S(2)}) copy-start(bf16[128,2048]{1,0:T(8,128)(2,1)} %get-tuple-element.27.scaled_ref) | copy-start | bytes 1572868
  62.9 31.4 %all-to-all-start.1 = ((f32[128,1,2]{2,1,0:T(1,128)}), f32[128,1,2]{2,1,0:T(1,128)S(1)}, u32[]{:S(2)}, u32[]{:S(2)}) async-start(f32[128,1,2]{2,1,0:T(1,128)} %bitcast.5), calls=%async_computation.1 | async-start | bytes 131072 | tf_op jit(solution)/shard_map/all_to_all | solution.py:237
  81.6 12.7 %copy-start.5 = (s32[128,1]{0,1:T(1,128)S(1)}, s32[128,1]{0,1:T(1,128)}, u32[]{:S(2)}) copy-start(s32[128,1]{0,1:T(1,128)} %param.10) | copy-start | bytes 1540
  81.6 12.7 %copy-start.6 = (s32[1,128]{1,0:T(1,128)S(1)}, s32[1,128]{1,0:T(1,128)}, u32[]{:S(2)}) copy-start(s32[1,128]{1,0:T(1,128)} %get-tuple-element.29.slot_ref) | copy-start | bytes 1540

commit v8 on v7

--- a/solution.py
+++ b/solution.py
@@ -152,10 +152,15 @@
     value_ref[...] = add_blocks(total, scaled_ref, jobs, blocks_ref, (h1_ref[...].astype(jnp.float32)[0:1],))
 
 
-def score_last(scaled_ref, near_ref, w0_hbm, h0_ref, w1_hbm, h1_ref, answer_out, total_ref, blocks_ref, arrived):
-    jobs = fetch_blocks((w0_hbm, w1_hbm), blocks_ref, arrived)
-    heads = (h0_ref[...].astype(jnp.float32), h1_ref[...].astype(jnp.float32)[1:2])
-    total_ref[...] = add_blocks(near_ref[...], scaled_ref, jobs, blocks_ref, heads)
+def score_middle(scaled_ref, near_ref, w_hbm, h_ref, value_ref, blocks_ref, arrived):
+    jobs = fetch_blocks((w_hbm,), blocks_ref, arrived)
+    value_ref[...] = add_blocks(near_ref[...], scaled_ref, jobs, blocks_ref, (h_ref[...].astype(jnp.float32),))
+
+
+def score_last(scaled_ref, near_ref, w_hbm, h_ref, answer_out, total_ref, blocks_ref, arrived):
+    jobs = fetch_blocks((w_hbm,), blocks_ref, arrived)
+    head = h_ref[...].astype(jnp.float32)[1:2]
+    total_ref[...] = add_blocks(near_ref[...], scaled_ref, jobs, blocks_ref, (head,))
     agents, slots = answer_out.shape
     for k in range(slots):
         answer_out[:, k : k + 1] = total_ref[pl.ds(k, agents, stride=slots), :]
@@ -225,13 +230,16 @@
         scratch=[pltpu.VMEM(received.shape, bf16), fetched, pltpu.SemaphoreType.DMA((1,)), here],
         limit=REST_VMEM,
     )
+    near = score_call(
+        score_middle, (scaled, near, sib_w, sib_h), shape((visits, 1), f32), 0, hbm=(2,), scratch=copied(1), limit=REST_VMEM
+    )
     answers = score_call(
         score_last,
-        (scaled, near, sib_w, sib_h, far_sib_w, far_h),
+        (scaled, near, far_sib_w, far_h),
         shape((n_agents, 2), f32),
         0,
-        hbm=(2, 4),
-        scratch=[pltpu.VMEM((visits, 1), f32)] + copied(2),
+        hbm=(2,),
+        scratch=[pltpu.VMEM((visits, 1), f32)] + copied(1),
         limit=REST_VMEM,
     )
     returned = lax.all_to_all(answers, exchange, 0, 0, axis_index_groups=groups, tiled=True)

time: 95.4 us -> 95.6 us (level)
  Pallas kernels: 15.1 us -> 16.7 us
  starting transfers between devices: 57.9 us -> 56.4 us
    pallas_call x4 -> x5, Pallas kernels: 12 us -> 13.5 us  [score_call(): pl.pallas_call(body, in_specs=[anywhere if i in hbm else vmem for i in ra...]
    all_to_all x1, starting transfers between devices: 18.7 us -> 17.2 us  [per_device(): lax.all_to_all(answers, exchange, 0, 0, axis_index_groups=groups, tiled=T...]
  transfers between devices with their start and end apart: 7 -> 7, of which waited for: 4 -> 4; matrix products, arithmetic and copies ran while one was open for 1% -> 1% of each run, Pallas kernels for 11% -> 14%
where the time goes in v8:
time: 95.6 us; the launch traced here: 95 us
  starting transfers between devices  56.4 us (59%)
  waiting for transfers between devices  18.6 us (19%)
  Pallas kernels  16.7 us (17%)
  local copies, waits for them, and re-layouts  1.75 us (2%)
    all_to_all x1, starting transfers between devices, per_device(): lax.all_to_all(outgoing, exchange, 0, 0, axis_index_groups=groups, tiled=...  19.2 us
    all_to_all x1, starting transfers between devices, per_device(): lax.all_to_all(answers, exchange, 0, 0, axis_index_groups=groups, tiled=T...  17.2 us
    pallas_call x5, Pallas kernels, score_call(): pl.pallas_call(body, in_specs=[anywhere if i in hbm else vmem for i in ra...  13.5 us
    all_to_all x1, waiting for transfers between devices, per_device(): lax.all_to_all(answers, exchange, 0, 0, axis_index_groups=groups, tiled=T...  8.56 us
    ppermute x1, starting transfers between devices, per_device(): far_sib_w = lax.ppermute(far_w, 'c', SWAP)  8.16 us
    ppermute x1, waiting for transfers between devices, per_device(): far_h = lax.ppermute(jnp.concatenate([heads, sib_h], axis=0), 'xl', SWAP)  6.27 us
    ppermute x1, starting transfers between devices, per_device(): far_w = lax.ppermute(own_w, 'xl', SWAP)  3.95 us
    ppermute x1, starting transfers between devices, per_device(): sib_h = lax.ppermute(near_h, 'c', SWAP)  3.14 us
  transfers between devices with their start and end apart: 7, of which 4 were waited for; matrix products, arithmetic and copies ran while one was open for 1% of the time, Pallas kernels for 14%

profile of v8, /device:TPU:1, one launch (start us, length us, event | category | flops | bytes accessed | tf_op | source)
XLA Modules:
  0.0 95.0 jit_solution(15197910724713099602)
XLA Ops:
  0.6 4.0 %collective-permute-start = (bf16[2048,512]{1,0:T(8,128)(2,1)}, bf16[2048,512]{1,0:T(8,128)(2,1)}, u32[]{:S(2)}, u32[]{:S(2)}) collective-permute-start(bf16[2048,512]{1,0:T(8,128)(2,1)} %bitcast.9), channel_id=1, source_target_pairs={{0,2},{2,0},{1,3},{3,1},{4,6},{6,4},{5,7},{7,5},{8,10},{10,8},{9,1... | collective-permute-start | bytes 6291464 | tf_op jit(solution)/shard_map/ppermute | solution.py:198
  4.6 2.5 %fill_slots.1 = (bf16[128,2,2048]{2,1,0:T(2,128)(2,1)}, s32[1,128]{1,0:T(1,128)}) custom-call(s32[1,128]{1,0:T(1,128)} %bitcast.14, s32[1,128]{1,0:T(1,128)} %bitcast.17, bf16[128,2048]{1,0:T(8,128)(2,1)} %x_ref.1), custom_call_target="tpu_custom_call" | custom-call | flops 199999995904 | tf_op jit(solution)/shard_map/fill_slots/pallas_call | solution.py:65
  7.1 0.0 copy-start
  7.1 0.0 copy-start.2
  7.1 19.2 %all-to-all-start = ((bf16[128,2,2048]{2,1,0:T(2,128)(2,1)}), bf16[128,2,2048]{2,1,0:T(2,128)(2,1)S(1)}, u32[]{:S(2)}, u32[]{:S(2)}) async-start(bf16[128,2,2048]{2,1,0:T(2,128)(2,1)} %get-tuple-element.21), calls=%async_computation | async-start | bytes 2097152 | tf_op jit(solution)/shard_map/all_to_all | solution.py:202
  26.3 3.1 %collective-permute-start.1 = (bf16[1,512]{1,0:T(2,128)(2,1)}, bf16[1,512]{1,0:T(2,128)(2,1)S(1)}, u32[]{:S(2)}, u32[]{:S(2)}) collective-permute-start(bf16[1,512]{1,0:T(2,128)(2,1)} %h0_ref.1), channel_id=1, source_target_pairs={{0,1},{1,0},{2,3},{3,2},{4,5},{5,4},{6,7},{7,6},{8,9},{9,8},{10,11... | collective-permute-start | bytes 3080 | tf_op jit(solution)/shard_map/ppermute | solution.py:203
  29.5 1.0 %collective-permute-done.1.h_ref.h0_ref = bf16[1,512]{1,0:T(2,128)(2,1)S(1)} collective-permute-done((bf16[1,512]{1,0:T(2,128)(2,1)}, bf16[1,512]{1,0:T(2,128)(2,1)S(1)}, u32[]{:S(2)}, u32[]{:S(2)}) %collective-permute-start.1) | collective-permute-done | bytes 1056 | tf_op jit(solution)/shard_map/ppermute | solution.py:203
  30.5 0.7 pad_maximum_fusion
  31.2 2.2 %collective-permute-start.2 = (bf16[2,512]{1,0:T(2,128)(2,1)S(1)}, bf16[2,512]{1,0:T(2,128)(2,1)S(1)}, u32[]{:S(2)}, u32[]{:S(2)}) collective-permute-start(bf16[2,512]{1,0:T(2,128)(2,1)S(1)} %pad_maximum_fusion), channel_id=1, source_target_pairs={{0,2},{2,0},{1,3},{3,1},{4,6},{6,4},{5,7},{7,5},{8,10},{10,8},{9,1... | collective-permute-start | bytes 6152 | tf_op jit(solution)/shard_map/ppermute | solution.py:206
  33.4 0.0 copy-done
  33.4 0.0 copy-done.2
  33.5 0.0 copy-start.1
  33.5 1.0 %copy-done.1 = bf16[128,2048]{1,0:T(8,128)(2,1)S(1)} copy-done((bf16[128,2048]{1,0:T(8,128)(2,1)S(1)}, bf16[128,2048]{1,0:T(8,128)(2,1)}, u32[]{:S(2)}) %copy-start.1) | copy-done | bytes 524312
  34.5 0.0 copy-start.3
  34.5 0.7 copy-done.3
  35.2 0.0 copy-start.4
  35.2 1.3 %score_own.1 = (bf16[128,2048]{1,0:T(8,128)(2,1)}, f32[128,1]{1,0:T(8,128)S(1)}) custom-call(bf16[128,2048]{1,0:T(8,128)(2,1)S(1)} %copy-done.1, f32[1,2048]{1,0:T(1,128)S(1)} %copy-done.2, bf16[2048,512]{1,0:T(8,128)(2,1)S(1)} %bitcast.10, bf16[1,512]{1,0:T(2,128)(2,1)S(1)} %copy-done.3), custom_call_target="tpu_custom_call" | custom-call | tf_op jit(solution)/shard_map/score_own/pallas_call | solution.py:180
  36.4 2.5 %collective-permute-start.3 = (bf16[2048,512]{1,0:T(8,128)(2,1)S(1)}, bf16[2048,512]{1,0:T(8,128)(2,1)}, u32[]{:S(2)}, u32[]{:S(2)}) collective-permute-start(bf16[2048,512]{1,0:T(8,128)(2,1)S(1)} %bitcast.11), channel_id=1, source_target_pairs={{0,1},{1,0},{2,3},{3,2},{4,5},{5,4},{6,7},{7,6},{8,9},{9,8},{10,11... | collective-permute-start | bytes 6291464 | tf_op jit(solution)/shard_map/ppermute | solution.py:205
  39.0 6.3 %collective-permute-done.2.h1_ref.h_ref.h12_ref = bf16[2,512]{1,0:T(2,128)(2,1)S(1)} collective-permute-done((bf16[2,512]{1,0:T(2,128)(2,1)S(1)}, bf16[2,512]{1,0:T(2,128)(2,1)S(1)}, u32[]{:S(2)}, u32[]{:S(2)}) %collective-permute-start.2) | collective-permute-done | bytes 2080 | tf_op jit(solution)/shard_map/ppermute | solution.py:206
  45.2 0.0 collective-permute-done.w1_hbm
  45.2 8.2 %collective-permute-start.4 = (bf16[2048,512]{1,0:T(8,128)(2,1)}, bf16[2048,512]{1,0:T(8,128)(2,1)}, u32[]{:S(2)}, u32[]{:S(2)}) collective-permute-start(bf16[2048,512]{1,0:T(8,128)(2,1)} %collective-permute-done.w1_hbm), channel_id=1, source_target_pairs={{0,1},{1,0},{2,3},{3,2},{4,5},{5,4},{6,7},{7,6},{8,9},{9,8},{10,11... | collective-permute-start | bytes 6291464 | tf_op jit(solution)/shard_map/ppermute | solution.py:217
  53.4 2.8 %all-to-all-done.x_hbm = bf16[128,2,2048]{2,1,0:T(2,128)(2,1)S(1)} async-done(((bf16[128,2,2048]{2,1,0:T(2,128)(2,1)}), bf16[128,2,2048]{2,1,0:T(2,128)(2,1)S(1)}, u32[]{:S(2)}, u32[]{:S(2)}) %all-to-all-start) | async-done | bytes 1048608 | tf_op jit(solution)/shard_map/all_to_all | solution.py:202
  56.2 0.0 copy-done.4
  56.2 2.5 %score_first.1 = (bf16[256,2048]{1,0:T(8,128)(2,1)S(1)}, f32[256,1]{1,0:T(8,128)S(1)}) custom-call(bf16[128,2,2048]{2,1,0:T(2,128)(2,1)S(1)} %all-to-all-done.x_hbm, f32[1,2048]{1,0:T(1,128)S(1)} %copy-done.2, bf16[2048,512]{1,0:T(8,128)(2,1)S(1)} %bitcast.12, bf16[1,512]{1,0:T(2,128)(2,1)S(1)} %copy-done.4, bf16[2048,512]{1,0:T(8,128)(2,1)} %collective-permute-done.w1_hbm, ...), custom_call_target="tpu_custom_call" | custom-call | flops 5000000000 | tf_op jit(solution)/shard_map/score_first/pallas_call | solution.py:180
  58.7 0.0 collective-permute-done.3.w_hbm.w0_hbm
  58.7 2.4 %score_middle.1.near_ref = f32[256,1]{1,0:T(8,128)S(1)} custom-call(bf16[256,2048]{1,0:T(8,128)(2,1)S(1)} %get-tuple-element.24.scaled_ref, f32[256,1]{1,0:T(8,128)S(1)} %get-tuple-element.25.near_ref, bf16[2048,512]{1,0:T(8,128)(2,1)} %collective-permute-done.3.w_hbm.w0_hbm, bf16[1,512]{1,0:T(2,128)(2,1)S(1)} %collective-permute-done.1.h_ref.h0_ref), custom_call_target="tpu_custom_call" | custom-call | tf_op jit(solution)/shard_map/score_middle/pallas_call | solution.py:180
  61.2 0.0 copy-start.7
  61.2 0.0 collective-permute-done.4.w_hbm.w2_hbm
  61.2 3.2 %score_last.1 = f32[128,2]{1,0:T(8,128)} custom-call(bf16[256,2048]{1,0:T(8,128)(2,1)S(1)} %get-tuple-element.24.scaled_ref, f32[256,1]{1,0:T(8,128)S(1)} %score_middle.1.near_ref, bf16[2048,512]{1,0:T(8,128)(2,1)} %collective-permute-done.4.w_hbm.w2_hbm, bf16[2,512]{1,0:T(2,128)(2,1)S(1)} %collective-permute-done.2.h1_ref.h_ref.h12_ref), custom_call_target="tpu_custom_call" | custom-call | tf_op jit(solution)/shard_map/score_last/pallas_call | solution.py:180
  64.4 17.2 %all-to-all-start.1 = ((f32[128,1,2]{2,1,0:T(1,128)}), f32[128,1,2]{2,1,0:T(1,128)S(1)}, u32[]{:S(2)}, u32[]{:S(2)}) async-start(f32[128,1,2]{2,1,0:T(1,128)} %bitcast.5), calls=%async_computation.1 | async-start | bytes 131072 | tf_op jit(solution)/shard_map/all_to_all | solution.py:245
  81.7 0.0 copy-done.7
  81.7 0.0 copy-start.5
  81.7 0.0 copy-start.6
  81.7 4.1 %score_own_rest.1 = f32[1,128]{1,0:T(1,128)} custom-call(bf16[128,2048]{1,0:T(8,128)(2,1)S(1)} %copy-done.7, f32[128,1]{1,0:T(8,128)S(1)} %get-tuple-element.28.near_ref, bf16[2048,512]{1,0:T(8,128)(2,1)} %collective-permute-done.3.w_hbm.w0_hbm, bf16[1,512]{1,0:T(2,128)(2,1)S(1)} %collective-permute-done.1.h_ref.h0_ref, ...), custom_call_target="tpu_custom_call" | custom-call | flops 5000000000 | tf_op jit(solution)/shard_map/score_own_rest/pallas_call | solution.py:180
  85.8 8.6 %all-to-all-done.1 = f32[128,1,2]{2,1,0:T(1,128)S(1)} async-done(((f32[128,1,2]{2,1,0:T(1,128)}), f32[128,1,2]{2,1,0:T(1,128)S(1)}, u32[]{:S(2)}, u32[]{:S(2)}) %all-to-all-start.1) | async-done | bytes 1056 | tf_op jit(solution)/shard_map/all_to_all | solution.py:245
  94.4 0.0 copy-done.5
  94.4 0.0 copy-done.6
  94.4 0.6 pick_answers.1
Async XLA Ops:
  0.6 44.6 %collective-permute-start = (bf16[2048,512]{1,0:T(8,128)(2,1)}, bf16[2048,512]{1,0:T(8,128)(2,1)}, u32[]{:S(2)}, u32[]{:S(2)}) collective-permute-start(bf16[2048,512]{1,0:T(8,128)(2,1)} %bitcast.9), channel_id=1, source_target_pairs={{0,2},{2,0},{1,3},{3,1},{4,6},{6,4},{5,7},{7,5},{8,10},{10,8},{9,1... | collective-permute-start | bytes 6291464 | tf_op jit(solution)/shard_map/ppermute | solution.py:198
  7.1 26.3 %copy-start = (bf16[1,2048,512]{2,1,0:T(8,128)(2,1)S(1)}, bf16[1,2048,512]{2,1,0:T(8,128)(2,1)}, u32[]{:S(2)}) copy-start(bf16[1,2048,512]{2,1,0:T(8,128)(2,1)} %param.7) | copy-start | bytes 6291460
  7.1 26.3 %copy-start.2 = (f32[1,2048]{1,0:T(1,128)S(1)}, f32[1,2048]{1,0:T(1,128)}, u32[]{:S(2)}) copy-start(f32[1,2048]{1,0:T(1,128)} %gain_ref.3) | copy-start | bytes 24580
  7.1 49.1 %all-to-all-start = ((bf16[128,2,2048]{2,1,0:T(2,128)(2,1)}), bf16[128,2,2048]{2,1,0:T(2,128)(2,1)S(1)}, u32[]{:S(2)}, u32[]{:S(2)}) async-start(bf16[128,2,2048]{2,1,0:T(2,128)(2,1)} %get-tuple-element.21), calls=%async_computation | async-start | bytes 2097152 | tf_op jit(solution)/shard_map/all_to_all | solution.py:202
  26.3 4.2 %collective-permute-start.1 = (bf16[1,512]{1,0:T(2,128)(2,1)}, bf16[1,512]{1,0:T(2,128)(2,1)S(1)}, u32[]{:S(2)}, u32[]{:S(2)}) collective-permute-start(bf16[1,512]{1,0:T(2,128)(2,1)} %h0_ref.1), channel_id=1, source_target_pairs={{0,1},{1,0},{2,3},{3,2},{4,5},{5,4},{6,7},{7,6},{8,9},{9,8},{10,11... | collective-permute-start | bytes 3080 | tf_op jit(solution)/shard_map/ppermute | solution.py:203
  31.2 14.0 %collective-permute-start.2 = (bf16[2,512]{1,0:T(2,128)(2,1)S(1)}, bf16[2,512]{1,0:T(2,128)(2,1)S(1)}, u32[]{:S(2)}, u32[]{:S(2)}) collective-permute-start(bf16[2,512]{1,0:T(2,128)(2,1)S(1)} %pad_maximum_fusion), channel_id=1, source_target_pairs={{0,2},{2,0},{1,3},{3,1},{4,6},{6,4},{5,7},{7,5},{8,10},{10,8},{9,1... | collective-permute-start | bytes 6152 | tf_op jit(solution)/shard_map/ppermute | solution.py:206
  33.5 1.0 %copy-start.1 = (bf16[128,2048]{1,0:T(8,128)(2,1)S(1)}, bf16[128,2048]{1,0:T(8,128)(2,1)}, u32[]{:S(2)}) copy-start(bf16[128,2048]{1,0:T(8,128)(2,1)} %x_ref.1) | copy-start | bytes 1572868
  34.5 0.7 copy-start.3
  35.2 21.0 %copy-start.4 = (bf16[1,512]{1,0:T(2,128)(2,1)S(1)}, bf16[1,512]{1,0:T(2,128)(2,1)}, u32[]{:S(2)}) copy-start(bf16[1,512]{1,0:T(2,128)(2,1)} %h0_ref.1) | copy-start | bytes 3076
  36.4 22.3 %collective-permute-start.3 = (bf16[2048,512]{1,0:T(8,128)(2,1)S(1)}, bf16[2048,512]{1,0:T(8,128)(2,1)}, u32[]{:S(2)}, u32[]{:S(2)}) collective-permute-start(bf16[2048,512]{1,0:T(8,128)(2,1)S(1)} %bitcast.11), channel_id=1, source_target_pairs={{0,1},{1,0},{2,3},{3,2},{4,5},{5,4},{6,7},{7,6},{8,9},{9,8},{10,11... | collective-permute-start | bytes 6291464 | tf_op jit(solution)/shard_map/ppermute | solution.py:205
  45.2 16.0 %collective-permute-start.4 = (bf16[2048,512]{1,0:T(8,128)(2,1)}, bf16[2048,512]{1,0:T(8,128)(2,1)}, u32[]{:S(2)}, u32[]{:S(2)}) collective-permute-start(bf16[2048,512]{1,0:T(8,128)(2,1)} %collective-permute-done.w1_hbm), channel_id=1, source_target_pairs={{0,1},{1,0},{2,3},{3,2},{4,5},{5,4},{6,7},{7,6},{8,9},{9,8},{10,11... | collective-permute-start | bytes 6291464 | tf_op jit(solution)/shard_map/ppermute | solution.py:217
  61.2 20.4 %copy-start.7 = (bf16[128,2048]{1,0:T(8,128)(2,1)S(1)}, bf16[128,2048]{1,0:T(8,128)(2,1)}, u32[]{:S(2)}) copy-start(bf16[128,2048]{1,0:T(8,128)(2,1)} %get-tuple-element.27.scaled_ref) | copy-start | bytes 1572868
  64.4 29.9 %all-to-all-start.1 = ((f32[128,1,2]{2,1,0:T(1,128)}), f32[128,1,2]{2,1,0:T(1,128)S(1)}, u32[]{:S(2)}, u32[]{:S(2)}) async-start(f32[128,1,2]{2,1,0:T(1,128)} %bitcast.5), calls=%async_computation.1 | async-start | bytes 131072 | tf_op jit(solution)/shard_map/all_to_all | solution.py:245
  81.7 12.7 %copy-start.5 = (s32[128,1]{0,1:T(1,128)S(1)}, s32[128,1]{0,1:T(1,128)}, u32[]{:S(2)}) copy-start(s32[128,1]{0,1:T(1,128)} %param.10) | copy-start | bytes 1540
  81.7 12.7 %copy-start.6 = (s32[1,128]{1,0:T(1,128)S(1)}, s32[1,128]{1,0:T(1,128)}, u32[]{:S(2)}) copy-start(s32[1,128]{1,0:T(1,128)} %get-tuple-element.29.slot_ref) | copy-start | bytes 1540

commit v9 on v7

--- a/solution.py
+++ b/solution.py
@@ -10,12 +10,11 @@
 NZ, NXH, NY, NXL, NC = 8, 2, 8, 2, 2
 AXES = ("z", "xh", "y", "xl", "c")
 SWAP = [(0, 1), (1, 0)]
-COST_FIRST = 5
+COST_FIRST = 20
 COST_OWN = 5
 SLOTS_VMEM = 60 * 1024 * 1024
 SCORE_VMEM = 16 * 1024 * 1024
 REST_VMEM = 32 * 1024 * 1024
-STEP = 512
 SCALE_AGENTS = 32
 
 
@@ -113,20 +112,24 @@
 
 
 def fetch_blocks(weights, blocks_ref, arrived):
-    jobs = []
-    for n, w_hbm in enumerate(weights):
-        for start in range(0, w_hbm.shape[1], STEP):
-            i = len(jobs)
-            copy = pltpu.make_async_copy(w_hbm.at[:, pl.ds(start, STEP)], blocks_ref.at[i], arrived.at[i])
+    jobs, started = [], 0
+    for i, parts in enumerate(weights):
+        copies, top = [], 0
+        for part in parts:
+            rows = part.shape[0]
+            copy = pltpu.make_async_copy(part, blocks_ref.at[i, pl.ds(top, rows), :], arrived.at[started])
             copy.start()
-            jobs.append((copy, n, start))
+            copies.append(copy)
+            started, top = started + 1, top + rows
+        jobs.append(copies)
     return jobs
 
 
 def add_blocks(total, rows_ref, jobs, blocks_ref, heads):
-    for i, (copy, n, start) in enumerate(jobs):
-        copy.wait()
-        total += values(rows_ref[...], blocks_ref[i], heads[n][:, start : start + STEP])
+    for i, copies in enumerate(jobs):
+        for copy in copies:
+            copy.wait()
+        total += values(rows_ref[...], blocks_ref[i], heads[i])
     return total
 
 
@@ -137,14 +140,11 @@
 
 
 def score_first(
-    x_hbm, gain_ref, w0_ref, h0_ref, w1_hbm, h1_ref, scaled_ref, value_ref, x_ref, blocks_ref, rows_here, arrived
+    x_ref, gain_ref, w0_ref, h0_ref, w1a_hbm, w1b_hbm, h1_ref, scaled_ref, value_ref, blocks_ref, arrived
 ):
     agents, slots, _ = x_ref.shape
-    visit_copy = pltpu.make_async_copy(x_hbm, x_ref, rows_here.at[0])
-    visit_copy.start()
-    jobs = fetch_blocks((w1_hbm,), blocks_ref, arrived)
+    jobs = fetch_blocks(((w1a_hbm, w1b_hbm),), blocks_ref, arrived)
     gain = gain_ref[...]
-    visit_copy.wait()
     for start in range(0, agents, SCALE_AGENTS):
         rows = x_ref[start : start + SCALE_AGENTS].reshape(SCALE_AGENTS * slots, gain.shape[1])
         scaled_ref[start * slots : (start + SCALE_AGENTS) * slots, :] = scaled_rows(rows, gain)
@@ -152,8 +152,8 @@
     value_ref[...] = add_blocks(total, scaled_ref, jobs, blocks_ref, (h1_ref[...].astype(jnp.float32)[0:1],))
 
 
-def score_last(scaled_ref, near_ref, w0_hbm, h0_ref, w1_hbm, h1_ref, answer_out, total_ref, blocks_ref, arrived):
-    jobs = fetch_blocks((w0_hbm, w1_hbm), blocks_ref, arrived)
+def score_last(scaled_ref, near_ref, w0_hbm, h0_ref, w1a_hbm, w1b_hbm, h1_ref, answer_out, total_ref, blocks_ref, arrived):
+    jobs = fetch_blocks(((w0_hbm,), (w1a_hbm, w1b_hbm)), blocks_ref, arrived)
     heads = (h0_ref[...].astype(jnp.float32), h1_ref[...].astype(jnp.float32)[1:2])
     total_ref[...] = add_blocks(near_ref[...], scaled_ref, jobs, blocks_ref, heads)
     agents, slots = answer_out.shape
@@ -161,8 +161,10 @@
         answer_out[:, k : k + 1] = total_ref[pl.ds(k, agents, stride=slots), :]
 
 
-def score_own_rest(scaled_ref, near_ref, w0_hbm, h0_ref, w1_hbm, w2_hbm, h12_ref, value_out, blocks_ref, arrived):
-    jobs = fetch_blocks((w0_hbm, w1_hbm, w2_hbm), blocks_ref, arrived)
+def score_own_rest(
+    scaled_ref, near_ref, w0_hbm, h0_ref, w1a_hbm, w1b_hbm, w2a_hbm, w2b_hbm, h12_ref, value_out, blocks_ref, arrived
+):
+    jobs = fetch_blocks(((w0_hbm,), (w1a_hbm, w1b_hbm), (w2a_hbm, w2b_hbm)), blocks_ref, arrived)
     far_heads = h12_ref[...].astype(jnp.float32)
     heads = (h0_ref[...].astype(jnp.float32), far_heads[0:1], far_heads[1:2])
     total = add_blocks(near_ref[...], scaled_ref, jobs, blocks_ref, heads)
@@ -190,7 +192,10 @@
     own_w = weights[0]
     exchange = ("z", "xh", "y", "xl")
 
-    far_w = lax.ppermute(own_w, "xl", SWAP)
+    half = width // 2
+    far_a = lax.ppermute(own_w[:half], "xl", SWAP)
+    far_b = lax.ppermute(own_w[half:], "xl", SWAP)
+    far_sib_a = lax.ppermute(far_a, "c", SWAP)
     owner = pairing.reshape(1, rows_dev)
     outgoing, slot = slots_call(owner, valid.reshape(1, rows_dev), observations, n_agents)
     near_h, slot = lax.optimization_barrier((heads, slot))
@@ -208,29 +213,27 @@
         [pltpu.HBM((rows_dev, width), bf16), shape((rows_dev, 1), f32)],
         0,
     )
-    far_w, far_h, own_scaled = lax.optimization_barrier((far_w, far_h, own_scaled))
-    far_sib_w = lax.ppermute(far_w, "c", SWAP)
-    blocks = units // STEP
+    far_b, far_sib_a, far_h, own_scaled = lax.optimization_barrier((far_b, far_sib_a, far_h, own_scaled))
+    far_sib_b = lax.ppermute(far_b, "c", SWAP)
 
     def copied(count):
-        return [pltpu.VMEM((count * blocks, width, STEP), bf16), pltpu.SemaphoreType.DMA((count * blocks,))]
-
-    fetched, here = copied(1)
+        return [pltpu.VMEM((count, width, units), bf16), pltpu.SemaphoreType.DMA((2 * count,))]
+
     scaled, near = score_call(
         score_first,
-        (received, gains, own_w, heads, far_w, far_h),
+        (received, gains, own_w, heads, far_a, far_b, far_h),
         [shape((visits, width), bf16), shape((visits, 1), f32)],
         COST_FIRST,
-        hbm=(0, 4),
-        scratch=[pltpu.VMEM(received.shape, bf16), fetched, pltpu.SemaphoreType.DMA((1,)), here],
+        hbm=(4, 5),
+        scratch=copied(1),
         limit=REST_VMEM,
     )
     answers = score_call(
         score_last,
-        (scaled, near, sib_w, sib_h, far_sib_w, far_h),
+        (scaled, near, sib_w, sib_h, far_sib_a, far_sib_b, far_h),
         shape((n_agents, 2), f32),
         0,
-        hbm=(2, 4),
+        hbm=(2, 4, 5),
         scratch=[pltpu.VMEM((visits, 1), f32)] + copied(2),
         limit=REST_VMEM,
     )
@@ -238,10 +241,10 @@
     own_scaled, answers = lax.optimization_barrier((own_scaled, answers))
     own_value = score_call(
         score_own_rest,
-        (own_scaled, own_near, sib_w, sib_h, far_w, far_sib_w, far_h),
+        (own_scaled, own_near, sib_w, sib_h, far_a, far_b, far_sib_a, far_sib_b, far_h),
         shape((1, rows_dev), f32),
         COST_OWN,
-        hbm=(2, 4, 5),
+        hbm=(2, 4, 5, 6, 7),
         scratch=copied(3),
         limit=REST_VMEM,
     )

time: 95.4 us -> 99.2 us (1.040)
  local copies, waits for them, and re-layouts: 1.75 us -> 5.05 us
  Pallas kernels: 15.1 us -> 16.2 us
    slice x0 -> x1, local copies, waits for them, and re-layouts: none -> 3 us  [per_device(): far_a = lax.ppermute(own_w[:half], 'xl', SWAP)]
    all_to_all x1, waiting for transfers between devices: 2.79 us -> 0.01 us  [per_device(): lax.all_to_all(outgoing, exchange, 0, 0, axis_index_groups=groups, tiled=...]
    ppermute x1, waiting for transfers between devices: 6.26 us -> 8.55 us  [per_device(): far_h = lax.ppermute(jnp.concatenate([heads, sib_h], axis=0), 'xl', SWAP)]
    ppermute x2 -> x4, starting transfers between devices: 12.1 us -> 13.6 us  [the longest x1 4.03 us: per_device(): far_sib_b = lax.ppermute(far_b, 'c', SWAP)]
    all_to_all x1, starting transfers between devices: 18.7 us -> 17.3 us  [per_device(): lax.all_to_all(answers, exchange, 0, 0, axis_index_groups=groups, tiled=T...]
    ppermute x1, starting transfers between devices: 3.14 us -> 1.92 us  [per_device(): sib_h = lax.ppermute(near_h, 'c', SWAP)]
    pallas_call x4, Pallas kernels: 12 us -> 13.1 us  [score_call(): pl.pallas_call(body, in_specs=[anywhere if i in hbm else vmem for i in ra...]
    unnamed x16 -> x20, local copies, waits for them, and re-layouts: 1.75 us -> 2.05 us
  transfers between devices with their start and end apart: 7 -> 9, of which waited for: 4 -> 3; matrix products, arithmetic and copies ran while one was open for 1% -> 1% of each run, Pallas kernels for 11% -> 12%
where the time goes in v9:
time: 99.2 us; the launch traced here: 98.6 us
  starting transfers between devices  57.2 us (58%)
  waiting for transfers between devices  18.5 us (19%)
  Pallas kernels  16.2 us (16%)
  local copies, waits for them, and re-layouts  5.05 us (5%)
    all_to_all x1, starting transfers between devices, per_device(): lax.all_to_all(outgoing, exchange, 0, 0, axis_index_groups=groups, tiled=...  19.2 us
    all_to_all x1, starting transfers between devices, per_device(): lax.all_to_all(answers, exchange, 0, 0, axis_index_groups=groups, tiled=T...  17.3 us
    pallas_call x4, Pallas kernels, score_call(): pl.pallas_call(body, in_specs=[anywhere if i in hbm else vmem for i in ra...  13.1 us
    all_to_all x1, waiting for transfers between devices, per_device(): lax.all_to_all(answers, exchange, 0, 0, axis_index_groups=groups, tiled=T...  8.64 us
    ppermute x1, waiting for transfers between devices, per_device(): far_h = lax.ppermute(jnp.concatenate([heads, sib_h], axis=0), 'xl', SWAP)  8.55 us
    ppermute x1, starting transfers between devices, per_device(): far_sib_b = lax.ppermute(far_b, 'c', SWAP)  4.03 us
    ppermute x1, starting transfers between devices, per_device(): far_a = lax.ppermute(own_w[:half], 'xl', SWAP)  3.94 us
    ppermute x1, starting transfers between devices, per_device(): far_sib_a = lax.ppermute(far_a, 'c', SWAP)  3.43 us
  transfers between devices with their start and end apart: 9, of which 3 were waited for; matrix products, arithmetic and copies ran while one was open for 1% of the time, Pallas kernels for 12%

profile of v9, /device:TPU:1, one launch (start us, length us, event | category | flops | bytes accessed | tf_op | source)
XLA Modules:
  0.0 98.6 jit_solution(6511625204584640248)
XLA Ops:
  0.6 3.0 %slice_bitcast_fusion = (bf16[1024,512]{1,0:T(8,128)(2,1)}, bf16[1024,512]{1,0:T(8,128)(2,1)}) fusion(bf16[1,2048,512]{2,1,0:T(8,128)(2,1)} %param.7), kind=kLoop, calls=%fused_computation | loop fusion | bytes 4194304 | tf_op jit(solution)/shard_map/slice | solution.py:196
  3.6 3.9 %collective-permute-start.1 = (bf16[1024,512]{1,0:T(8,128)(2,1)}, bf16[1024,512]{1,0:T(8,128)(2,1)}, u32[]{:S(2)}, u32[]{:S(2)}) collective-permute-start(bf16[1024,512]{1,0:T(8,128)(2,1)} %get-tuple-element.32), channel_id=1, source_target_pairs={{0,2},{2,0},{1,3},{3,1},{4,6},{6,4},{5,7},{7,5},{8,10},{10,8},{9,1... | collective-permute-start | bytes 3145736 | tf_op jit(solution)/shard_map/ppermute | solution.py:196
  7.6 2.5 %fill_slots.1 = (bf16[128,2,2048]{2,1,0:T(2,128)(2,1)}, s32[1,128]{1,0:T(1,128)}) custom-call(s32[1,128]{1,0:T(1,128)} %bitcast.17, s32[1,128]{1,0:T(1,128)} %bitcast.20, bf16[128,2048]{1,0:T(8,128)(2,1)} %x_ref.1), custom_call_target="tpu_custom_call" | custom-call | flops 199999995904 | tf_op jit(solution)/shard_map/fill_slots/pallas_call | solution.py:64
  10.1 0.0 copy-start
  10.1 0.0 copy-start.5
  10.1 0.0 copy-start.6
  10.1 19.2 %all-to-all-start = ((bf16[128,2,2048]{2,1,0:T(2,128)(2,1)}), bf16[128,2,2048]{2,1,0:T(2,128)(2,1)S(1)}, u32[]{:S(2)}, u32[]{:S(2)}) async-start(bf16[128,2,2048]{2,1,0:T(2,128)(2,1)} %get-tuple-element.22), calls=%async_computation | async-start | bytes 2097152 | tf_op jit(solution)/shard_map/all_to_all | solution.py:202
  29.4 2.2 %collective-permute-start = (bf16[1024,512]{1,0:T(8,128)(2,1)}, bf16[1024,512]{1,0:T(8,128)(2,1)}, u32[]{:S(2)}, u32[]{:S(2)}) collective-permute-start(bf16[1024,512]{1,0:T(8,128)(2,1)} %get-tuple-element.33), channel_id=1, source_target_pairs={{0,2},{2,0},{1,3},{3,1},{4,6},{6,4},{5,7},{7,5},{8,10},{10,8},{9,1... | collective-permute-start | bytes 3145736 | tf_op jit(solution)/shard_map/ppermute | solution.py:197
  31.6 0.0 collective-permute-done.1.w1a_hbm
  31.6 3.4 %collective-permute-start.2 = (bf16[1024,512]{1,0:T(8,128)(2,1)}, bf16[1024,512]{1,0:T(8,128)(2,1)S(1)}, u32[]{:S(2)}, u32[]{:S(2)}) collective-permute-start(bf16[1024,512]{1,0:T(8,128)(2,1)} %collective-permute-done.1.w1a_hbm), channel_id=1, source_target_pairs={{0,1},{1,0},{2,3},{3,2},{4,5},{5,4},{6,7},{7,6},{8,9},{9,8},{10,11... | collective-permute-start | bytes 3145736 | tf_op jit(solution)/shard_map/ppermute | solution.py:198
  35.0 1.9 %collective-permute-start.3 = (bf16[1,512]{1,0:T(2,128)(2,1)}, bf16[1,512]{1,0:T(2,128)(2,1)S(1)}, u32[]{:S(2)}, u32[]{:S(2)}) collective-permute-start(bf16[1,512]{1,0:T(2,128)(2,1)} %h0_ref.1), channel_id=1, source_target_pairs={{0,1},{1,0},{2,3},{3,2},{4,5},{5,4},{6,7},{7,6},{8,9},{9,8},{10,11... | collective-permute-start | bytes 3080 | tf_op jit(solution)/shard_map/ppermute | solution.py:203
  37.0 1.3 %collective-permute-done.3.h0_ref = bf16[1,512]{1,0:T(2,128)(2,1)S(1)} collective-permute-done((bf16[1,512]{1,0:T(2,128)(2,1)}, bf16[1,512]{1,0:T(2,128)(2,1)S(1)}, u32[]{:S(2)}, u32[]{:S(2)}) %collective-permute-start.3) | collective-permute-done | bytes 1056 | tf_op jit(solution)/shard_map/ppermute | solution.py:203
  38.3 0.0 copy-done
  38.3 2.1 %collective-permute-start.5 = (bf16[2048,512]{1,0:T(8,128)(2,1)S(1)}, bf16[2048,512]{1,0:T(8,128)(2,1)}, u32[]{:S(2)}, u32[]{:S(2)}) collective-permute-start(bf16[2048,512]{1,0:T(8,128)(2,1)S(1)} %bitcast.13), channel_id=1, source_target_pairs={{0,1},{1,0},{2,3},{3,2},{4,5},{5,4},{6,7},{7,6},{8,9},{9,8},{10,11... | collective-permute-start | bytes 6291464 | tf_op jit(solution)/shard_map/ppermute | solution.py:205
  40.4 0.7 pad_maximum_fusion
  41.1 3.1 %collective-permute-start.4 = (bf16[2,512]{1,0:T(2,128)(2,1)S(1)}, bf16[2,512]{1,0:T(2,128)(2,1)S(1)}, u32[]{:S(2)}, u32[]{:S(2)}) collective-permute-start(bf16[2,512]{1,0:T(2,128)(2,1)S(1)} %pad_maximum_fusion), channel_id=1, source_target_pairs={{0,2},{2,0},{1,3},{3,1},{4,6},{6,4},{5,7},{7,5},{8,10},{10,8},{9,1... | collective-permute-start | bytes 6152 | tf_op jit(solution)/shard_map/ppermute | solution.py:206
  44.1 0.0 copy-done.5
  44.1 0.0 copy-done.6
  44.2 0.0 copy-start.4
  44.2 1.0 %copy-done.4 = bf16[128,2048]{1,0:T(8,128)(2,1)S(1)} copy-done((bf16[128,2048]{1,0:T(8,128)(2,1)S(1)}, bf16[128,2048]{1,0:T(8,128)(2,1)}, u32[]{:S(2)}) %copy-start.4) | copy-done | bytes 524312
  45.2 1.3 %score_own.1 = (bf16[128,2048]{1,0:T(8,128)(2,1)}, f32[128,1]{1,0:T(8,128)S(1)}) custom-call(bf16[128,2048]{1,0:T(8,128)(2,1)S(1)} %copy-done.4, f32[1,2048]{1,0:T(1,128)S(1)} %copy-done.5, bf16[2048,512]{1,0:T(8,128)(2,1)S(1)} %bitcast.14, bf16[1,512]{1,0:T(2,128)(2,1)S(1)} %copy-done.6), custom_call_target="tpu_custom_call" | custom-call | tf_op jit(solution)/shard_map/score_own/pallas_call | solution.py:177
  46.5 8.6 %collective-permute-done.4.h1_ref.h12_ref = bf16[2,512]{1,0:T(2,128)(2,1)S(1)} collective-permute-done((bf16[2,512]{1,0:T(2,128)(2,1)S(1)}, bf16[2,512]{1,0:T(2,128)(2,1)S(1)}, u32[]{:S(2)}, u32[]{:S(2)}) %collective-permute-start.4) | collective-permute-done | bytes 2080 | tf_op jit(solution)/shard_map/ppermute | solution.py:206
  55.0 0.0 collective-permute-done.w1b_hbm
  55.0 0.0 collective-permute-done.2.w1a_hbm.w2a_hbm
  55.0 0.0 copy-start.1
  55.0 1.0 copy-done.1
  56.0 4.0 %collective-permute-start.6 = (bf16[1024,512]{1,0:T(8,128)(2,1)}, bf16[1024,512]{1,0:T(8,128)(2,1)}, u32[]{:S(2)}, u32[]{:S(2)}) collective-permute-start(bf16[1024,512]{1,0:T(8,128)(2,1)} %collective-permute-done.w1b_hbm), channel_id=1, source_target_pairs={{0,1},{1,0},{2,3},{3,2},{4,5},{5,4},{6,7},{7,6},{8,9},{9,8},{10,11... | collective-permute-start | bytes 3145736 | tf_op jit(solution)/shard_map/ppermute | solution.py:217
  60.0 0.0 all-to-all-done.x_ref
  60.1 0.0 copy-start.2
  60.1 3.6 %score_first.1 = (bf16[256,2048]{1,0:T(8,128)(2,1)S(1)}, f32[256,1]{1,0:T(8,128)S(1)}) custom-call(bf16[128,2,2048]{2,1,0:T(2,128)(2,1)S(1)} %all-to-all-done.x_ref, f32[1,2048]{1,0:T(1,128)S(1)} %copy-done.5, bf16[2048,512]{1,0:T(8,128)(2,1)S(1)} %bitcast.15, bf16[1,512]{1,0:T(2,128)(2,1)S(1)} %copy-done.6, ...), custom_call_target="tpu_custom_call" | custom-call | flops 20000000000 | tf_op jit(solution)/shard_map/score_first/pallas_call | solution.py:177
  63.7 0.0 collective-permute-done.5.w0_hbm
  63.7 0.0 collective-permute-done.6.w1b_hbm.w2b_hbm
  63.7 0.0 copy-done.2
  63.7 0.0 copy-start.3
  63.8 0.0 copy-start.9
  63.8 4.2 %score_last.1 = f32[128,2]{1,0:T(8,128)} custom-call(bf16[256,2048]{1,0:T(8,128)(2,1)S(1)} %get-tuple-element.25.scaled_ref, f32[256,1]{1,0:T(8,128)S(1)} %get-tuple-element.26.near_ref, bf16[2048,512]{1,0:T(8,128)(2,1)} %collective-permute-done.5.w0_hbm, bf16[1,512]{1,0:T(2,128)(2,1)S(1)} %collective-permute-done.3.h0_ref, bf16[1024,512]{1,0:T(8,128)(2,1)S(1)} %copy-done.2, ...), custom_call_target="tpu_custom_call" | custom-call | tf_op jit(solution)/shard_map/score_last/pallas_call | solution.py:177
  67.9 17.3 %all-to-all-start.1 = ((f32[128,1,2]{2,1,0:T(1,128)}), f32[128,1,2]{2,1,0:T(1,128)S(1)}, u32[]{:S(2)}, u32[]{:S(2)}) async-start(f32[128,1,2]{2,1,0:T(1,128)} %bitcast.7), calls=%async_computation.1 | async-start | bytes 131072 | tf_op jit(solution)/shard_map/all_to_all | solution.py:240
  85.3 0.0 copy-done.3
  85.3 0.0 copy-done.9
  85.3 0.0 copy-start.7
  85.3 0.0 copy-start.8
  85.3 4.0 %score_own_rest.1 = f32[1,128]{1,0:T(1,128)} custom-call(bf16[128,2048]{1,0:T(8,128)(2,1)S(1)} %copy-done.9, f32[128,1]{1,0:T(8,128)S(1)} %get-tuple-element.30.near_ref, bf16[2048,512]{1,0:T(8,128)(2,1)} %collective-permute-done.5.w0_hbm, bf16[1,512]{1,0:T(2,128)(2,1)S(1)} %collective-permute-done.3.h0_ref, ...), custom_call_target="tpu_custom_call" | custom-call | flops 5000000000 | tf_op jit(solution)/shard_map/score_own_rest/pallas_call | solution.py:177
  89.3 8.6 %all-to-all-done.1 = f32[128,1,2]{2,1,0:T(1,128)S(1)} async-done(((f32[128,1,2]{2,1,0:T(1,128)}), f32[128,1,2]{2,1,0:T(1,128)S(1)}, u32[]{:S(2)}, u32[]{:S(2)}) %all-to-all-start.1) | async-done | bytes 1056 | tf_op jit(solution)/shard_map/all_to_all | solution.py:240
  98.0 0.0 copy-done.7
  98.0 0.0 copy-done.8
  98.0 0.6 pick_answers.1
Async XLA Ops:
  3.6 28.0 %collective-permute-start.1 = (bf16[1024,512]{1,0:T(8,128)(2,1)}, bf16[1024,512]{1,0:T(8,128)(2,1)}, u32[]{:S(2)}, u32[]{:S(2)}) collective-permute-start(bf16[1024,512]{1,0:T(8,128)(2,1)} %get-tuple-element.32), channel_id=1, source_target_pairs={{0,2},{2,0},{1,3},{3,1},{4,6},{6,4},{5,7},{7,5},{8,10},{10,8},{9,1... | collective-permute-start | bytes 3145736 | tf_op jit(solution)/shard_map/ppermute | solution.py:196
  10.1 28.2 %copy-start = (bf16[1,2048,512]{2,1,0:T(8,128)(2,1)S(1)}, bf16[1,2048,512]{2,1,0:T(8,128)(2,1)}, u32[]{:S(2)}) copy-start(bf16[1,2048,512]{2,1,0:T(8,128)(2,1)} %param.7) | copy-start | bytes 6291460
  10.1 34.0 %copy-start.5 = (f32[1,2048]{1,0:T(1,128)S(1)}, f32[1,2048]{1,0:T(1,128)}, u32[]{:S(2)}) copy-start(f32[1,2048]{1,0:T(1,128)} %gain_ref.3) | copy-start | bytes 24580
  10.1 34.0 %copy-start.6 = (bf16[1,512]{1,0:T(2,128)(2,1)S(1)}, bf16[1,512]{1,0:T(2,128)(2,1)}, u32[]{:S(2)}) copy-start(bf16[1,512]{1,0:T(2,128)(2,1)} %h0_ref.1) | copy-start | bytes 3076
  10.1 49.9 %all-to-all-start = ((bf16[128,2,2048]{2,1,0:T(2,128)(2,1)}), bf16[128,2,2048]{2,1,0:T(2,128)(2,1)S(1)}, u32[]{:S(2)}, u32[]{:S(2)}) async-start(bf16[128,2,2048]{2,1,0:T(2,128)(2,1)} %get-tuple-element.22), calls=%async_computation | async-start | bytes 2097152 | tf_op jit(solution)/shard_map/all_to_all | solution.py:202
  29.4 25.7 %collective-permute-start = (bf16[1024,512]{1,0:T(8,128)(2,1)}, bf16[1024,512]{1,0:T(8,128)(2,1)}, u32[]{:S(2)}, u32[]{:S(2)}) collective-permute-start(bf16[1024,512]{1,0:T(8,128)(2,1)} %get-tuple-element.33), channel_id=1, source_target_pairs={{0,2},{2,0},{1,3},{3,1},{4,6},{6,4},{5,7},{7,5},{8,10},{10,8},{9,1... | collective-permute-start | bytes 3145736 | tf_op jit(solution)/shard_map/ppermute | solution.py:197
  31.6 23.4 %collective-permute-start.2 = (bf16[1024,512]{1,0:T(8,128)(2,1)}, bf16[1024,512]{1,0:T(8,128)(2,1)S(1)}, u32[]{:S(2)}, u32[]{:S(2)}) collective-permute-start(bf16[1024,512]{1,0:T(8,128)(2,1)} %collective-permute-done.1.w1a_hbm), channel_id=1, source_target_pairs={{0,1},{1,0},{2,3},{3,2},{4,5},{5,4},{6,7},{7,6},{8,9},{9,8},{10,11... | collective-permute-start | bytes 3145736 | tf_op jit(solution)/shard_map/ppermute | solution.py:198
  35.0 3.3 %collective-permute-start.3 = (bf16[1,512]{1,0:T(2,128)(2,1)}, bf16[1,512]{1,0:T(2,128)(2,1)S(1)}, u32[]{:S(2)}, u32[]{:S(2)}) collective-permute-start(bf16[1,512]{1,0:T(2,128)(2,1)} %h0_ref.1), channel_id=1, source_target_pairs={{0,1},{1,0},{2,3},{3,2},{4,5},{5,4},{6,7},{7,6},{8,9},{9,8},{10,11... | collective-permute-start | bytes 3080 | tf_op jit(solution)/shard_map/ppermute | solution.py:203
  38.3 25.4 %collective-permute-start.5 = (bf16[2048,512]{1,0:T(8,128)(2,1)S(1)}, bf16[2048,512]{1,0:T(8,128)(2,1)}, u32[]{:S(2)}, u32[]{:S(2)}) collective-permute-start(bf16[2048,512]{1,0:T(8,128)(2,1)S(1)} %bitcast.13), channel_id=1, source_target_pairs={{0,1},{1,0},{2,3},{3,2},{4,5},{5,4},{6,7},{7,6},{8,9},{9,8},{10,11... | collective-permute-start | bytes 6291464 | tf_op jit(solution)/shard_map/ppermute | solution.py:205
  41.1 14.0 %collective-permute-start.4 = (bf16[2,512]{1,0:T(2,128)(2,1)S(1)}, bf16[2,512]{1,0:T(2,128)(2,1)S(1)}, u32[]{:S(2)}, u32[]{:S(2)}) collective-permute-start(bf16[2,512]{1,0:T(2,128)(2,1)S(1)} %pad_maximum_fusion), channel_id=1, source_target_pairs={{0,2},{2,0},{1,3},{3,1},{4,6},{6,4},{5,7},{7,5},{8,10},{10,8},{9,1... | collective-permute-start | bytes 6152 | tf_op jit(solution)/shard_map/ppermute | solution.py:206
  44.2 1.0 %copy-start.4 = (bf16[128,2048]{1,0:T(8,128)(2,1)S(1)}, bf16[128,2048]{1,0:T(8,128)(2,1)}, u32[]{:S(2)}) copy-start(bf16[128,2048]{1,0:T(8,128)(2,1)} %x_ref.1) | copy-start | bytes 1572868
  55.0 1.0 copy-start.1
  56.0 7.7 %collective-permute-start.6 = (bf16[1024,512]{1,0:T(8,128)(2,1)}, bf16[1024,512]{1,0:T(8,128)(2,1)}, u32[]{:S(2)}, u32[]{:S(2)}) collective-permute-start(bf16[1024,512]{1,0:T(8,128)(2,1)} %collective-permute-done.w1b_hbm), channel_id=1, source_target_pairs={{0,1},{1,0},{2,3},{3,2},{4,5},{5,4},{6,7},{7,6},{8,9},{9,8},{10,11... | collective-permute-start | bytes 3145736 | tf_op jit(solution)/shard_map/ppermute | solution.py:217
  60.1 3.7 %copy-start.2 = (bf16[1024,512]{1,0:T(8,128)(2,1)S(1)}, bf16[1024,512]{1,0:T(8,128)(2,1)}, u32[]{:S(2)}) copy-start(bf16[1024,512]{1,0:T(8,128)(2,1)} %copy-done.1) | copy-start | bytes 3145732
  63.7 21.5 %copy-start.3 = (bf16[1024,512]{1,0:T(8,128)(2,1)S(1)}, bf16[1024,512]{1,0:T(8,128)(2,1)}, u32[]{:S(2)}) copy-start(bf16[1024,512]{1,0:T(8,128)(2,1)} %copy-done.1) | copy-start | bytes 3145732
  63.8 21.5 %copy-start.9 = (bf16[128,2048]{1,0:T(8,128)(2,1)S(1)}, bf16[128,2048]{1,0:T(8,128)(2,1)}, u32[]{:S(2)}) copy-start(bf16[128,2048]{1,0:T(8,128)(2,1)} %get-tuple-element.29.scaled_ref) | copy-start | bytes 1572868
  67.9 30.0 %all-to-all-start.1 = ((f32[128,1,2]{2,1,0:T(1,128)}), f32[128,1,2]{2,1,0:T(1,128)S(1)}, u32[]{:S(2)}, u32[]{:S(2)}) async-start(f32[128,1,2]{2,1,0:T(1,128)} %bitcast.7), calls=%async_computation.1 | async-start | bytes 131072 | tf_op jit(solution)/shard_map/all_to_all | solution.py:240
  85.3 12.7 %copy-start.7 = (s32[128,1]{0,1:T(1,128)S(1)}, s32[128,1]{0,1:T(1,128)}, u32[]{:S(2)}) copy-start(s32[128,1]{0,1:T(1,128)} %param.10) | copy-start | bytes 1540
  85.3 12.7 %copy-start.8 = (s32[1,128]{1,0:T(1,128)S(1)}, s32[1,128]{1,0:T(1,128)}, u32[]{:S(2)}) copy-start(s32[1,128]{1,0:T(1,128)} %get-tuple-element.31.slot_ref) | copy-start | bytes 1540
